TPU v7x, 32 devices: a whole 2x2x4 slice. The times are simulated.
32 devices in a mesh: rep: 4 (over y, core), shard: 8 (over z, x).
Axes of the slice: x: 2, y: 2, z: 4, core: 2. Of those that a mesh axis runs over, the one named last changes fastest.
Arguments:
- tokens: bfloat16 [64, 1024, 512], P('rep', 'shard'), may hold values from -6 to 6
- cotangent: bfloat16 [64, 1024, 512], P('rep', 'shard'), may hold values from -6 to 6
- doc_lengths: int32 [64, 16], P('rep'), may hold values from 1 to 768, 1024 in all within a row
- attend: bfloat16 [512, 1536], P('shard'), may hold values from -0.25 to 0.25
- project: bfloat16 [512, 512], P('shard'), may hold values from -2 to 2
- widen: bfloat16 [512, 2048], P('shard'), may hold values from -0.25 to 0.25
- narrow: bfloat16 [2048, 512], P('shard'), may hold values from -0.125 to 0.125
- hidden_bias: bfloat16 [2048], P('shard'), may hold values from -3 to 3
- final_bias: bfloat16 [512], P('shard'), may hold values from -1.796875 to 1.796875
- gain_first: bfloat16 [512], P('shard'), may hold values from 0.5 to 1.5
- shift_first: bfloat16 [512], P('shard'), may hold values from -1.796875 to 1.796875
- gain_second: bfloat16 [512], P('shard'), may hold values from 0.5 to 1.5
- shift_second: bfloat16 [512], P('shard'), may hold values from -1.796875 to 1.796875
Outputs:
- block_out: float32 [64, 1024, 512], P('rep', 'shard')
- tokens_grad: float32 [64, 1024, 512], P('rep', 'shard')
- attend_grad: float32 [512, 1536], P('shard')
- project_grad: float32 [512, 512], P('shard')
- widen_grad: float32 [512, 2048], P('shard')
- narrow_grad: float32 [2048, 512], P('shard')
- hidden_bias_grad: float32 [2048], P('shard')
- final_bias_grad: float32 [512], P('shard')
- gain_first_grad: float32 [512], P('shard')
- shift_first_grad: float32 [512], P('shard')
- gain_second_grad: float32 [512], P('shard')
- shift_second_grad: float32 [512], P('shard')
Inputs may be any that keep to these rules, and one draw needn't show every extreme that they name: `doc_lengths`: row s lists the lengths of the 16 documents packed in order into sequence s; they fill all 1024 positions, and the longest is 768.
All inputs are finite; a program needn't handle non-finite values.
Results may differ from a plain program's by a relative error of at most 0.017.
Values may be sent and summed in bfloat16 or wider, within the bound.
No kernel may reach another device: no remote copies, remote signals or barrier semaphores. Data moves between devices by JAX's collectives and lax.ppermute only.
A program may use at most 192 MiB of HBM per device.

v0:
```python
import jax
import jax.numpy as jnp
from jax import lax
from jax.sharding import PartitionSpec as P

HEADS = 8


epsilon = 1e-05
masked = -1e30


def for_sending(x):
    return jax.tree.map(lambda a: a.astype(jnp.bfloat16) if a.dtype == jnp.float32 else a, x)


def layer_norm(values, scale_gain, shift_add):
    center = values - jnp.mean(values, axis=-1, keepdims=True)
    variance = jnp.mean(center * center, axis=-1, keepdims=True)
    return center * lax.rsqrt(variance + epsilon) * scale_gain + shift_add


def doc_layout(lengths, positions, span_rows, span_count):
    doc_ends = jnp.cumsum(lengths, axis=-1, dtype=jnp.int32)
    doc_starts = doc_ends - lengths
    segment = jnp.sum(
        (positions[None, :, None] >= doc_ends[:, None, :]).astype(jnp.int32),
        axis=-1,
        dtype=jnp.int32,
    )
    span_last = (jnp.arange(span_count, dtype=jnp.int32) + 1) * span_rows - 1
    last_doc = jnp.sum(
        (span_last[None, :, None] >= doc_ends[:, None, :]).astype(jnp.int32),
        axis=-1,
        dtype=jnp.int32,
    )
    picked = last_doc[:, :, None] == jnp.arange(lengths.shape[-1], dtype=jnp.int32)[None, None, :]
    last_start = jnp.sum(jnp.where(picked, doc_starts[:, None, :], 0), axis=-1, dtype=jnp.int32)
    counts = jnp.minimum(span_rows, span_last[None, :] + 1 - last_start)
    return (segment, last_doc, counts)


def score_bias(segment, last_doc, counts, position_span):
    span_rows = segment.shape[1]
    row_ids = jnp.arange(span_rows, dtype=jnp.int32)
    causal = row_ids[None, :, None] >= row_ids[None, None, :]
    same_doc = segment[:, :, None] == segment[:, None, :]
    direct = jnp.where(causal & same_doc, 0.0, masked)
    earlier = jnp.arange(counts.shape[1], dtype=jnp.int32)[None, None, :] < position_span
    doc_match = last_doc[:, None, :] == segment[:, :, None]
    pooled_bias = jnp.where(
        earlier & doc_match, jnp.log(counts.astype(jnp.float32))[:, None, :], masked
    )
    return jnp.concatenate([direct.astype(jnp.float32), pooled_bias], axis=-1)


def gelu_exact(values):
    return jax.nn.gelu(values, approximate=False)


def local(
    tokens,
    cotangent,
    doc_lengths,
    attend,
    project,
    widen,
    narrow,
    hidden_bias,
    final_bias,
    gain_first,
    shift_first,
    gain_second,
    shift_second,
):
    fetched = (
        lax.all_gather(attend, "shard", axis=0, tiled=True),
        lax.all_gather(project, "shard", axis=0, tiled=True),
        lax.all_gather(widen, "shard", axis=0, tiled=True),
        lax.all_gather(narrow, "shard", axis=0, tiled=True),
        lax.all_gather(hidden_bias, "shard", axis=0, tiled=True),
        lax.all_gather(final_bias, "shard", axis=0, tiled=True),
        lax.all_gather(gain_first, "shard", axis=0, tiled=True),
        lax.all_gather(shift_first, "shard", axis=0, tiled=True),
        lax.all_gather(gain_second, "shard", axis=0, tiled=True),
        lax.all_gather(shift_second, "shard", axis=0, tiled=True),
    )
    attend_all, project_all, widen_all, narrow_all = (
        fetched[0],
        fetched[1],
        fetched[2],
        fetched[3],
    )
    hidden_all = fetched[4].astype(jnp.float32)
    final_all = fetched[5].astype(jnp.float32)
    first_gain = fetched[6].astype(jnp.float32)
    first_shift = fetched[7].astype(jnp.float32)
    second_gain = fetched[8].astype(jnp.float32)
    second_shift = fetched[9].astype(jnp.float32)
    seq_count, span_rows, model_width = tokens.shape
    head_size = model_width // HEADS
    score_scale = head_size ** (-0.5)
    shard_index = lax.axis_index("shard")
    span_count = lax.axis_size("shard")
    positions = shard_index * span_rows + jnp.arange(span_rows, dtype=jnp.int32)
    segment, last_doc, counts = doc_layout(doc_lengths, positions, span_rows, span_count)
    bias_all = score_bias(segment, last_doc, counts, shard_index)
    own_doc = lax.dynamic_index_in_dim(last_doc, shard_index, 1, keepdims=True)
    own_count = lax.dynamic_index_in_dim(counts, shard_index, 1, keepdims=True).astype(jnp.float32)
    member = segment == own_doc
    inputs = tokens.astype(jnp.float32)
    normed_one, first_pull = jax.vjp(layer_norm, inputs, first_gain, first_shift)
    low_one = normed_one.astype(jnp.bfloat16)
    qkv_all = jnp.dot(low_one, attend_all, preferred_element_type=jnp.float32).astype(jnp.bfloat16)
    pooled = (
        jnp.einsum(
            "st,std->sd",
            member.astype(jnp.bfloat16),
            qkv_all[:, :, model_width:],
            preferred_element_type=jnp.float32,
        )
        / own_count
    )
    summaries = lax.all_gather(pooled.astype(jnp.bfloat16)[:, None, :], "shard", axis=1, tiled=True)
    queries = qkv_all[:, :, :model_width].reshape(seq_count, span_rows, HEADS, head_size)
    key_all = jnp.concatenate(
        [qkv_all[:, :, model_width : 2 * model_width], summaries[:, :, :model_width]], axis=1
    )
    value_all = jnp.concatenate(
        [qkv_all[:, :, 2 * model_width :], summaries[:, :, model_width:]], axis=1
    )
    key_all = key_all.reshape(seq_count, span_rows + span_count, HEADS, head_size)
    value_all = value_all.reshape(seq_count, span_rows + span_count, HEADS, head_size)

    def scores_of():
        raw_scores = jnp.einsum(
            "sqhe,skhe->shqk", queries, key_all, preferred_element_type=jnp.float32
        )
        return raw_scores * score_scale + bias_all[:, None]

    scores = scores_of()
    row_max = jnp.max(scores, axis=-1, keepdims=True)
    exped = jnp.exp(scores - row_max)
    row_total = jnp.sum(exped, axis=-1, keepdims=True)
    log_total = row_max + jnp.log(row_total)
    attn_probs = (exped / row_total).astype(jnp.bfloat16)
    attn_out = jnp.einsum(
        "shqk,skhe->sqhe", attn_probs, value_all, preferred_element_type=jnp.float32
    )
    attn_low = attn_out.reshape(seq_count, span_rows, model_width).astype(jnp.bfloat16)
    residual = inputs + jnp.dot(attn_low, project_all, preferred_element_type=jnp.float32)
    normed_two, second_pull = jax.vjp(layer_norm, residual, second_gain, second_shift)
    low_two = normed_two.astype(jnp.bfloat16)
    pre_act = jnp.dot(low_two, widen_all, preferred_element_type=jnp.float32) + hidden_all
    activation, gelu_pull = jax.vjp(gelu_exact, pre_act)
    activ_low = activation.astype(jnp.bfloat16)
    block_out = (
        residual + jnp.dot(activ_low, narrow_all, preferred_element_type=jnp.float32) + final_all
    )
    attend_back, project_back, widen_back, narrow_back = (
        lax.all_gather(attend, "shard", axis=0, tiled=True),
        lax.all_gather(project, "shard", axis=0, tiled=True),
        lax.all_gather(widen, "shard", axis=0, tiled=True),
        lax.all_gather(narrow, "shard", axis=0, tiled=True),
    )
    grad_narrow = jnp.einsum(
        "stf,std->fd", activ_low, cotangent, preferred_element_type=jnp.float32
    )
    grad_final = jnp.sum(cotangent, axis=(0, 1), dtype=jnp.float32)
    grad_activ = jnp.einsum(
        "std,fd->stf", cotangent, narrow_back, preferred_element_type=jnp.float32
    )
    grad_pre = gelu_pull(grad_activ)[0].astype(jnp.bfloat16)
    grad_hidden = jnp.sum(grad_pre, axis=(0, 1), dtype=jnp.float32)
    grad_widen = jnp.einsum("std,stf->df", low_two, grad_pre, preferred_element_type=jnp.float32)
    grad_normed_two = jnp.einsum(
        "stf,df->std", grad_pre, widen_back, preferred_element_type=jnp.float32
    )
    grad_resid_norm, grad_gain_two, grad_shift_two = second_pull(grad_normed_two)
    grad_resid = cotangent.astype(jnp.float32) + grad_resid_norm
    grad_branch = grad_resid.astype(jnp.bfloat16)
    grad_project = jnp.einsum(
        "std,ste->de", attn_low, grad_branch, preferred_element_type=jnp.float32
    )
    grad_attn = jnp.einsum(
        "ste,de->std", grad_branch, project_back, preferred_element_type=jnp.float32
    )
    grad_attn = grad_attn.astype(jnp.bfloat16).reshape(seq_count, span_rows, HEADS, head_size)
    probs_again = jnp.exp(scores_of() - log_total)
    grad_probs = jnp.einsum(
        "sqhe,skhe->shqk", grad_attn, value_all, preferred_element_type=jnp.float32
    )
    grad_scores = probs_again * (
        grad_probs - jnp.sum(probs_again * grad_probs, axis=-1, keepdims=True)
    )
    grad_scores = grad_scores.astype(jnp.bfloat16)
    grad_queries = (
        jnp.einsum("shqk,skhe->sqhe", grad_scores, key_all, preferred_element_type=jnp.float32)
        * score_scale
    )
    grad_keys = (
        jnp.einsum("shqk,sqhe->skhe", grad_scores, queries, preferred_element_type=jnp.float32)
        * score_scale
    )
    grad_values = jnp.einsum(
        "shqk,sqhe->skhe",
        probs_again.astype(jnp.bfloat16),
        grad_attn,
        preferred_element_type=jnp.float32,
    )
    grad_keys = grad_keys.reshape(seq_count, span_rows + span_count, model_width)
    grad_values = grad_values.reshape(seq_count, span_rows + span_count, model_width)
    grad_summary = jnp.concatenate([grad_keys[:, span_rows:], grad_values[:, span_rows:]], axis=-1)
    own_grad = lax.psum_scatter(
        grad_summary.astype(jnp.bfloat16), "shard", scatter_dimension=1, tiled=True
    ).astype(jnp.float32)
    spread = (member.astype(jnp.float32) / own_count)[:, :, None]
    grad_pairs = (
        jnp.concatenate([grad_keys[:, :span_rows], grad_values[:, :span_rows]], axis=-1)
        + spread * own_grad
    )
    grad_qkv = jnp.concatenate(
        [grad_queries.reshape(seq_count, span_rows, model_width), grad_pairs], axis=-1
    ).astype(jnp.bfloat16)
    grad_attend = jnp.einsum("std,ste->de", low_one, grad_qkv, preferred_element_type=jnp.float32)
    grad_normed_one = jnp.einsum(
        "ste,de->std", grad_qkv, attend_back, preferred_element_type=jnp.float32
    )
    grad_input_norm, grad_gain_one, grad_shift_one = first_pull(grad_normed_one)
    tokens_grad = grad_resid + grad_input_norm
    shares = (
        lax.psum_scatter(
            grad_attend.astype(jnp.bfloat16), "shard", scatter_dimension=0, tiled=True
        ).astype(jnp.float32),
        lax.psum_scatter(
            grad_project.astype(jnp.bfloat16), "shard", scatter_dimension=0, tiled=True
        ).astype(jnp.float32),
        lax.psum_scatter(
            grad_widen.astype(jnp.bfloat16), "shard", scatter_dimension=0, tiled=True
        ).astype(jnp.float32),
        lax.psum_scatter(
            grad_narrow.astype(jnp.bfloat16), "shard", scatter_dimension=0, tiled=True
        ).astype(jnp.float32),
        lax.psum_scatter(
            grad_hidden.astype(jnp.bfloat16), "shard", scatter_dimension=0, tiled=True
        ).astype(jnp.float32),
        lax.psum_scatter(
            grad_final.astype(jnp.bfloat16), "shard", scatter_dimension=0, tiled=True
        ).astype(jnp.float32),
        lax.psum_scatter(
            grad_gain_one.astype(jnp.bfloat16), "shard", scatter_dimension=0, tiled=True
        ).astype(jnp.float32),
        lax.psum_scatter(
            grad_shift_one.astype(jnp.bfloat16), "shard", scatter_dimension=0, tiled=True
        ).astype(jnp.float32),
        lax.psum_scatter(
            grad_gain_two.astype(jnp.bfloat16), "shard", scatter_dimension=0, tiled=True
        ).astype(jnp.float32),
        lax.psum_scatter(
            grad_shift_two.astype(jnp.bfloat16), "shard", scatter_dimension=0, tiled=True
        ).astype(jnp.float32),
    )
    totals = jax.tree.map(
        lambda part: part.astype(jnp.float32), lax.psum(for_sending(tuple(shares)), "rep")
    )
    return (
        block_out,
        tokens_grad,
        totals[0],
        totals[1],
        totals[2],
        totals[3],
        totals[4],
        totals[5],
        totals[6],
        totals[7],
        totals[8],
        totals[9],
    )


def solution(mesh):
    return jax.shard_map(
        local,
        mesh=mesh,
        in_specs=(
            P("rep", "shard", None),
            P("rep", "shard", None),
            P("rep", None),
            P("shard", None),
            P("shard", None),
            P("shard", None),
            P("shard", None),
            P("shard"),
            P("shard"),
            P("shard"),
            P("shard"),
            P("shard"),
            P("shard"),
        ),
        out_specs=(
            P("rep", "shard", None),
            P("rep", "shard", None),
            P("shard", None),
            P("shard", None),
            P("shard", None),
            P("shard", None),
            P("shard"),
            P("shard"),
            P("shard"),
            P("shard"),
            P("shard"),
            P("shard"),
        ),
        check_vma=False,
    )
```

profile of v0, /device:TPU:0, one launch (start us, length us, event | category | flops | bytes accessed | tf_op | source)
XLA Modules:
  0.0 703.8 jit_solution(4761683515033215881)
XLA Ops:
  15.6 23.1 %all-reduce.12 = (bf16[512]{0:T(512)(128)(2,1)S(1)}, bf16[512]{0:T(512)(128)(2,1)S(1)}, bf16[512]{0:T(512)(128)(2,1)S(1)}, bf16[512]{0:T(512)(128)(2,1)S(1)}) all-reduce(bf16[512]{0:T(512)(128)(2,1)S(1)} %dynamic-update-slice.1, bf16[512]{0:T(512)(128)(2,1)S(1)} %dynamic-update-slice, ...), channel_id=1, replica_groups=mesh['rep'=4,'shard'=8] {'shard'}, use_global_device_ids=true, to_apply=%add.1 | all-reduce | flops 2048 | bytes 8192
  38.8 16.3 %all-gather.1 = bf16[8,1,256]{2,1,0:T(2,128)(2,1)S(1)} all-gather(bf16[1,1,256]{2,1,0:T(2,128)(2,1)S(1)} %reshape.247), channel_id=1, replica_groups=mesh['rep'=4,'shard'=8] {'shard'}, dimensions={0}, use_global_device_ids=true | all-gather | bytes 4608 | tf_op jit(solution)/shard_map/all_gather | solution.py:81
  58.0 1.9 convert_reduce_fusion
  61.0 34.4 %all_gather.41 = bf16[512,512]{1,0:T(8,128)(2,1)} all-gather(bf16[64,512]{1,0:T(8,128)(2,1)S(1)} %copy-done.22), channel_id=1, replica_groups=mesh['rep'=4,'shard'=8] {'shard'}, dimensions={0}, use_global_device_ids=true | all-gather | bytes 589824 | tf_op jit(solution)/shard_map/all_gather | solution.py:78
  96.6 5.3 convolution_convert_fusion
  102.0 2.1 fusion.60
  104.8 31.2 %all-gather = bf16[16,8192]{1,0:T(8,128)(2,1)S(1)} all-gather(bf16[16,1024]{1,0:T(8,128)(2,1)S(1)} %fusion.51), channel_id=2, replica_groups=mesh['rep'=4,'shard'=8] {'shard'}, dimensions={1}, use_global_device_ids=true | all-gather | bytes 294912 | tf_op jit(solution)/shard_map/all_gather | solution.py:124
  136.2 2.5 pad_maximum_fusion.7
  138.8 5.8 copy.115
  144.5 3.9 copy.94
  148.4 5.7 copy.116
  154.1 5.4 fusion.63
  159.6 2.4 fusion.9
  162.0 2.1 copy-done
  164.9 2.2 fusion.40
  167.1 1.4 fusion.64
  168.6 1.9 copy-done.2
  171.3 11.1 %fusion.8 = (u16[128,2048]{1,0:T(8,128)(2,1)S(1)}, u16[128,2048]{1,0:T(8,128)(2,1)S(1)}, f32[16,128,2048]{2,1,0:T(8,128)S(1)}) fusion(f32[2048]{0:T(1024)S(1)} %bitcast.113, bf16[512,2048]{1,0:T(8,128)(2,1)} %all-gather.8.cloned.1.call-done, f32[16,128,512]{2,1,0:T(8,128)} %copy-done.2, f32[512]{0:T(512)S(1)} %convert_element_type.186, ...), kind=kOutput, calls=%fused_computation.30 | convolution fusion | flops 4358406144 | bytes 24145920 | tf_op jit(solution)/shard_map/dot_general | solution.py:154
  182.5 5.7 copy-done.8
  188.2 39.2 %multiply_convert_fusion = (bf16[16,128,2048]{2,1,0:T(8,128)(2,1)}, f32[16,128,2048]{2,1,0:T(8,128)}) fusion(f32[16,128,2048]{2,1,0:T(8,128)S(1)} %get-tuple-element.61, f32[2048]{0:T(1024)S(1)} %bitcast.114, u16[128,2048]{1,0:T(8,128)(2,1)S(1)} %get-tuple-element.13, u16[128,2048]{1,0:T(8,128)(2,1)S(1)} %get-tuple-element.12), kind=kLoop, calls=%fused_computation.8 | loop fusion | flops 297795584 | bytes 42999808 | tf_op jit(solution)/shard_map/convert_element_type | solution.py:156
  227.4 22.0 %fusion.65 = (bf16[2048]{0:T(1024)(128)(2,1)S(1)}, bf16[16,128,2048]{2,1,0:T(8,128)(2,1)}) fusion(f32[16,128,2048]{2,1,0:T(8,128)} %get-tuple-element.43, bf16[16,128,512]{2,1,0:T(8,128)(2,1)} %param.14, bf16[2048,512]{1,0:T(8,128)(2,1)} %all-gather.10.cloned.1.call-done, f32[16,128,2048]{2,1,0:T(8,128)} %copy-done.8, f32[2048]{0:T(1024)S(1)} %bitcast.115), kind=kOutput, calls=%fused_computation.133 | convolution fusion | flops 4362074112 | bytes 46149632 | tf_op jit(solution)/shard_map/std,fd->stf/dot_general | solution.py:170
  249.4 11.4 %multiply_reduce_fusion.1 = (bf16[512]{0:T(512)(128)(2,1)S(1)}, f32[16,128]{1,0:T(8,128)S(1)}, bf16[512]{0:T(512)(128)(2,1)S(1)}, f32[16,128,512]{2,1,0:T(8,128)S(1)}) fusion(f32[16,128,512]{2,1,0:T(8,128)} %copy-done.2, f32[16,128]{1,0:T(8,128)S(1)} %fusion.54, f32[16,128]{1,0:T(8,128)S(1)} %broadcast_multiply_fusion.1, f32[512]{0:T(512)S(1)} %convert_element_type.185, ...), kind=kOutput, calls=%fused_computation.58 | convolution fusion | flops 4303352832 | bytes 18903040 | tf_op jit(solution)/shard_map/stf,df->std/dot_general | solution.py:176
  260.8 1.7 fusion.59
  263.1 1.4 copy-done.4
  265.8 2.7 convolution_convert_fusion.1
  268.6 4.1 copy.98
  272.7 11.6 %multiply_reduce_fusion = (f32[16,8,128]{2,1,0:T(8,128)S(1)}, f32[16,8,128,136]{2,3,1,0:T(8,128)}) fusion(f32[16,8,128,136]{2,3,1,0:T(8,128)} %copy-done, f32[16,8,128]{2,1,0:T(8,128)S(1)} %log_add_fusion, bf16[16,128,8,64]{1,3,2,0:T(8,128)(2,1)} %bitcast.101, bf16[16,136,8,64]{1,3,2,0:T(8,128)(2,1)} %bitcast.105), kind=kOutput, calls=%fused_computation.22 | convolution fusion | flops 291880960 | bytes 22282240 | tf_op jit(solution)/shard_map/sqhe,skhe->shqk/dot_general | solution.py:190
  284.4 6.5 fusion.17
  290.8 10.2 %multiply_convert_fusion.1 = bf16[16,8,128,136]{2,3,1,0:T(8,128)(2,1)} fusion(f32[16,8,128,136]{2,3,1,0:T(8,128)} %get-tuple-element.66, f32[16,8,128,136]{2,3,1,0:T(8,128)} %copy-done, f32[16,8,128]{2,1,0:T(8,128)S(1)} %get-tuple-element.65, f32[16,8,128]{2,1,0:T(8,128)S(1)} %log_add_fusion), kind=kLoop, calls=%fused_computation.21 | loop fusion | flops 8912896 | bytes 22413312 | tf_op jit(solution)/shard_map/convert_element_type | solution.py:196
  301.0 6.0 broadcast_multiply_fusion
  307.0 3.2 copy-done.5
  310.3 1.6 slice.50
  311.9 1.9 copy.119
  313.8 3.9 slice.51
  317.7 1.9 copy.120
  320.4 6.3 multiply_convert_fusion.2
  326.7 4.6 slice.48
  331.3 4.6 slice.49
  335.9 4.1 copy.105
  340.1 5.4 copy.117
  345.5 5.4 copy.118
  350.8 4.3 fusion.46
  355.2 25.2 %reduce-scatter.6.cloned.1.call-done = bf16[16,1,1024]{2,0,1:T(8,128)(2,1)} async-done(((bf16[16,8,1024]{2,0,1:T(8,128)(2,1)}), bf16[16,1,1024]{2,0,1:T(8,128)(2,1)}) %reduce-scatter.6.cloned.1.call-update) | async-done | bytes 32784 | tf_op jit(solution)/shard_map/reduce_scatter | solution.py:214
  381.2 4.2 fusion.6
  385.3 2.0 copy-done.11
  387.4 5.0 fusion.31
  392.4 10.8 %bitcast_convert_fusion.1 = bf16[512,2048]{1,0:T(8,128)(2,1)} fusion(bf16[16,128,2048]{2,1,0:T(8,128)(2,1)} %get-tuple-element.63, f32[16,128,512]{2,1,0:T(8,128)} %copy-done.2, f32[512]{0:T(512)S(1)} %convert_element_type.186, f32[512]{0:T(512)S(1)} %convert_element_type.185, f32[16,128]{1,0:T(8,128)S(1)} %fusion.54, ...), kind=kOutput, calls=%fused_computation.57 | convolution fusion | flops 4301258752 | bytes 14700544 | tf_op jit(solution)/shard_map/std,stf->df/dot_general | solution.py:175
  403.5 10.0 %bitcast_convert_fusion = bf16[2048,512]{1,0:T(8,128)(2,1)} fusion(bf16[16,128,2048]{2,1,0:T(8,128)(2,1)} %get-tuple-element.42, bf16[16,128,512]{2,1,0:T(8,128)(2,1)} %param.14), kind=kOutput, calls=%fused_computation.56 | convolution fusion | flops 4296015872 | bytes 12582912 | tf_op jit(solution)/shard_map/stf,std->fd/dot_general | solution.py:166
  414.9 1.9 reduce_sum.223
  417.1 6.4 fusion.57
  423.6 2.0 copy-done.9
  425.5 2.1 fusion.23
  427.6 35.4 %all-reduce.11 = (bf16[512]{0:T(512)(128)(2,1)S(1)}, bf16[2048]{0:T(1024)(128)(2,1)S(1)}, bf16[512]{0:T(512)(128)(2,1)S(1)}, bf16[512]{0:T(512)(128)(2,1)S(1)}, ...) all-reduce(bf16[512]{0:T(512)(128)(2,1)S(1)} %dynamic-update-slice., ...), channel_id=1, replica_groups=mesh['rep'=4,'shard'=8] {'shard'}, use_global_device_ids=true, to_apply=%add.4 | all-reduce | flops 5120 | bytes 20480
  463.5 6.3 all-reduce.13
  472.9 11.9 %add_add_fusion.4 = f32[16,128,512]{2,1,0:T(8,128)} fusion(f32[16,128,512]{2,1,0:T(8,128)} %copy-done.2, f32[512]{0:T(512)S(1)} %convert_element_type.190, bf16[16,128,2048]{2,1,0:T(8,128)(2,1)} %get-tuple-element.42, bf16[2048,512]{1,0:T(8,128)(2,1)} %all-gather.10.cloned.1.call-done), kind=kOutput, calls=%fused_computation.64 | convolution fusion | flops 4297064448 | bytes 18876416 | tf_op jit(solution)/shard_map/dot_general | solution.py:158
  484.8 27.9 %reduce-scatter.8.cloned.1.call-done = bf16[64,1536]{1,0:T(8,128)(2,1)} async-done(((bf16[512,1536]{1,0:T(8,128)(2,1)}), bf16[64,1536]{1,0:T(8,128)(2,1)}) %reduce-scatter.8.cloned.1.call-update) | async-done | bytes 196624 | tf_op jit(solution)/shard_map/reduce_scatter | solution.py:232
  512.7 70.3 %reduce-scatter.12.cloned.1.call-done = bf16[64,2048]{1,0:T(8,128)(2,1)} async-done(((bf16[512,2048]{1,0:T(8,128)(2,1)}), bf16[64,2048]{1,0:T(8,128)(2,1)}) %reduce-scatter.12.cloned.1.call-update) | async-done | bytes 262160 | tf_op jit(solution)/shard_map/reduce_scatter | solution.py:238
  583.0 70.3 %reduce-scatter.14.cloned.1.call-done = bf16[256,512]{1,0:T(8,128)(2,1)} async-done(((bf16[2048,512]{1,0:T(8,128)(2,1)}), bf16[256,512]{1,0:T(8,128)(2,1)}) %reduce-scatter.14.cloned.1.call-update) | async-done | bytes 262160 | tf_op jit(solution)/shard_map/reduce_scatter | solution.py:241
  653.3 6.4 add_add_fusion.2
  659.7 30.3 %all-reduce.17.cloned.1.call-done = (bf16[64,1536]{1,0:T(8,128)(2,1)}, bf16[64,512]{1,0:T(8,128)(2,1)}, bf16[64,2048]{1,0:T(8,128)(2,1)}, bf16[256,512]{1,0:T(8,128)(2,1)}) async-done(((bf16[64,1536]{1,0:T(8,128)(2,1)}, bf16[64,512]{1,0:T(8,128)(2,1)}, bf16[64,2048]{1,0:T(8,128)(2,1)}, bf16[256,512]{1,0:T(8,128)(2,1)}), (bf16[64,1536]{1,0:T(8,128)(2,1)}, bf16[64,512]{1,0:T(8,128)(2,1)}, ...) | async-done | bytes 786448 | tf_op jit(solution)/shard_map/psum | solution.py:264
  690.0 1.5 convert_element_type.201
  691.5 1.7 convert_element_type.199
  693.2 1.8 convert_element_type.203
  695.0 1.8 convert_element_type.205
  (145 shorter events, 23.2 us)
Async XLA Ops:
  7.2 52.8 %copy-start.1 = (bf16[16,128,512]{2,1,0:T(8,128)(2,1)S(1)}, bf16[16,128,512]{2,1,0:T(8,128)(2,1)}, u32[]{:S(2)}) copy-start(bf16[16,128,512]{2,1,0:T(8,128)(2,1)} %param.13) | copy-start | bytes 6291460
  7.2 53.8 %copy-start.22 = (bf16[64,512]{1,0:T(8,128)(2,1)S(1)}, bf16[64,512]{1,0:T(8,128)(2,1)}, u32[]{:S(2)}) copy-start(bf16[64,512]{1,0:T(8,128)(2,1)} %param.17) | copy-start | bytes 196612
  7.2 89.4 %all-gather.6.cloned.1.call-start = ((), (), s32[]{:S(2)}) async-start(), calls=%async_computation.5 | async-start | bytes 1769472 | tf_op jit(solution)/shard_map/all_gather | solution.py:77
  7.9 163.4 %all-gather.8.cloned.1.call-start = ((), (), s32[]{:S(2)}) async-start(), calls=%async_computation.6 | async-start | bytes 2359296 | tf_op jit(solution)/shard_map/all_gather | solution.py:79
  8.7 218.7 %all-gather.10.cloned.1.call-start = ((), (), s32[]{:S(2)}) async-start(), calls=%async_computation.7 | async-start | bytes 2359296 | tf_op jit(solution)/shard_map/all_gather | solution.py:80
  9.4 370.9 %reduce-scatter.6.cloned.1.call-start = ((), (), s32[]{:S(2)}) async-start(), calls=%async_computation.8 | async-start | bytes 294912 | tf_op jit(solution)/shard_map/reduce_scatter | solution.py:214
  38.7 57.9 %copy-start.26 = (f32[512]{0:T(512)}, f32[512]{0:T(512)S(1)}, u32[]{:S(2)}) copy-start(f32[512]{0:T(512)S(1)} %convert_element_type.173) | copy-start | bytes 6148
  38.7 57.9 %copy-start.24 = (f32[512]{0:T(512)}, f32[512]{0:T(512)S(1)}, u32[]{:S(2)}) copy-start(f32[512]{0:T(512)S(1)} %convert_element_type.172) | copy-start | bytes 6148
  60.0 42.0 %copy-start.16 = (f32[16,128]{1,0:T(8,128)}, f32[16,128]{1,0:T(8,128)S(1)}, u32[]{:S(2)}) copy-start(f32[16,128]{1,0:T(8,128)S(1)} %broadcast_multiply_fusion.2) | copy-start | bytes 24580
  61.0 35.4 %copy-start.20 = (f32[16,128]{1,0:T(8,128)}, f32[16,128]{1,0:T(8,128)S(1)}, u32[]{:S(2)}) copy-start(f32[16,128]{1,0:T(8,128)S(1)} %fusion.24) | copy-start | bytes 24580
  61.0 41.0 %copy-start.18 = (f32[16,128]{1,0:T(8,128)}, f32[16,128]{1,0:T(8,128)S(1)}, u32[]{:S(2)}) copy-start(f32[16,128]{1,0:T(8,128)S(1)} %fusion.53) | copy-start | bytes 24580
  159.6 4.5 copy-start
  159.6 5.3 copy-start.10
  164.9 2.2 copy-start.14
  167.1 1.5 copy-start.12
  168.6 1.9 copy-start.2
  182.5 5.7 copy-start.8
  249.4 11.4 %copy-start.3 = (f32[16,128,512]{2,1,0:T(8,128)S(1)}, f32[16,128,512]{2,1,0:T(8,128)}, u32[]{:S(2)}) copy-start(f32[16,128,512]{2,1,0:T(8,128)} %copy-done.2) | copy-start | bytes 12582916
  260.8 1.7 copy-start.7
  262.5 2.0 copy-start.4
  264.5 1.3 copy-start.13
  268.6 15.8 %slice-start = ((s8[8912896]{0:T(1024)(128)(4,1)}), s8[524288]{0:T(1024)(128)(4,1)S(1)}, s32[]{:S(2)}) async-start(s8[8912896]{0:T(1024)(128)(4,1)} %bitcast.93), calls=%async_computation.14 | async-start | bytes 1048576
  272.7 11.7 %slice-start.1 = ((s8[8912896]{0:T(1024)(128)(4,1)}), s8[4194304]{0:T(1024)(128)(4,1)S(1)}, s32[]{:S(2)}) async-start(s8[8912896]{0:T(1024)(128)(4,1)} %bitcast.93), calls=%async_computation.15 | async-start | bytes 8388608
  272.7 11.7 %slice-start.2 = ((s8[8912896]{0:T(1024)(128)(4,1)}), s8[4194304]{0:T(1024)(128)(4,1)S(1)}, s32[]{:S(2)}) async-start(s8[8912896]{0:T(1024)(128)(4,1)} %bitcast.93), calls=%async_computation.16 | async-start | bytes 8388608
  272.7 11.6 %copy-start.6 = (bf16[16,128,512]{1,2,0:T(8,128)(2,1)S(1)}, bf16[16,128,512]{1,2,0:T(8,128)(2,1)}, u32[]{:S(2)}) copy-start(bf16[16,128,512]{1,2,0:T(8,128)(2,1)} %copy.98) | copy-start | bytes 6291460
  307.0 3.2 copy-start.5
  320.3 164.5 %reduce-scatter.10.cloned.1.call-start = ((), (), s32[]{:S(2)}) async-start(), calls=%async_computation.10 | async-start | bytes 589824 | tf_op jit(solution)/shard_map/reduce_scatter | solution.py:235
  350.8 30.3 %copy-start.23 = (f32[16,128]{1,0:T(8,128)S(1)}, f32[16,128]{1,0:T(8,128)}, u32[]{:S(2)}) copy-start(f32[16,128]{1,0:T(8,128)} %get-tuple-element.44) | copy-start | bytes 24580
  355.1 157.6 %reduce-scatter.8.cloned.1.call-start = ((), (), s32[]{:S(2)}) async-start(), calls=%async_computation.9 | async-start | bytes 1769472 | tf_op jit(solution)/shard_map/reduce_scatter | solution.py:232
  381.1 6.2 copy-start.15
  381.1 6.2 copy-start.17
  381.1 6.2 copy-start.19
  381.1 6.2 copy-start.25
  381.1 6.2 copy-start.27
  385.3 2.0 copy-start.11
  392.4 190.7 %reduce-scatter.12.cloned.1.call-start = ((), (), s32[]{:S(2)}) async-start(), calls=%async_computation.11 | async-start | bytes 2359296 | tf_op jit(solution)/shard_map/reduce_scatter | solution.py:238
  403.2 250.1 %reduce-scatter.14.cloned.1.call-start = ((), (), s32[]{:S(2)}) async-start(), calls=%async_computation.12 | async-start | bytes 2359296 | tf_op jit(solution)/shard_map/reduce_scatter | solution.py:241
  413.5 3.3 copy-start.28
  413.5 276.5 %all-reduce.17.cloned.1.call-start = ((), (), s32[]{:S(2)}) async-start(), calls=%async_computation.13 | async-start | bytes 1572864 | tf_op jit(solution)/shard_map/psum | solution.py:264
  417.1 6.4 copy-start.21
  423.5 2.0 copy-start.9
Sparse Core Ops, SparseCore 0:
  10.2 47.0 all-gather.5
  59.4 52.0 all-gather.7
  113.6 48.4 all-gather.9
  320.5 59.8 reduce-scatter.5
  384.1 61.0 reduce-scatter.9
  448.8 63.8 reduce-scatter.7
  516.2 66.7 reduce-scatter.11
  586.6 66.6 reduce-scatter.13
  655.9 34.0 all-reduce.16
where the time goes:
time: 710 us; the launch traced here: 704 us
  waiting for transfers between devices  226 us (32%)
  blocking collectives  147 us (21%)
  matrix products  141 us (20%)
  other arithmetic  90.3 us (13%)
  local copies, waits for them, and re-layouts  82 us (12%)
  between operations  17 us (2%)
    reduce_scatter x1, waiting for transfers between devices, local(): lax.psum_scatter(grad_widen.astype(jnp.bfloat16), 'shard', scatter_dimens...  70.3 us
    reduce_scatter x1, waiting for transfers between devices, local(): lax.psum_scatter(grad_narrow.astype(jnp.bfloat16), 'shard', scatter_dimen...  70.3 us
    unnamed x2, blocking collectives  58.5 us
    unnamed x87, local copies, waits for them, and re-layouts  41.4 us
    convert_element_type x1, other arithmetic, local(): activ_low = activation.astype(jnp.bfloat16)  39.2 us
    all_gather x1, blocking collectives, local(): lax.all_gather(project, 'shard', axis=0, tiled=True)  34.4 us
    all_gather x1, blocking collectives, local(): lax.all_gather(pooled.astype(jnp.bfloat16)[:, None, :], 'shard', axis=1,...  31.2 us
    psum x1, waiting for transfers between devices, local(): lax.psum(for_sending(tuple(shares)), 'rep')  30.3 us
  transfers between devices with their start and end apart: 9, of which 5 were waited for; matrix products, arithmetic and copies ran while one was open for 28% of the time, Pallas kernels for 0%

commit v1 on v0

v1 whole, which is shorter than its diff:
```python
import functools

import jax
import jax.numpy as jnp
from jax import lax
from jax.experimental import pallas as pl
from jax.experimental.pallas import tpu as pltpu
from jax.sharding import PartitionSpec as P

HEADS = 8
epsilon = 1e-05
masked = -1e30
F32 = jnp.float32
BF = jnp.bfloat16
MIB = 1 << 20


def dot(a, b):
    return jnp.dot(a, b, preferred_element_type=F32)


def dot_nt(a, b):
    return lax.dot_general(a, b, (((1,), (1,)), ((), ())), preferred_element_type=F32)


def dot_tn(a, b):
    return lax.dot_general(a, b, (((0,), (0,)), ((), ())), preferred_element_type=F32)


def normed(v):
    center = v - jnp.mean(v, axis=-1, keepdims=True)
    rstd = lax.rsqrt(jnp.mean(center * center, axis=-1, keepdims=True) + epsilon)
    return center * rstd, rstd


def norm_back(e, n, rstd):
    return rstd * (
        e - jnp.mean(e, axis=-1, keepdims=True) - n * jnp.mean(e * n, axis=-1, keepdims=True)
    )


def two_heads_lanes(t):
    half = t.shape[0] // 2
    zero = jnp.zeros((half, t.shape[1]), t.dtype)
    left = jnp.concatenate([t[:half], zero], axis=0)
    right = jnp.concatenate([zero, t[half:]], axis=0)
    return jnp.concatenate([left, right], axis=1)


def two_heads_rows(a):
    first = lax.broadcasted_iota(jnp.int32, a.shape, 1) < a.shape[1] // 2
    zero = jnp.zeros_like(a)
    return jnp.concatenate([jnp.where(first, a, zero), jnp.where(first, zero, a)], axis=0)


def diagonal(t):
    rows, cols = t.shape[0] // 2, t.shape[1] // 2
    return jnp.concatenate([t[:rows, :cols], t[rows:, cols:]], axis=0)


def span_bias(doc_from, pooled):
    span = doc_from.shape[1]
    key = lax.broadcasted_iota(jnp.int32, (span, span), 0)
    query = lax.broadcasted_iota(jnp.int32, (span, span), 1)
    direct = jnp.where((key >= doc_from) & (key <= query), 0.0, masked).astype(F32)
    both = jnp.concatenate([direct, pooled], axis=0)
    return jnp.concatenate([both, both], axis=1)


def copies(meta, sizes, pieces, place, sems):
    zs, xs = sizes
    z, x, core = meta[0], meta[1], meta[2]
    started = []
    for which in range(2):
        half = core if which == 0 else 1 - core
        for kx in range(xs):
            ref = pieces[which * xs + kx]
            for kz in range(zs):
                shard = lax.rem(z - kz + zs, zs) * xs + lax.rem(x - kx + xs, xs)
                for src, dst in place(ref, kz, shard, half):
                    copy = pltpu.make_async_copy(src, dst, sems.at[len(started)])
                    copy.start()
                    started.append(copy)
    for copy in started:
        copy.wait()


def pool_kernel(rel_ref, x_ref, out_ref, *, seqs, span):
    n, _ = normed(x_ref[...].astype(F32))
    for i in range(seqs):
        first = rel_ref[pl.program_id(0) * seqs + i]
        row = lax.broadcasted_iota(jnp.int32, (span, n.shape[1]), 0)
        part = jnp.where(row >= first, n[i * span : (i + 1) * span], 0.0)
        count = jnp.full((1, 1), span - first, jnp.int32).astype(F32)
        out_ref[i] = jnp.sum(part, axis=0, keepdims=True) / count


def attend_kernel(meta, *refs, sizes, seqs, span, npieces, rps):
    x_ref, gain_ref, shift_ref, pool_ref, from_ref, pbias_ref = refs[:6]
    pieces = refs[6 : 6 + npieces]
    w_ref, qkv_ref, o_ref, lse_ref, sems = refs[6 + npieces :]
    width = x_ref.shape[1]
    nh = w_ref.shape[1] // 2

    @pl.when(pl.program_id(0) == 0)
    def _():
        def place(ref, kz, shard, half):
            yield (
                ref.at[pl.ds(kz * rps, rps), :],
                w_ref.at[
                    pl.ds(pl.multiple_of(shard * rps, rps), rps),
                    pl.ds(pl.multiple_of(half * nh, 128), nh),
                ],
            )

        copies(meta, sizes, pieces, place, sems)

    gain, shift = gain_ref[...], shift_ref[...]
    n, _ = normed(x_ref[...].astype(F32))
    h = (n * gain + shift).astype(BF)
    qkv = dot(h, w_ref[...]).astype(BF)
    q = qkv[:, :width] * jnp.asarray((width // HEADS) ** -0.5, BF)
    qkv_ref[:, :width] = q
    qkv_ref[:, width:] = qkv[:, width:]
    cp = pool_ref.shape[1]
    pooled_h = pool_ref[...].astype(F32).reshape(seqs * cp, width) * gain + shift
    kvb = dot(pooled_h.astype(BF), w_ref[:, width:]).astype(BF)
    for s in range(seqs):
        rows = slice(s * span, (s + 1) * span)
        prow = slice(s * cp, (s + 1) * cp)
        bias = span_bias(from_ref[s], pbias_ref[s])
        for p in range(HEADS // 2):
            col = slice(p * 128, (p + 1) * 128)
            kcol = slice(width + p * 128, width + (p + 1) * 128)
            vcol = slice(2 * width + p * 128, 2 * width + (p + 1) * 128)
            keys = jnp.concatenate([qkv[rows, kcol], kvb[prow, col]], axis=0)
            vals = jnp.concatenate(
                [qkv[rows, vcol], kvb[prow, width + p * 128 : width + (p + 1) * 128]], axis=0
            )
            scores = dot(keys, two_heads_lanes(q[rows, col].T)) + bias
            top = jnp.max(scores, axis=0, keepdims=True)
            e = jnp.exp(scores - top)
            total = jnp.sum(e, axis=0, keepdims=True)
            prob = (e * (1.0 / total)).astype(BF)
            lse_ref[s, p : p + 1, :] = top + jnp.log(total)
            out = diagonal(dot_tn(vals, prob)).astype(BF)
            o_ref[rows, col] = out.T


def ffn_kernel(meta, *refs, sizes, npieces, rps, chunk):
    o_ref, x_ref, y_ref, hb_ref, fb_ref, gain_ref, shift_ref = refs[:7]
    pieces = refs[7 : 7 + npieces]
    (
        out_ref,
        dr_ref,
        keep_ref,
        send_ref,
        wp_ref,
        vec_ref,
        w1_ref,
        w2_ref,
        acc1_ref,
        acc2_ref,
        accp_ref,
        sems,
    ) = refs[7 + npieces :]
    width, hidden = w1_ref.shape
    per = hidden // width
    ph, wh = width // 2, hidden // 2
    step = pl.program_id(0)

    @pl.when(step == 0)
    def _():
        def place(ref, kz, shard, half):
            src = pl.ds(kz * rps, rps)
            row = pl.ds(pl.multiple_of(shard * rps, rps), rps)
            yield (
                ref.at[src, pl.ds(0, ph)],
                wp_ref.at[row, pl.ds(pl.multiple_of(half * ph, 128), ph)],
            )
            yield (
                ref.at[src, pl.ds(ph, wh)],
                w1_ref.at[row, pl.ds(pl.multiple_of(half * wh, 128), wh)],
            )
            for j in range(per // 2):
                at = (shard * per + half * (per // 2) + j) * rps
                yield (
                    ref.at[src, pl.ds(ph + wh + j * width, width)],
                    w2_ref.at[pl.ds(pl.multiple_of(at, rps), rps), :],
                )

        copies(meta, sizes, pieces, place, sems)
        acc1_ref[...] = jnp.zeros_like(acc1_ref)
        acc2_ref[...] = jnp.zeros_like(acc2_ref)
        accp_ref[...] = jnp.zeros_like(accp_ref)
        vec_ref[...] = jnp.zeros_like(vec_ref)

    o, y = o_ref[...], y_ref[...]
    r1 = x_ref[...].astype(F32) + dot(o, wp_ref[...])
    n, rstd = normed(r1)
    h = (n * gain_ref[...] + shift_ref[...]).astype(BF)
    ht = h.T
    out = r1 + fb_ref[...]
    dh = jnp.zeros_like(r1)
    for j in range(hidden // chunk):
        at = slice(j * chunk, (j + 1) * chunk)
        u = dot(h, w1_ref[:, at]) + hb_ref[:, at]
        da = dot_nt(y, w2_ref[at, :])
        cdf = 0.5 + 0.5 * lax.erf(u * 0.7071067811865476)
        pdf = jnp.exp(u * u * -0.5) * 0.3989422804014327
        a = (u * cdf).astype(BF)
        du = (da * (cdf + u * pdf)).astype(BF)
        out += dot(a, w2_ref[at, :])
        dh += dot_nt(du, w1_ref[:, at])
        acc1_ref[:, at] += dot(ht, du)
        acc2_ref[at, :] += dot_tn(a, y)
        vec_ref[0:1, at] += jnp.sum(du.astype(F32), axis=0, keepdims=True)
    out_ref[...] = out
    yf = y.astype(F32)
    dr = yf + norm_back(dh * gain_ref[...], n, rstd)
    dr_ref[...] = dr
    accp_ref[...] += dot_tn(o, dr.astype(BF))
    vec_ref[1:2, :width] += jnp.sum(yf, axis=0, keepdims=True)
    vec_ref[2:3, :width] += jnp.sum(dh * n, axis=0, keepdims=True)
    vec_ref[3:4, :width] += jnp.sum(dh, axis=0, keepdims=True)

    @pl.when(step == pl.num_programs(0) - 1)
    def _():
        for which, ref in ((0, keep_ref), (1, send_ref)):
            half = meta[2] if which == 0 else 1 - meta[2]
            pcol = pl.ds(pl.multiple_of(half * ph, 128), ph)
            ref[:, :ph] = accp_ref[:, pcol].astype(BF)
            ref[:, ph : ph + wh] = acc1_ref[:, pl.ds(pl.multiple_of(half * wh, 128), wh)].astype(BF)
            for shard in range(width // rps):
                for j in range(per):
                    at = (shard * per + j) * rps
                    ref[shard * rps : (shard + 1) * rps, ph + wh + j * ph : ph + wh + (j + 1) * ph] = (
                        acc2_ref[at : at + rps, pcol].astype(BF)
                    )


def back_kernel(
    meta,
    dr_ref,
    x_ref,
    qkv_ref,
    lse_ref,
    w_ref,
    wp_ref,
    gain_ref,
    shift_ref,
    pool_ref,
    from_ref,
    pbias_ref,
    part_ref,
    dpool_ref,
    keep_ref,
    send_ref,
    vec_ref,
    acc_ref,
    dqkv_ref,
    dkvb_ref,
    *,
    seqs,
    span,
):
    width = x_ref.shape[1]
    scale = (width // HEADS) ** -0.5
    step = pl.program_id(0)

    @pl.when(step == 0)
    def _():
        acc_ref[...] = jnp.zeros_like(acc_ref)
        vec_ref[...] = jnp.zeros_like(vec_ref)

    gain, shift = gain_ref[...], shift_ref[...]
    cp = pool_ref.shape[1]
    pool = pool_ref[...].astype(F32).reshape(seqs * cp, width)
    pooled_h = (pool * gain + shift).astype(BF)
    kvb = dot(pooled_h, w_ref[:, width:]).astype(BF)
    dr = dr_ref[...]
    do = dot_nt(dr.astype(BF), wp_ref[...]).astype(BF)
    for s in range(seqs):
        rows = slice(s * span, (s + 1) * span)
        prow = slice(s * cp, (s + 1) * cp)
        bias = span_bias(from_ref[s], pbias_ref[s])
        for p in range(HEADS // 2):
            col = slice(p * 128, (p + 1) * 128)
            kcol = slice(width + p * 128, width + (p + 1) * 128)
            vcol = slice(2 * width + p * 128, 2 * width + (p + 1) * 128)
            v2col = slice(width + p * 128, width + (p + 1) * 128)
            q = qkv_ref[rows, col]
            g = do[rows, col]
            keys = jnp.concatenate([qkv_ref[rows, kcol], kvb[prow, col]], axis=0)
            vals = jnp.concatenate([qkv_ref[rows, vcol], kvb[prow, v2col]], axis=0)
            scores = dot(keys, two_heads_lanes(q.T)) + bias
            prob = jnp.exp(scores - lse_ref[s, p : p + 1, :])
            dprob = dot(vals, two_heads_lanes(g.T))
            weighted = prob * dprob
            ds = (weighted - prob * jnp.sum(weighted, axis=0, keepdims=True)).astype(BF)
            dq = (diagonal(dot_tn(keys, ds)) * scale).astype(BF)
            dk = dot(ds, two_heads_rows(q)).astype(BF)
            dv = dot(prob.astype(BF), two_heads_rows(g)).astype(BF)
            dqkv_ref[rows, col] = dq.T
            dqkv_ref[rows, kcol] = dk[:span]
            dqkv_ref[rows, vcol] = dv[:span]
            dkvb_ref[prow, col] = dk[span:]
            dkvb_ref[prow, v2col] = dv[span:]
    n, rstd = normed(x_ref[...].astype(F32))
    h = (n * gain + shift).astype(BF)
    dqkv, dkvb = dqkv_ref[...], dkvb_ref[...]
    acc_ref[...] += dot_tn(h, dqkv)
    acc_ref[:, width:] += dot_tn(pooled_h, dkvb)
    dh = dot_nt(dqkv, w_ref[...])
    dpool = dot_nt(dkvb, w_ref[:, width:])
    dpool_ref[...] = dpool.astype(BF).reshape(seqs, cp, width)
    vec_ref[0:1, :] += jnp.sum(dh * n, axis=0, keepdims=True) + jnp.sum(
        dpool * pool, axis=0, keepdims=True
    )
    vec_ref[1:2, :] += jnp.sum(dh, axis=0, keepdims=True) + jnp.sum(dpool, axis=0, keepdims=True)
    part_ref[...] = dr + norm_back(dh * gain, n, rstd)

    @pl.when(step == pl.num_programs(0) - 1)
    def _():
        nh = acc_ref.shape[1] // 2
        for which, ref in ((0, keep_ref), (1, send_ref)):
            half = meta[2] if which == 0 else 1 - meta[2]
            ref[...] = acc_ref[:, pl.ds(pl.multiple_of(half * nh, 128), nh)].astype(BF)


def last_kernel(rel_ref, part_ref, x_ref, dpool_ref, gain_ref, out_ref, *, seqs, span):
    n, rstd = normed(x_ref[...].astype(F32))
    for i in range(seqs):
        first = rel_ref[pl.program_id(0) * seqs + i]
        rows = slice(i * span, (i + 1) * span)
        count = jnp.full((1, 1), span - first, jnp.int32).astype(F32)
        share = dpool_ref[i] / count * gain_ref[...]
        row = lax.broadcasted_iota(jnp.int32, (span, n.shape[1]), 0)
        e = jnp.where(row >= first, share, 0.0)
        out_ref[rows, :] = part_ref[rows, :] + norm_back(e, n[rows], rstd[rows])


def params(mib):
    return pltpu.CompilerParams(
        dimension_semantics=("arbitrary",), vmem_limit_bytes=mib * MIB
    )


def local(
    tokens,
    cotangent,
    doc_lengths,
    attend,
    project,
    widen,
    narrow,
    hidden_bias,
    final_bias,
    gain_first,
    shift_first,
    gain_second,
    shift_second,
    *,
    sizes,
):
    zs, xs, ys, cs = sizes
    nshard = zs * xs
    seq_count, span, width = tokens.shape
    rows = seq_count * span
    hidden = widen.shape[1]
    rps = attend.shape[0]
    rep, shard = lax.axis_index("rep"), lax.axis_index("shard")
    z, x, y, core = shard // xs, shard % xs, rep // cs, rep % cs
    meta = jnp.stack([z, x, core]).astype(jnp.int32)

    def send(a, dz=0, dx=0, dy=0, dc=0):
        perm = []
        for r in range(ys * cs):
            for s in range(nshard):
                r2 = (r // cs + dy) % ys * cs + (r % cs + dc) % cs
                s2 = (s // xs + dz) % zs * xs + (s % xs + dx) % xs
                perm.append((r * nshard + s, r2 * nshard + s2))
        return lax.ppermute(a, ("rep", "shard"), perm)

    def gather(a):
        col = jnp.concatenate([a] + [send(a, dz=k) for k in range(1, zs)], axis=0)
        return [col] + [send(col, dx=k) for k in range(1, xs)]

    def gather_halves(a):
        mine = gather(a)
        return mine + [send(m, dc=1) for m in mine]

    ndoc = doc_lengths.shape[1]
    upto = jnp.arange(ndoc)[:, None] <= jnp.arange(ndoc)[None, :]
    ends = jnp.sum(jnp.where(upto[None], doc_lengths[:, :, None], 0), axis=1, dtype=jnp.int32)
    starts = ends - doc_lengths
    base = shard * span
    positions = base + jnp.arange(span, dtype=jnp.int32)
    segment = jnp.sum(
        (positions[None, :, None] >= ends[:, None, :]).astype(jnp.int32), axis=-1, dtype=jnp.int32
    )

    def start_at(at):
        before = starts[:, None, :] <= at[..., None]
        return jnp.max(jnp.where(before, starts[:, None, :], 0), axis=-1)

    doc_from = (start_at(positions[None, :]) - base)[:, None, :]
    slot = jnp.arange(nshard, dtype=jnp.int32)
    slot_span = (z - slot % zs + zs) % zs * xs + (x - slot // zs + xs) % xs
    slot_last = slot_span * span + span - 1
    last_doc = jnp.sum(
        (slot_last[None, :, None] >= ends[:, None, :]).astype(jnp.int32), axis=-1, dtype=jnp.int32
    )
    counts = jnp.minimum(span, slot_last[None, :] + 1 - start_at(slot_last[None, :]))
    seen = (slot_span[None, :, None] < shard) & (last_doc[:, :, None] == segment[:, None, :])
    pbias = jnp.where(seen, jnp.log(counts.astype(F32))[:, :, None], masked)
    cp = max(16, -(-nshard // 16) * 16)
    pbias = jnp.pad(pbias, ((0, 0), (0, cp - nshard), (0, 0)), constant_values=masked)
    rel = span - counts[:, 0]

    nh = attend.shape[1] // 2
    attend_parts = gather_halves(lax.dynamic_slice_in_dim(attend, core * nh, nh, 1))
    x2 = tokens.reshape(rows, width)
    y2 = cotangent.reshape(rows, width)
    smem = pl.BlockSpec(memory_space=pltpu.SMEM)
    hbm = pl.BlockSpec(memory_space=pl.ANY)
    pool_seqs = 4
    pool = pl.pallas_call(
        functools.partial(pool_kernel, seqs=pool_seqs, span=span),
        grid=(seq_count // pool_seqs,),
        in_specs=[smem, pl.BlockSpec((pool_seqs * span, width), lambda i: (i, 0))],
        out_specs=pl.BlockSpec((pool_seqs, 1, width), lambda i: (i, 0, 0)),
        out_shape=jax.ShapeDtypeStruct((seq_count, 1, width), F32),
        compiler_params=params(16),
        name="pool",
    )(rel, x2)
    small = jnp.concatenate(
        [hidden_bias, final_bias, gain_first, shift_first, gain_second, shift_second]
    )
    nsmall = small.shape[0]
    srows = -(-nsmall // width)
    small = jnp.pad(small, (0, srows * width - nsmall)).reshape(srows, width)
    packed = jnp.concatenate([pool.reshape(seq_count, width).astype(BF), small], axis=0)
    slots = jnp.concatenate(gather(packed), axis=0).reshape(nshard, seq_count + srows, width)
    pool_all = jnp.transpose(slots[:, :seq_count], (1, 0, 2))
    pool_all = jnp.pad(pool_all, ((0, 0), (0, cp - nshard), (0, 0)))
    which = slot_span[None, :] == jnp.arange(nshard)[:, None]
    values = slots[:, seq_count:].reshape(nshard, srows * width).astype(F32)
    values = jnp.sum(jnp.where(which[:, :, None], values[None], 0.0), axis=1)
    hs = hidden_bias.shape[0]
    hidden_all = values[:, :hs].reshape(1, hidden)
    final_all, gain1, shift1, gain2, shift2 = (
        values[:, hs + i * rps : hs + (i + 1) * rps].reshape(1, width) for i in range(5)
    )

    per = hidden // width
    ph, wh = width // 2, hidden // 2
    nhalf = lax.dynamic_slice_in_dim(narrow, core * (narrow.shape[0] // 2), narrow.shape[0] // 2, 0)
    ffn_half = jnp.concatenate(
        [
            lax.dynamic_slice_in_dim(project, core * ph, ph, 1),
            lax.dynamic_slice_in_dim(widen, core * wh, wh, 1),
        ]
        + [nhalf[j * rps : (j + 1) * rps] for j in range(per // 2)],
        axis=1,
    )
    ffn_parts = gather_halves(ffn_half)

    seqs = 2
    row_spec = lambda n, w: pl.BlockSpec((n, w), lambda i, m: (i, 0))
    all_spec = lambda a, b: pl.BlockSpec((a, b), lambda i, m: (0, 0))
    seq_spec = lambda n, a, b: pl.BlockSpec((n, a, b), lambda i, m: (i, 0, 0))
    npieces = 2 * xs
    w_all, qkv, o, lse = pl.pallas_call(
        functools.partial(
            attend_kernel, sizes=(zs, xs), seqs=seqs, span=span, npieces=npieces, rps=rps
        ),
        grid_spec=pltpu.PrefetchScalarGridSpec(
            num_scalar_prefetch=1,
            grid=(seq_count // seqs,),
            in_specs=[
                row_spec(seqs * span, width),
                all_spec(1, width),
                all_spec(1, width),
                seq_spec(seqs, cp, width),
                seq_spec(seqs, 1, span),
                seq_spec(seqs, cp, span),
            ]
            + [hbm] * npieces,
            out_specs=[
                all_spec(width, 3 * width),
                row_spec(seqs * span, 3 * width),
                row_spec(seqs * span, width),
                seq_spec(seqs, HEADS // 2, 2 * span),
            ],
            scratch_shapes=[pltpu.SemaphoreType.DMA((2 * nshard,))],
        ),
        out_shape=[
            jax.ShapeDtypeStruct((width, 3 * width), BF),
            jax.ShapeDtypeStruct((rows, 3 * width), BF),
            jax.ShapeDtypeStruct((rows, width), BF),
            jax.ShapeDtypeStruct((seq_count, HEADS // 2, 2 * span), F32),
        ],
        compiler_params=params(40),
        name="attention",
    )(meta, x2, gain1, shift1, pool_all, doc_from, pbias, *attend_parts)

    tile = 256
    packet = ph + wh + per * ph
    block_out, dr, keep_f, send_f, wp_all, vec_f = pl.pallas_call(
        functools.partial(ffn_kernel, sizes=(zs, xs), npieces=npieces, rps=rps, chunk=512),
        grid_spec=pltpu.PrefetchScalarGridSpec(
            num_scalar_prefetch=1,
            grid=(rows // tile,),
            in_specs=[
                row_spec(tile, width),
                row_spec(tile, width),
                row_spec(tile, width),
                all_spec(1, hidden),
                all_spec(1, width),
                all_spec(1, width),
                all_spec(1, width),
            ]
            + [hbm] * npieces,
            out_specs=[
                row_spec(tile, width),
                row_spec(tile, width),
                all_spec(width, packet),
                all_spec(width, packet),
                all_spec(width, width),
                all_spec(8, hidden),
            ],
            scratch_shapes=[
                pltpu.VMEM((width, hidden), BF),
                pltpu.VMEM((hidden, width), BF),
                pltpu.VMEM((width, hidden), F32),
                pltpu.VMEM((hidden, width), F32),
                pltpu.VMEM((width, width), F32),
                pltpu.SemaphoreType.DMA((2 * nshard * (2 + per // 2),)),
            ],
        ),
        out_shape=[
            jax.ShapeDtypeStruct((rows, width), F32),
            jax.ShapeDtypeStruct((rows, width), F32),
            jax.ShapeDtypeStruct((width, packet), BF),
            jax.ShapeDtypeStruct((width, packet), BF),
            jax.ShapeDtypeStruct((width, width), BF),
            jax.ShapeDtypeStruct((8, hidden), F32),
        ],
        compiler_params=params(56),
        name="ffn",
    )(meta, o, x2, y2, hidden_all, final_all, gain2, shift2, *ffn_parts)

    seqs = 4
    part, dpool, keep_a, send_a, vec_a = pl.pallas_call(
        functools.partial(back_kernel, seqs=seqs, span=span),
        grid_spec=pltpu.PrefetchScalarGridSpec(
            num_scalar_prefetch=1,
            grid=(seq_count // seqs,),
            in_specs=[
                row_spec(seqs * span, width),
                row_spec(seqs * span, width),
                row_spec(seqs * span, 3 * width),
                seq_spec(seqs, HEADS // 2, 2 * span),
                all_spec(width, 3 * width),
                all_spec(width, width),
                all_spec(1, width),
                all_spec(1, width),
                seq_spec(seqs, cp, width),
                seq_spec(seqs, 1, span),
                seq_spec(seqs, cp, span),
            ],
            out_specs=[
                row_spec(seqs * span, width),
                seq_spec(seqs, cp, width),
                all_spec(width, 3 * width // 2),
                all_spec(width, 3 * width // 2),
                all_spec(8, width),
            ],
            scratch_shapes=[
                pltpu.VMEM((width, 3 * width), F32),
                pltpu.VMEM((seqs * span, 3 * width), BF),
                pltpu.VMEM((seqs * cp, 2 * width), BF),
            ],
        ),
        out_shape=[
            jax.ShapeDtypeStruct((rows, width), F32),
            jax.ShapeDtypeStruct((seq_count, cp, width), BF),
            jax.ShapeDtypeStruct((width, 3 * width // 2), BF),
            jax.ShapeDtypeStruct((width, 3 * width // 2), BF),
            jax.ShapeDtypeStruct((8, width), F32),
        ],
        compiler_params=params(56),
        name="back",
    )(meta, dr, x2, qkv, lse, w_all, wp_all, gain1, shift1, pool_all, doc_from, pbias)

    def add(parts, kind):
        total = parts[0].astype(F32)
        for p in parts[1:]:
            total = total + p.astype(F32)
        return total.astype(kind)

    def reduce_packet(keep, sent):
        kind = keep.dtype
        part = add([keep, send(sent, dc=1)], kind)
        n = part.shape[1] // ys
        k = part.shape[0] // nshard
        view = part.reshape(zs, xs, k, ys * n)

        def corner(dx, dy):
            at = (0, (x + dx) % xs, 0, (y + dy) % ys * n)
            return lax.dynamic_slice(view, at, (zs, 1, k, n)).reshape(zs * k, n)

        part = add(
            [
                send(corner(dx, dy), dx=dx, dy=dy) if dx or dy else corner(0, 0)
                for dx in range(xs)
                for dy in range(ys)
            ],
            kind,
        )
        level = lambda dz: lax.dynamic_slice_in_dim(part, (z + dz) % zs * k, k, 0)
        part = add([send(level(dz), dz=dz) if dz else level(0) for dz in range(zs)], kind)
        total = []
        found = {
            (dy, dc): send(part, dy=dy, dc=dc) if dy or dc else part
            for dy in range(ys)
            for dc in range(cs)
        }
        for at in range(ys * cs):
            picked = jnp.zeros(part.shape, F32)
            for (dy, dc), piece in found.items():
                mine = ((y - dy + ys) % ys == at % ys) & ((core - dc + cs) % cs == at // ys)
                picked = jnp.where(mine, piece.astype(F32), picked)
            total.append(picked)
        return jnp.concatenate(total, axis=1)

    grad_f = reduce_packet(keep_f, send_f)
    halves = [grad_f[:, i * packet : (i + 1) * packet] for i in range(2)]
    grad_project = jnp.concatenate([h[:, :ph] for h in halves], axis=1)
    grad_widen = jnp.concatenate([h[:, ph : ph + wh] for h in halves], axis=1)
    grad_narrow = jnp.concatenate(
        [
            jnp.concatenate(
                [h[:, ph + wh + j * ph : ph + wh + (j + 1) * ph] for h in halves], axis=1
            )
            for j in range(per)
        ],
        axis=0,
    )
    grad_attend = reduce_packet(keep_a, send_a)

    dp = jnp.transpose(dpool[:, :nshard], (1, 0, 2)).reshape(xs, zs, seq_count, width)
    level = add([send(dp[:, k], dz=-k) if k else dp[:, 0] for k in range(zs)], BF)
    own = add([send(level[k], dx=-k) if k else level[0] for k in range(xs)], F32)
    seqs = 4
    tokens_grad = pl.pallas_call(
        functools.partial(last_kernel, seqs=seqs, span=span),
        grid=(seq_count // seqs,),
        in_specs=[
            smem,
            pl.BlockSpec((seqs * span, width), lambda i: (i, 0)),
            pl.BlockSpec((seqs * span, width), lambda i: (i, 0)),
            pl.BlockSpec((seqs, 1, width), lambda i: (i, 0, 0)),
            pl.BlockSpec((1, width), lambda i: (0, 0)),
        ],
        out_specs=pl.BlockSpec((seqs * span, width), lambda i: (i, 0)),
        out_shape=jax.ShapeDtypeStruct((rows, width), F32),
        compiler_params=params(24),
        name="last",
    )(rel, part, x2, own.reshape(seq_count, 1, width), gain1)

    vec = jnp.concatenate(
        [vec_f[0].reshape(nshard, hs)]
        + [
            v.reshape(nshard, rps)
            for v in (vec_f[1, :width], vec_a[0], vec_a[1], vec_f[2, :width], vec_f[3, :width])
        ],
        axis=1,
    )
    quarter = -(-vec.shape[1] // (ys * cs * 128)) * 128
    vec = jnp.pad(vec, ((0, 0), (0, quarter * ys * cs - vec.shape[1])))
    half = quarter * ys
    vec = reduce_packet(
        lax.dynamic_slice_in_dim(vec, core * half, half, 1),
        lax.dynamic_slice_in_dim(vec, (1 - core) * half, half, 1),
    )[0]
    vecs = [vec[:hs]] + [vec[hs + i * rps : hs + (i + 1) * rps] for i in range(5)]
    return (
        block_out.reshape(tokens.shape),
        tokens_grad.reshape(tokens.shape),
        grad_attend,
        grad_project,
        grad_widen,
        grad_narrow,
        *vecs,
    )


def solution(mesh):
    first = mesh.devices[0]
    xs = len({d.coords[0] for d in first})
    cs = len({d.core_on_chip for d in mesh.devices[:, 0]})
    sizes = (mesh.shape["shard"] // xs, xs, mesh.shape["rep"] // cs, cs)
    row = P("shard", None)
    vec = P("shard")
    act = P("rep", "shard", None)
    return jax.shard_map(
        functools.partial(local, sizes=sizes),
        mesh=mesh,
        in_specs=(act, act, P("rep", None), row, row, row, row) + (vec,) * 6,
        out_specs=(act, act, row, row, row, row) + (vec,) * 6,
        check_vma=False,
    )
```

time: 710 us -> 300 us (0.42)
  blocking collectives: 147 us -> 0 us
  matrix products: 141 us -> 0 us
  waiting for transfers between devices: 226 us -> 88.1 us
  Pallas kernels: 0 us -> 116 us
  other arithmetic: 90.3 us -> 12 us
  local copies, waits for them, and re-layouts: 82 us -> 17.4 us
  starting transfers between devices: 0.61 us -> 64.1 us
  between operations: 17 us -> 1.43 us
    reduce_scatter x5 -> x0, waiting for transfers between devices: 194 us -> none  [the longest x1 70.3 us: local(): lax.psum_scatter(grad_widen.astype(jnp.bfloat16), 'shard', scatter_dimens...]
    dot_general x19 -> x0, matrix products: 141 us -> none  [the longest x1 22 us: local(): jnp.einsum('std,fd->stf', cotangent, narrow_back, preferred_element_type=...]
    pallas_call x0 -> x5, Pallas kernels: none -> 116 us  [the longest x1 46.6 us: local(): pl.pallas_call(functools.partial(ffn_kernel, sizes=(zs, xs), npieces=npie...]
    ppermute x0 -> x50, waiting for transfers between devices: none -> 88.1 us  [send(): return lax.ppermute(a, ('rep', 'shard'), perm)]
    all_gather x3 -> x0, blocking collectives: 81.9 us -> none  [the longest x1 34.4 us: local(): lax.all_gather(project, 'shard', axis=0, tiled=True)]
    ppermute x0 -> x50, starting transfers between devices: none -> 64.1 us  [send(): return lax.ppermute(a, ('rep', 'shard'), perm)]
    unnamed x2 -> x0, blocking collectives: 58.5 us -> none
    convert_element_type x21 -> x8, other arithmetic: 60.1 us -> 2.65 us  [the longest x7 2.62 us: add(): return total.astype(kind)]
  transfers between devices with their start and end apart: 9 -> 50, of which waited for: 5 -> 24; matrix products, arithmetic and copies ran while one was open for 28% -> 5% of each run, Pallas kernels for 0% -> 11%
where the time goes in v1:
time: 300 us; the launch traced here: 299 us
  Pallas kernels  116 us (39%)
  waiting for transfers between devices  88.1 us (29%)
  starting transfers between devices  64.1 us (21%)
  local copies, waits for them, and re-layouts  17.4 us (6%)
  other arithmetic  12 us (4%)
    ppermute x50, waiting for transfers between devices, send(): return lax.ppermute(a, ('rep', 'shard'), perm)  88.1 us
    ppermute x50, starting transfers between devices, send(): return lax.ppermute(a, ('rep', 'shard'), perm)  64.1 us
    pallas_call x1, Pallas kernels, local(): pl.pallas_call(functools.partial(ffn_kernel, sizes=(zs, xs), npieces=npie...  46.6 us
    pallas_call x1, Pallas kernels, local(): pl.pallas_call(functools.partial(back_kernel, seqs=seqs, span=span), grid...  35 us
    pallas_call x1, Pallas kernels, local(): pl.pallas_call(functools.partial(attend_kernel, sizes=(zs, xs), seqs=seqs...  27.2 us
    unnamed x56, local copies, waits for them, and re-layouts  6.61 us
  transfers between devices with their start and end apart: 50, of which 24 were waited for; matrix products, arithmetic and copies ran while one was open for 5% of the time, Pallas kernels for 11%

profile of v1, /device:TPU:0, one launch (start us, length us, event | category | flops | bytes accessed | tf_op | source)
XLA Modules:
  0.0 298.6 jit_solution(16946161174611291019)
XLA Ops:
  0.7 1.0 constant_dynamic-slice_fusion.26
  3.3 3.0 %collective-permute-start.10 = (bf16[64,2304]{1,0:T(8,128)(2,1)}, bf16[64,2304]{1,0:T(8,128)(2,1)S(1)}, u32[]{:S(2)}, u32[]{:S(2)}) collective-permute-start(bf16[64,2304]{1,0:T(8,128)(2,1)} %pad_maximum_fusion.4), channel_id=1, source_target_pairs={{0,2},{1,3},{2,4},{3,5},{4,6},{5,7},{6,0},{7,1},{8,10},{9,11},{10,... | collective-permute-start | bytes 884744 | tf_op jit(solution)/shard_map/ppermute | solution.py:383
  6.3 2.6 collective-permute-start.11
  8.9 1.3 collective-permute-start.12
  12.6 3.9 %collective-permute-done.10 = bf16[64,2304]{1,0:T(8,128)(2,1)S(1)} collective-permute-done((bf16[64,2304]{1,0:T(8,128)(2,1)}, bf16[64,2304]{1,0:T(8,128)(2,1)S(1)}, u32[]{:S(2)}, u32[]{:S(2)}) %collective-permute-start.10) | collective-permute-done | bytes 294944 | tf_op jit(solution)/shard_map/ppermute | solution.py:383
  16.5 11.8 %collective-permute-done.11 = bf16[64,2304]{1,0:T(8,128)(2,1)S(1)} collective-permute-done((bf16[64,2304]{1,0:T(8,128)(2,1)}, bf16[64,2304]{1,0:T(8,128)(2,1)S(1)}, u32[]{:S(2)}, u32[]{:S(2)}) %collective-permute-start.11) | collective-permute-done | bytes 294944 | tf_op jit(solution)/shard_map/ppermute | solution.py:383
  28.3 1.1 pad_maximum_fusion.refs_7_
  29.4 1.5 collective-permute-start.13
  31.0 2.2 pool.1
  33.5 6.8 %collective-permute-start = (bf16[18,512]{1,0:T(8,128)(2,1)S(1)}, bf16[18,512]{1,0:T(8,128)(2,1)S(1)}, u32[]{:S(2)}, u32[]{:S(2)}) collective-permute-start(bf16[18,512]{1,0:T(8,128)(2,1)S(1)} %pad_maximum_fusion.6), channel_id=1, source_target_pairs={{0,2},{1,3},{2,4},{3,5},{4,6},{5,7},{6,0},{7,1},{8,10},{9,11},{10,... | collective-permute-start | bytes 55304 | tf_op jit(solution)/shard_map/ppermute | solution.py:383
  40.3 1.6 collective-permute-start.1
  42.7 0.9 constant_dynamic-slice_fusion.25
  43.6 1.2 collective-permute-start.4
  45.1 1.4 collective-permute-start.5
  46.5 1.6 collective-permute-start.6
  48.1 9.4 %collective-permute-done.13.refs_8_ = bf16[256,2304]{1,0:T(8,128)(2,1)} collective-permute-done((bf16[256,2304]{1,0:T(8,128)(2,1)}, bf16[256,2304]{1,0:T(8,128)(2,1)}, u32[]{:S(2)}, u32[]{:S(2)}) %collective-permute-start.13) | collective-permute-done | bytes 1179680 | tf_op jit(solution)/shard_map/ppermute | solution.py:383
  58.0 1.6 collective-permute-start.3
  60.3 2.7 collective-permute-done.3
  64.0 7.2 %collective-permute-done.7.refs_7_ = bf16[256,768]{1,0:T(8,128)(2,1)S(1)} collective-permute-done((bf16[256,768]{1,0:T(8,128)(2,1)S(1)}, bf16[256,768]{1,0:T(8,128)(2,1)S(1)}, u32[]{:S(2)}, u32[]{:S(2)}) %collective-permute-start.7) | collective-permute-done | bytes 393248 | tf_op jit(solution)/shard_map/ppermute | solution.py:383
  74.1 27.2 %attention.1 = (bf16[512,1536]{1,0:T(8,128)(2,1)S(1)}, bf16[2048,1536]{1,0:T(8,128)(2,1)S(1)}, bf16[2048,512]{1,0:T(8,128)(2,1)S(1)}, f32[16,4,256]{2,1,0:T(4,128)S(1)}) custom-call(s32[3]{0:T(128)S(1)} %pad_add_fusion.meta, bf16[2048,512]{1,0:T(8,128)(2,1)S(1)} %bitcast.95, f32[1,512]{1,0:T(1,128)S(1)} %reshape.311.refs_1_.gain_ref, ...), custom_call_target="tpu_custom_call" | custom-call | tf_op jit(solution)/shard_map/attention/pallas_call | solution.py:474
  101.3 2.7 copy-done.4
  103.9 1.4 copy-done.7
  105.3 1.1 copy-done.8
  107.1 46.6 %ffn.1 = (f32[2048,512]{1,0:T(8,128)}, f32[2048,512]{1,0:T(8,128)}, bf16[512,2304]{1,0:T(8,128)(2,1)}, bf16[512,2304]{1,0:T(8,128)(2,1)}, bf16[512,512]{1,0:T(8,128)(2,1)}, /*index=5*/f32[8,2048]{1,0:T(8,128)}) custom-call(s32[3]{0:T(128)} %copy-done.15, bf16[2048,512]{1,0:T(8,128)(2,1)} %copy-done.7, bf16[2048,512]{1,0:T(8,128)(2,1)} %bitcast.92, ...), custom_call_target="tpu_custom_call" | custom-call | tf_op jit(solution)/shard_map/ffn/pallas_call | solution.py:510
  153.7 0.9 slice_reduce_fusion
  155.4 35.0 %back.1 = (f32[2048,512]{1,0:T(8,128)}, bf16[16,16,512]{2,1,0:T(8,128)(2,1)}, bf16[512,768]{1,0:T(8,128)(2,1)}, bf16[512,768]{1,0:T(8,128)(2,1)}, f32[8,512]{1,0:T(8,128)}) custom-call(s32[3]{0:T(128)} %copy-done.15, f32[2048,512]{1,0:T(8,128)} %get-tuple-element.29.dr_ref, bf16[2048,512]{1,0:T(8,128)(2,1)} %bitcast.93, bf16[2048,1536]{1,0:T(8,128)(2,1)} %copy-done.4, ...), custom_call_target="tpu_custom_call" | custom-call | tf_op jit(solution)/shard_map/back/pallas_call | solution.py:555
  193.3 1.6 collective-permute-start.41
  194.9 1.5 collective-permute-start.42
  197.4 1.1 collective-permute-done.42
  198.5 2.4 collective-permute-done.43
  200.9 6.9 %collective-permute-start.44 = (f32[1,256]{1,0:T(1,128)S(1)}, f32[1,256]{1,0:T(1,128)S(1)}, u32[]{:S(2)}, u32[]{:S(2)}) collective-permute-start(f32[1,256]{1,0:T(1,128)S(1)} %get-tuple-element.99), channel_id=1, source_target_pairs={{0,2},{1,3},{2,4},{3,5},{4,6},{5,7},{6,0},{7,1},{8,10},{9,11},{10,... | collective-permute-start | bytes 3080 | tf_op jit(solution)/shard_map/ppermute | solution.py:383
  208.4 1.9 collective-permute-start.46
  210.3 0.9 slice_bitcast_fusion
  211.2 1.1 collective-permute-done.45
  213.0 1.3 collective-permute-start.49
  214.3 1.1 collective-permute-done.47
  215.4 3.3 %collective-permute-start.16 = (bf16[2,16,512]{2,1,0:T(8,128)(2,1)S(1)}, bf16[2,16,512]{2,1,0:T(8,128)(2,1)S(1)}, u32[]{:S(2)}, u32[]{:S(2)}) collective-permute-start(bf16[2,16,512]{2,1,0:T(8,128)(2,1)S(1)} %get-tuple-element.85), channel_id=1, source_target_pairs={{0,6},{1,7},{2,0},{3,1},{4,2},{5,3},{6,4},{7,5},{8,14},{9,15},{10,... | collective-permute-start | bytes 98312 | tf_op jit(solution)/shard_map/ppermute | solution.py:383
  218.7 1.2 collective-permute-start.18
  220.5 1.5 add_convert_fusion.1
  223.5 2.1 collective-permute-start.23
  225.7 3.4 %collective-permute-done.21 = bf16[256,384]{1,0:T(8,128)(2,1)S(1)} collective-permute-done((bf16[256,384]{1,0:T(8,128)(2,1)S(1)}, bf16[256,384]{1,0:T(8,128)(2,1)S(1)}, u32[]{:S(2)}, u32[]{:S(2)}) %collective-permute-start.21) | collective-permute-done | bytes 196640 | tf_op jit(solution)/shard_map/ppermute | solution.py:383
  229.1 1.4 collective-permute-done.22
  230.5 2.8 collective-permute-done.23
  233.4 1.6 collective-permute-start.24
  235.0 1.2 collective-permute-start.25
  236.2 1.4 collective-permute-start.26
  238.4 1.0 collective-permute-done.24
  239.4 1.2 collective-permute-done.25
  241.9 1.7 collective-permute-start.31
  244.1 1.3 collective-permute-start.33
  246.0 1.6 collective-permute-start.28
  247.7 4.7 %last.1 = f32[2048,512]{1,0:T(8,128)} custom-call(s32[16]{0:T(128)S(1)} %fusion.11.rel_ref, f32[2048,512]{1,0:T(8,128)S(1)} %copy-done.5, bf16[2048,512]{1,0:T(8,128)(2,1)S(1)} %bitcast.96, f32[16,1,512]{2,1,0:T(1,128)S(1)} %reshape.320.dpool_ref, f32[1,512]{1,0:T(1,128)S(1)} %copy-done.13), custom_call_target="tpu_custom_call" | custom-call | tf_op jit(solution)/shard_map/last/pallas_call | solution.py:657
  252.4 6.1 %collective-permute-done.28 = bf16[64,384]{1,0:T(8,128)(2,1)S(1)} collective-permute-done((bf16[64,384]{1,0:T(8,128)(2,1)S(1)}, bf16[64,384]{1,0:T(8,128)(2,1)S(1)}, u32[]{:S(2)}, u32[]{:S(2)}) %collective-permute-start.28) | collective-permute-done | bytes 49184 | tf_op jit(solution)/shard_map/ppermute | solution.py:383
  258.6 1.1 collective-permute-done.32
  259.7 12.1 %collective-permute-done.33 = bf16[256,1152]{1,0:T(8,128)(2,1)S(1)} collective-permute-done((bf16[256,1152]{1,0:T(8,128)(2,1)S(1)}, bf16[256,1152]{1,0:T(8,128)(2,1)S(1)}, u32[]{:S(2)}, u32[]{:S(2)}) %collective-permute-start.33) | collective-permute-done | bytes 589856 | tf_op jit(solution)/shard_map/ppermute | solution.py:383
  272.3 1.3 collective-permute-start.34
  273.5 2.0 collective-permute-start.35
  275.5 1.0 collective-permute-start.36
  276.5 4.4 %collective-permute-done.34 = bf16[64,1152]{1,0:T(8,128)(2,1)S(1)} collective-permute-done((bf16[64,1152]{1,0:T(8,128)(2,1)S(1)}, bf16[64,1152]{1,0:T(8,128)(2,1)S(1)}, u32[]{:S(2)}, u32[]{:S(2)}) %collective-permute-start.34) | collective-permute-done | bytes 147488 | tf_op jit(solution)/shard_map/ppermute | solution.py:383
  280.9 5.6 %collective-permute-done.35 = bf16[64,1152]{1,0:T(8,128)(2,1)S(1)} collective-permute-done((bf16[64,1152]{1,0:T(8,128)(2,1)S(1)}, bf16[64,1152]{1,0:T(8,128)(2,1)S(1)}, u32[]{:S(2)}, u32[]{:S(2)}) %collective-permute-start.35) | collective-permute-done | bytes 147488 | tf_op jit(solution)/shard_map/ppermute | solution.py:383
  286.6 1.5 collective-permute-start.38
  289.3 3.5 %collective-permute-done.37 = bf16[64,1152]{1,0:T(8,128)(2,1)S(1)} collective-permute-done((bf16[64,1152]{1,0:T(8,128)(2,1)S(1)}, bf16[64,1152]{1,0:T(8,128)(2,1)S(1)}, u32[]{:S(2)}, u32[]{:S(2)}) %collective-permute-start.37) | collective-permute-done | bytes 147488 | tf_op jit(solution)/shard_map/ppermute | solution.py:383
  292.7 3.2 %collective-permute-done.38 = bf16[64,1152]{1,0:T(8,128)(2,1)S(1)} collective-permute-done((bf16[64,1152]{1,0:T(8,128)(2,1)S(1)}, bf16[64,1152]{1,0:T(8,128)(2,1)S(1)}, u32[]{:S(2)}, u32[]{:S(2)}) %collective-permute-start.38) | collective-permute-done | bytes 147488 | tf_op jit(solution)/shard_map/ppermute | solution.py:383
  297.8 0.9 maximum_maximum_fusion
  (184 shorter events, 25.8 us)
Async XLA Ops:
  0.7 30.4 %copy-start.2 = (bf16[16,128,512]{2,1,0:T(8,128)(2,1)S(1)}, bf16[16,128,512]{2,1,0:T(8,128)(2,1)}, u32[]{:S(2)}) copy-start(bf16[16,128,512]{2,1,0:T(8,128)(2,1)} %param.13) | copy-start | bytes 6291460
  3.3 13.2 %collective-permute-start.10 = (bf16[64,2304]{1,0:T(8,128)(2,1)}, bf16[64,2304]{1,0:T(8,128)(2,1)S(1)}, u32[]{:S(2)}, u32[]{:S(2)}) collective-permute-start(bf16[64,2304]{1,0:T(8,128)(2,1)} %pad_maximum_fusion.4), channel_id=1, source_target_pairs={{0,2},{1,3},{2,4},{3,5},{4,6},{5,7},{6,0},{7,1},{8,10},{9,11},{10,... | collective-permute-start | bytes 884744 | tf_op jit(solution)/shard_map/ppermute | solution.py:383
  6.3 22.0 %collective-permute-start.11 = (bf16[64,2304]{1,0:T(8,128)(2,1)}, bf16[64,2304]{1,0:T(8,128)(2,1)S(1)}, u32[]{:S(2)}, u32[]{:S(2)}) collective-permute-start(bf16[64,2304]{1,0:T(8,128)(2,1)} %pad_maximum_fusion.4), channel_id=1, source_target_pairs={{0,4},{1,5},{2,6},{3,7},{4,0},{5,1},{6,2},{7,3},{8,12},{9,13},{10,... | collective-permute-start | bytes 884744 | tf_op jit(solution)/shard_map/ppermute | solution.py:383
  8.9 19.4 %collective-permute-start.12 = (bf16[64,2304]{1,0:T(8,128)(2,1)}, bf16[64,2304]{1,0:T(8,128)(2,1)S(1)}, u32[]{:S(2)}, u32[]{:S(2)}) collective-permute-start(bf16[64,2304]{1,0:T(8,128)(2,1)} %pad_maximum_fusion.4), channel_id=1, source_target_pairs={{0,6},{1,7},{2,0},{3,1},{4,2},{5,3},{6,4},{7,5},{8,14},{9,15},{10,... | collective-permute-start | bytes 884744 | tf_op jit(solution)/shard_map/ppermute | solution.py:383
  11.1 22.2 %copy-start.17 = (bf16[256]{0:T(256)(128)(2,1)S(1)}, bf16[256]{0:T(256)(128)(2,1)}, u32[]{:S(2)}) copy-start(bf16[256]{0:T(256)(128)(2,1)} %param.20) | copy-start | bytes 1540
  11.1 22.2 %copy-start.18 = (bf16[64]{0:T(256)(128)(2,1)S(1)}, bf16[64]{0:T(256)(128)(2,1)}, u32[]{:S(2)}) copy-start(bf16[64]{0:T(256)(128)(2,1)} %param.21) | copy-start | bytes 388
  11.1 22.2 %copy-start.19 = (bf16[64]{0:T(256)(128)(2,1)S(1)}, bf16[64]{0:T(256)(128)(2,1)}, u32[]{:S(2)}) copy-start(bf16[64]{0:T(256)(128)(2,1)} %param.22) | copy-start | bytes 388
  11.1 22.2 %copy-start.20 = (bf16[64]{0:T(256)(128)(2,1)S(1)}, bf16[64]{0:T(256)(128)(2,1)}, u32[]{:S(2)}) copy-start(bf16[64]{0:T(256)(128)(2,1)} %param.23) | copy-start | bytes 388
  11.1 22.2 %copy-start.21 = (bf16[64]{0:T(256)(128)(2,1)S(1)}, bf16[64]{0:T(256)(128)(2,1)}, u32[]{:S(2)}) copy-start(bf16[64]{0:T(256)(128)(2,1)} %param.24) | copy-start | bytes 388
  11.1 22.2 %copy-start.22 = (bf16[64]{0:T(256)(128)(2,1)S(1)}, bf16[64]{0:T(256)(128)(2,1)}, u32[]{:S(2)}) copy-start(bf16[64]{0:T(256)(128)(2,1)} %param.25) | copy-start | bytes 388
  29.4 28.1 %collective-permute-start.13 = (bf16[256,2304]{1,0:T(8,128)(2,1)}, bf16[256,2304]{1,0:T(8,128)(2,1)}, u32[]{:S(2)}, u32[]{:S(2)}) collective-permute-start(bf16[256,2304]{1,0:T(8,128)(2,1)} %pad_maximum_fusion.refs_7_), channel_id=1, source_target_pairs={{0,1},{1,0},{2,3},{3,2},{4,5},{5,4},{6,7},{7,6},{8,9},{9,8},{10,11... | collective-permute-start | bytes 3538952 | tf_op jit(solution)/shard_map/ppermute | solution.py:383
  33.5 11.7 %collective-permute-start = (bf16[18,512]{1,0:T(8,128)(2,1)S(1)}, bf16[18,512]{1,0:T(8,128)(2,1)S(1)}, u32[]{:S(2)}, u32[]{:S(2)}) collective-permute-start(bf16[18,512]{1,0:T(8,128)(2,1)S(1)} %pad_maximum_fusion.6), channel_id=1, source_target_pairs={{0,2},{1,3},{2,4},{3,5},{4,6},{5,7},{6,0},{7,1},{8,10},{9,11},{10,... | collective-permute-start | bytes 55304 | tf_op jit(solution)/shard_map/ppermute | solution.py:383
  40.3 6.2 %collective-permute-start.1 = (bf16[18,512]{1,0:T(8,128)(2,1)S(1)}, bf16[18,512]{1,0:T(8,128)(2,1)S(1)}, u32[]{:S(2)}, u32[]{:S(2)}) collective-permute-start(bf16[18,512]{1,0:T(8,128)(2,1)S(1)} %pad_maximum_fusion.6), channel_id=1, source_target_pairs={{0,4},{1,5},{2,6},{3,7},{4,0},{5,1},{6,2},{7,3},{8,12},{9,13},{10,... | collective-permute-start | bytes 55304 | tf_op jit(solution)/shard_map/ppermute | solution.py:383
  41.9 6.2 %collective-permute-start.2 = (bf16[18,512]{1,0:T(8,128)(2,1)S(1)}, bf16[18,512]{1,0:T(8,128)(2,1)S(1)}, u32[]{:S(2)}, u32[]{:S(2)}) collective-permute-start(bf16[18,512]{1,0:T(8,128)(2,1)S(1)} %pad_maximum_fusion.6), channel_id=1, source_target_pairs={{0,6},{1,7},{2,0},{3,1},{4,2},{5,3},{6,4},{7,5},{8,14},{9,15},{10,... | collective-permute-start | bytes 55304 | tf_op jit(solution)/shard_map/ppermute | solution.py:383
  43.6 14.4 %collective-permute-start.4 = (bf16[64,768]{1,0:T(8,128)(2,1)S(1)}, bf16[64,768]{1,0:T(8,128)(2,1)S(1)}, u32[]{:S(2)}, u32[]{:S(2)}) collective-permute-start(bf16[64,768]{1,0:T(8,128)(2,1)S(1)} %constant_dynamic-slice_fusion.25), channel_id=1, source_target_pairs={{0,2},{1,3},{2,4},{3,5},{4,6},{5,7},{6,0},{7,1},{8,10},{9,11},{10,... | collective-permute-start | bytes 294920 | tf_op jit(solution)/shard_map/ppermute | solution.py:383
  45.1 56.1 %copy-start.10 = (s32[16,128]{1,0:T(8,128)}, s32[16,128]{1,0:T(8,128)S(1)}, u32[]{:S(2)}) copy-start(s32[16,128]{1,0:T(8,128)S(1)} %broadcast_subtract_fusion) | copy-start | bytes 24580
  45.1 14.5 %collective-permute-start.5 = (bf16[64,768]{1,0:T(8,128)(2,1)S(1)}, bf16[64,768]{1,0:T(8,128)(2,1)S(1)}, u32[]{:S(2)}, u32[]{:S(2)}) collective-permute-start(bf16[64,768]{1,0:T(8,128)(2,1)S(1)} %constant_dynamic-slice_fusion.25), channel_id=1, source_target_pairs={{0,4},{1,5},{2,6},{3,7},{4,0},{5,1},{6,2},{7,3},{8,12},{9,13},{10,... | collective-permute-start | bytes 294920 | tf_op jit(solution)/shard_map/ppermute | solution.py:383
  46.5 13.1 %collective-permute-start.6 = (bf16[64,768]{1,0:T(8,128)(2,1)S(1)}, bf16[64,768]{1,0:T(8,128)(2,1)S(1)}, u32[]{:S(2)}, u32[]{:S(2)}) collective-permute-start(bf16[64,768]{1,0:T(8,128)(2,1)S(1)} %constant_dynamic-slice_fusion.25), channel_id=1, source_target_pairs={{0,6},{1,7},{2,0},{3,1},{4,2},{5,3},{6,4},{7,5},{8,14},{9,15},{10,... | collective-permute-start | bytes 294920 | tf_op jit(solution)/shard_map/ppermute | solution.py:383
  48.1 59.0 %collective-permute-start.14 = (bf16[256,2304]{1,0:T(8,128)(2,1)}, bf16[256,2304]{1,0:T(8,128)(2,1)}, u32[]{:S(2)}, u32[]{:S(2)}) collective-permute-start(bf16[256,2304]{1,0:T(8,128)(2,1)} %pad_maximum_fusion.refs_7_), channel_id=1, source_target_pairs={{0,8},{1,9},{2,10},{3,11},{4,12},{5,13},{6,14},{7,15},{8,0},{9,1},... | collective-permute-start | bytes 3538952 | tf_op jit(solution)/shard_map/ppermute | solution.py:383
  57.5 49.6 %collective-permute-start.15 = (bf16[256,2304]{1,0:T(8,128)(2,1)}, bf16[256,2304]{1,0:T(8,128)(2,1)}, u32[]{:S(2)}, u32[]{:S(2)}) collective-permute-start(bf16[256,2304]{1,0:T(8,128)(2,1)} %collective-permute-done.13.refs_8_), channel_id=1, source_target_pairs={{0,8},{1,9},{2,10},{3,11},{4,12},{5,13},{6,14},{7,15},{8,0},{9,1},... | collective-permute-start | bytes 3538952 | tf_op jit(solution)/shard_map/ppermute | solution.py:383
  58.0 5.0 %collective-permute-start.3 = (bf16[72,512]{1,0:T(8,128)(2,1)S(1)}, bf16[72,512]{1,0:T(8,128)(2,1)S(1)}, u32[]{:S(2)}, u32[]{:S(2)}) collective-permute-start(bf16[72,512]{1,0:T(8,128)(2,1)S(1)} %concatenate.60), channel_id=1, source_target_pairs={{0,1},{1,0},{2,3},{3,2},{4,5},{5,4},{6,7},{7,6},{8,9},{9,8},{10,11... | collective-permute-start | bytes 221192 | tf_op jit(solution)/shard_map/ppermute | solution.py:383
  59.6 11.6 %collective-permute-start.7 = (bf16[256,768]{1,0:T(8,128)(2,1)S(1)}, bf16[256,768]{1,0:T(8,128)(2,1)S(1)}, u32[]{:S(2)}, u32[]{:S(2)}) collective-permute-start(bf16[256,768]{1,0:T(8,128)(2,1)S(1)} %pad_maximum_fusion.2.refs_6_), channel_id=1, source_target_pairs={{0,1},{1,0},{2,3},{3,2},{4,5},{5,4},{6,7},{7,6},{8,9},{9,8},{10,11... | collective-permute-start | bytes 1179656 | tf_op jit(solution)/shard_map/ppermute | solution.py:383
  60.3 40.9 %copy-start.15 = (s32[3]{0:T(128)}, s32[3]{0:T(128)S(1)}, u32[]{:S(2)}) copy-start(s32[3]{0:T(128)S(1)} %pad_add_fusion.meta) | copy-start | bytes 40
  60.3 40.9 %copy-start.9 = (f32[16,16,128]{2,1,0:T(8,128)}, f32[16,16,128]{2,1,0:T(8,128)S(1)}, u32[]{:S(2)}) copy-start(f32[16,16,128]{2,1,0:T(8,128)S(1)} %pad.18.refs_5_.pbias_ref) | copy-start | bytes 393220
  63.7 89.9 %copy-start.6 = (bf16[16,16,512]{2,1,0:T(8,128)(2,1)}, bf16[16,16,512]{2,1,0:T(8,128)(2,1)S(1)}, u32[]{:S(2)}) copy-start(bf16[16,16,512]{2,1,0:T(8,128)(2,1)S(1)} %pad.17.refs_3_.pool_ref) | copy-start | bytes 786436
  63.9 10.1 %collective-permute-start.8 = (bf16[256,768]{1,0:T(8,128)(2,1)S(1)}, bf16[256,768]{1,0:T(8,128)(2,1)}, u32[]{:S(2)}, u32[]{:S(2)}) collective-permute-start(bf16[256,768]{1,0:T(8,128)(2,1)S(1)} %pad_maximum_fusion.2.refs_6_), channel_id=1, source_target_pairs={{0,8},{1,9},{2,10},{3,11},{4,12},{5,13},{6,14},{7,15},{8,0},{9,1},... | collective-permute-start | bytes 1179656 | tf_op jit(solution)/shard_map/ppermute | solution.py:383
  71.2 2.9 collective-permute-start.9
  71.4 82.3 %copy-start.12 = (f32[1,512]{1,0:T(1,128)}, f32[1,512]{1,0:T(1,128)S(1)}, u32[]{:S(2)}) copy-start(f32[1,512]{1,0:T(1,128)S(1)} %reshape.311.refs_1_.gain_ref) | copy-start | bytes 6148
  71.4 82.2 %copy-start.14 = (f32[1,512]{1,0:T(1,128)}, f32[1,512]{1,0:T(1,128)S(1)}, u32[]{:S(2)}) copy-start(f32[1,512]{1,0:T(1,128)S(1)} %reshape.312.refs_2_.shift_ref) | copy-start | bytes 6148
  155.4 41.5 %copy-start.23 = (bf16[512,2304]{1,0:T(8,128)(2,1)S(1)}, bf16[512,2304]{1,0:T(8,128)(2,1)}, u32[]{:S(2)}) copy-start(bf16[512,2304]{1,0:T(8,128)(2,1)} %get-tuple-element.39) | copy-start | bytes 7077892
  191.7 1.4 collective-permute-start.40
  193.3 4.1 %collective-permute-start.41 = (f32[4,256]{1,0:T(4,128)S(1)}, f32[4,256]{1,0:T(4,128)S(1)}, u32[]{:S(2)}, u32[]{:S(2)}) collective-permute-start(f32[4,256]{1,0:T(4,128)S(1)} %bitcast.117), channel_id=1, source_target_pairs={{0,16},{1,17},{2,18},{3,19},{4,20},{5,21},{6,22},{7,23},{8,24},{9,... | collective-permute-start | bytes 12296 | tf_op jit(solution)/shard_map/ppermute | solution.py:383
  194.9 3.6 %collective-permute-start.42 = (f32[4,256]{1,0:T(4,128)S(1)}, f32[4,256]{1,0:T(4,128)S(1)}, u32[]{:S(2)}, u32[]{:S(2)}) collective-permute-start(f32[4,256]{1,0:T(4,128)S(1)} %bitcast.118), channel_id=1, source_target_pairs={{0,1},{1,0},{2,3},{3,2},{4,5},{5,4},{6,7},{7,6},{8,9},{9,8},{10,11... | collective-permute-start | bytes 12296 | tf_op jit(solution)/shard_map/ppermute | solution.py:383
  196.4 4.5 %collective-permute-start.43 = (f32[4,256]{1,0:T(4,128)S(1)}, f32[4,256]{1,0:T(4,128)S(1)}, u32[]{:S(2)}, u32[]{:S(2)}) collective-permute-start(f32[4,256]{1,0:T(4,128)S(1)} %bitcast.119), channel_id=1, source_target_pairs={{0,17},{1,16},{2,19},{3,18},{4,21},{5,20},{6,23},{7,22},{8,25},{9,... | collective-permute-start | bytes 12296 | tf_op jit(solution)/shard_map/ppermute | solution.py:383
  196.9 44.0 %collective-permute-start.30 = (bf16[512,2304]{1,0:T(8,128)(2,1)S(1)}, bf16[512,2304]{1,0:T(8,128)(2,1)S(1)}, u32[]{:S(2)}, u32[]{:S(2)}) collective-permute-start(bf16[512,2304]{1,0:T(8,128)(2,1)S(1)} %copy-done.23), channel_id=1, source_target_pairs={{0,8},{1,9},{2,10},{3,11},{4,12},{5,13},{6,14},{7,15},{8,0},{9,1},... | collective-permute-start | bytes 7077896 | tf_op jit(solution)/shard_map/ppermute | solution.py:383
  196.9 23.6 %collective-permute-start.20 = (bf16[512,768]{1,0:T(8,128)(2,1)}, bf16[512,768]{1,0:T(8,128)(2,1)S(1)}, u32[]{:S(2)}, u32[]{:S(2)}) collective-permute-start(bf16[512,768]{1,0:T(8,128)(2,1)} %get-tuple-element.37), channel_id=1, source_target_pairs={{0,8},{1,9},{2,10},{3,11},{4,12},{5,13},{6,14},{7,15},{8,0},{9,1},... | collective-permute-start | bytes 2359304 | tf_op jit(solution)/shard_map/ppermute | solution.py:383
  200.9 10.3 %collective-permute-start.44 = (f32[1,256]{1,0:T(1,128)S(1)}, f32[1,256]{1,0:T(1,128)S(1)}, u32[]{:S(2)}, u32[]{:S(2)}) collective-permute-start(f32[1,256]{1,0:T(1,128)S(1)} %get-tuple-element.99), channel_id=1, source_target_pairs={{0,2},{1,3},{2,4},{3,5},{4,6},{5,7},{6,0},{7,1},{8,10},{9,11},{10,... | collective-permute-start | bytes 3080 | tf_op jit(solution)/shard_map/ppermute | solution.py:383
  207.8 4.5 %collective-permute-start.45 = (f32[1,256]{1,0:T(1,128)S(1)}, f32[1,256]{1,0:T(1,128)S(1)}, u32[]{:S(2)}, u32[]{:S(2)}) collective-permute-start(f32[1,256]{1,0:T(1,128)S(1)} %get-tuple-element.101), channel_id=1, source_target_pairs={{0,4},{1,5},{2,6},{3,7},{4,0},{5,1},{6,2},{7,3},{8,12},{9,13},{10,... | collective-permute-start | bytes 3080 | tf_op jit(solution)/shard_map/ppermute | solution.py:383
  208.4 3.9 %collective-permute-start.46 = (f32[1,256]{1,0:T(1,128)S(1)}, f32[1,256]{1,0:T(1,128)S(1)}, u32[]{:S(2)}, u32[]{:S(2)}) collective-permute-start(f32[1,256]{1,0:T(1,128)S(1)} %get-tuple-element.100), channel_id=1, source_target_pairs={{0,6},{1,7},{2,0},{3,1},{4,2},{5,3},{6,4},{7,5},{8,14},{9,15},{10,... | collective-permute-start | bytes 3080 | tf_op jit(solution)/shard_map/ppermute | solution.py:383
  212.3 3.1 %collective-permute-start.47 = (f32[1,256]{1,0:T(1,128)S(1)}, f32[1,256]{1,0:T(1,128)S(1)}, u32[]{:S(2)}, u32[]{:S(2)}) collective-permute-start(f32[1,256]{1,0:T(1,128)S(1)} %fusion.17), channel_id=1, source_target_pairs={{0,24},{1,25},{2,26},{3,27},{4,28},{5,29},{6,30},{7,31},{8,16},{9,... | collective-permute-start | bytes 3080 | tf_op jit(solution)/shard_map/ppermute | solution.py:383
  212.4 6.3 %collective-permute-start.48 = (f32[1,256]{1,0:T(1,128)S(1)}, f32[1,256]{1,0:T(1,128)S(1)}, u32[]{:S(2)}, u32[]{:S(2)}) collective-permute-start(f32[1,256]{1,0:T(1,128)S(1)} %fusion.17), channel_id=1, source_target_pairs={{0,16},{1,17},{2,18},{3,19},{4,20},{5,21},{6,22},{7,23},{8,24},{9,... | collective-permute-start | bytes 3080 | tf_op jit(solution)/shard_map/ppermute | solution.py:383
  213.0 5.8 %collective-permute-start.49 = (f32[1,256]{1,0:T(1,128)S(1)}, f32[1,256]{1,0:T(1,128)S(1)}, u32[]{:S(2)}, u32[]{:S(2)}) collective-permute-start(f32[1,256]{1,0:T(1,128)S(1)} %fusion.17), channel_id=1, source_target_pairs={{0,8},{1,9},{2,10},{3,11},{4,12},{5,13},{6,14},{7,15},{8,0},{9,1},... | collective-permute-start | bytes 3080 | tf_op jit(solution)/shard_map/ppermute | solution.py:383
  215.4 7.3 %collective-permute-start.16 = (bf16[2,16,512]{2,1,0:T(8,128)(2,1)S(1)}, bf16[2,16,512]{2,1,0:T(8,128)(2,1)S(1)}, u32[]{:S(2)}, u32[]{:S(2)}) collective-permute-start(bf16[2,16,512]{2,1,0:T(8,128)(2,1)S(1)} %get-tuple-element.85), channel_id=1, source_target_pairs={{0,6},{1,7},{2,0},{3,1},{4,2},{5,3},{6,4},{7,5},{8,14},{9,15},{10,... | collective-permute-start | bytes 98312 | tf_op jit(solution)/shard_map/ppermute | solution.py:383
  218.7 4.8 %collective-permute-start.17 = (bf16[2,16,512]{2,1,0:T(8,128)(2,1)S(1)}, bf16[2,16,512]{2,1,0:T(8,128)(2,1)S(1)}, u32[]{:S(2)}, u32[]{:S(2)}) collective-permute-start(bf16[2,16,512]{2,1,0:T(8,128)(2,1)S(1)} %get-tuple-element.86), channel_id=1, source_target_pairs={{0,4},{1,5},{2,6},{3,7},{4,0},{5,1},{6,2},{7,3},{8,12},{9,13},{10,... | collective-permute-start | bytes 98312 | tf_op jit(solution)/shard_map/ppermute | solution.py:383
  218.7 6.9 %collective-permute-start.18 = (bf16[2,16,512]{2,1,0:T(8,128)(2,1)S(1)}, bf16[2,16,512]{2,1,0:T(8,128)(2,1)S(1)}, u32[]{:S(2)}, u32[]{:S(2)}) collective-permute-start(bf16[2,16,512]{2,1,0:T(8,128)(2,1)S(1)} %get-tuple-element.87), channel_id=1, source_target_pairs={{0,2},{1,3},{2,4},{3,5},{4,6},{5,7},{6,0},{7,1},{8,10},{9,11},{10,... | collective-permute-start | bytes 98312 | tf_op jit(solution)/shard_map/ppermute | solution.py:383
  222.1 7.0 %collective-permute-start.21 = (bf16[256,384]{1,0:T(8,128)(2,1)S(1)}, bf16[256,384]{1,0:T(8,128)(2,1)S(1)}, u32[]{:S(2)}, u32[]{:S(2)}) collective-permute-start(bf16[256,384]{1,0:T(8,128)(2,1)S(1)} %bitcast.114), channel_id=1, source_target_pairs={{0,16},{1,17},{2,18},{3,19},{4,20},{5,21},{6,22},{7,23},{8,24},{9,... | collective-permute-start | bytes 589832 | tf_op jit(solution)/shard_map/ppermute | solution.py:383
  222.7 7.8 %collective-permute-start.22 = (bf16[256,384]{1,0:T(8,128)(2,1)S(1)}, bf16[256,384]{1,0:T(8,128)(2,1)S(1)}, u32[]{:S(2)}, u32[]{:S(2)}) collective-permute-start(bf16[256,384]{1,0:T(8,128)(2,1)S(1)} %bitcast.113), channel_id=1, source_target_pairs={{0,1},{1,0},{2,3},{3,2},{4,5},{5,4},{6,7},{7,6},{8,9},{9,8},{10,11... | collective-permute-start | bytes 589832 | tf_op jit(solution)/shard_map/ppermute | solution.py:383
  223.5 9.7 %collective-permute-start.23 = (bf16[256,384]{1,0:T(8,128)(2,1)S(1)}, bf16[256,384]{1,0:T(8,128)(2,1)S(1)}, u32[]{:S(2)}, u32[]{:S(2)}) collective-permute-start(bf16[256,384]{1,0:T(8,128)(2,1)S(1)} %bitcast.112), channel_id=1, source_target_pairs={{0,17},{1,16},{2,19},{3,18},{4,21},{5,20},{6,23},{7,22},{8,25},{9,... | collective-permute-start | bytes 589832 | tf_op jit(solution)/shard_map/ppermute | solution.py:383
  233.4 5.9 %collective-permute-start.24 = (bf16[64,384]{1,0:T(8,128)(2,1)S(1)}, bf16[64,384]{1,0:T(8,128)(2,1)S(1)}, u32[]{:S(2)}, u32[]{:S(2)}) collective-permute-start(bf16[64,384]{1,0:T(8,128)(2,1)S(1)} %get-tuple-element.82), channel_id=1, source_target_pairs={{0,2},{1,3},{2,4},{3,5},{4,6},{5,7},{6,0},{7,1},{8,10},{9,11},{10,... | collective-permute-start | bytes 147464 | tf_op jit(solution)/shard_map/ppermute | solution.py:383
  235.0 5.5 %collective-permute-start.25 = (bf16[64,384]{1,0:T(8,128)(2,1)S(1)}, bf16[64,384]{1,0:T(8,128)(2,1)S(1)}, u32[]{:S(2)}, u32[]{:S(2)}) collective-permute-start(bf16[64,384]{1,0:T(8,128)(2,1)S(1)} %get-tuple-element.84), channel_id=1, source_target_pairs={{0,4},{1,5},{2,6},{3,7},{4,0},{5,1},{6,2},{7,3},{8,12},{9,13},{10,... | collective-permute-start | bytes 147464 | tf_op jit(solution)/shard_map/ppermute | solution.py:383
  236.2 4.6 %collective-permute-start.26 = (bf16[64,384]{1,0:T(8,128)(2,1)S(1)}, bf16[64,384]{1,0:T(8,128)(2,1)S(1)}, u32[]{:S(2)}, u32[]{:S(2)}) collective-permute-start(bf16[64,384]{1,0:T(8,128)(2,1)S(1)} %get-tuple-element.83), channel_id=1, source_target_pairs={{0,6},{1,7},{2,0},{3,1},{4,2},{5,3},{6,4},{7,5},{8,14},{9,15},{10,... | collective-permute-start | bytes 147464 | tf_op jit(solution)/shard_map/ppermute | solution.py:383
  237.6 8.4 %collective-permute-start.19 = (bf16[16,512]{1,0:T(8,128)(2,1)S(1)}, bf16[16,512]{1,0:T(8,128)(2,1)S(1)}, u32[]{:S(2)}, u32[]{:S(2)}) collective-permute-start(bf16[16,512]{1,0:T(8,128)(2,1)S(1)} %slice_bitcast_fusion.5), channel_id=1, source_target_pairs={{0,1},{1,0},{2,3},{3,2},{4,5},{5,4},{6,7},{7,6},{8,9},{9,8},{10,11... | collective-permute-start | bytes 49160 | tf_op jit(solution)/shard_map/ppermute | solution.py:383
  240.8 6.8 %collective-permute-start.27 = (bf16[64,384]{1,0:T(8,128)(2,1)S(1)}, bf16[64,384]{1,0:T(8,128)(2,1)S(1)}, u32[]{:S(2)}, u32[]{:S(2)}) collective-permute-start(bf16[64,384]{1,0:T(8,128)(2,1)S(1)} %add_convert_fusion.3), channel_id=1, source_target_pairs={{0,24},{1,25},{2,26},{3,27},{4,28},{5,29},{6,30},{7,31},{8,16},{9,... | collective-permute-start | bytes 147464 | tf_op jit(solution)/shard_map/ppermute | solution.py:383
  241.9 16.7 %collective-permute-start.31 = (bf16[256,1152]{1,0:T(8,128)(2,1)S(1)}, bf16[256,1152]{1,0:T(8,128)(2,1)S(1)}, u32[]{:S(2)}, u32[]{:S(2)}) collective-permute-start(bf16[256,1152]{1,0:T(8,128)(2,1)S(1)} %bitcast.105), channel_id=1, source_target_pairs={{0,16},{1,17},{2,18},{3,19},{4,20},{5,21},{6,22},{7,23},{8,24},{9,... | collective-permute-start | bytes 1769480 | tf_op jit(solution)/shard_map/ppermute | solution.py:383
  243.5 16.2 %collective-permute-start.32 = (bf16[256,1152]{1,0:T(8,128)(2,1)S(1)}, bf16[256,1152]{1,0:T(8,128)(2,1)S(1)}, u32[]{:S(2)}, u32[]{:S(2)}) collective-permute-start(bf16[256,1152]{1,0:T(8,128)(2,1)S(1)} %bitcast.104), channel_id=1, source_target_pairs={{0,1},{1,0},{2,3},{3,2},{4,5},{5,4},{6,7},{7,6},{8,9},{9,8},{10,11... | collective-permute-start | bytes 1769480 | tf_op jit(solution)/shard_map/ppermute | solution.py:383
  244.1 27.8 %collective-permute-start.33 = (bf16[256,1152]{1,0:T(8,128)(2,1)S(1)}, bf16[256,1152]{1,0:T(8,128)(2,1)S(1)}, u32[]{:S(2)}, u32[]{:S(2)}) collective-permute-start(bf16[256,1152]{1,0:T(8,128)(2,1)S(1)} %bitcast.103), channel_id=1, source_target_pairs={{0,17},{1,16},{2,19},{3,18},{4,21},{5,20},{6,23},{7,22},{8,25},{9,... | collective-permute-start | bytes 1769480 | tf_op jit(solution)/shard_map/ppermute | solution.py:383
  246.0 12.5 %collective-permute-start.28 = (bf16[64,384]{1,0:T(8,128)(2,1)S(1)}, bf16[64,384]{1,0:T(8,128)(2,1)S(1)}, u32[]{:S(2)}, u32[]{:S(2)}) collective-permute-start(bf16[64,384]{1,0:T(8,128)(2,1)S(1)} %add_convert_fusion.3), channel_id=1, source_target_pairs={{0,16},{1,17},{2,18},{3,19},{4,20},{5,21},{6,22},{7,23},{8,24},{9,... | collective-permute-start | bytes 147464 | tf_op jit(solution)/shard_map/ppermute | solution.py:383
  247.6 10.9 %collective-permute-start.29 = (bf16[64,384]{1,0:T(8,128)(2,1)S(1)}, bf16[64,384]{1,0:T(8,128)(2,1)S(1)}, u32[]{:S(2)}, u32[]{:S(2)}) collective-permute-start(bf16[64,384]{1,0:T(8,128)(2,1)S(1)} %add_convert_fusion.3), channel_id=1, source_target_pairs={{0,8},{1,9},{2,10},{3,11},{4,12},{5,13},{6,14},{7,15},{8,0},{9,1},... | collective-permute-start | bytes 147464 | tf_op jit(solution)/shard_map/ppermute | solution.py:383
  272.3 8.7 %collective-permute-start.34 = (bf16[64,1152]{1,0:T(8,128)(2,1)S(1)}, bf16[64,1152]{1,0:T(8,128)(2,1)S(1)}, u32[]{:S(2)}, u32[]{:S(2)}) collective-permute-start(bf16[64,1152]{1,0:T(8,128)(2,1)S(1)} %get-tuple-element.66), channel_id=1, source_target_pairs={{0,2},{1,3},{2,4},{3,5},{4,6},{5,7},{6,0},{7,1},{8,10},{9,11},{10,... | collective-permute-start | bytes 442376 | tf_op jit(solution)/shard_map/ppermute | solution.py:383
  273.5 12.9 %collective-permute-start.35 = (bf16[64,1152]{1,0:T(8,128)(2,1)S(1)}, bf16[64,1152]{1,0:T(8,128)(2,1)S(1)}, u32[]{:S(2)}, u32[]{:S(2)}) collective-permute-start(bf16[64,1152]{1,0:T(8,128)(2,1)S(1)} %get-tuple-element.68), channel_id=1, source_target_pairs={{0,4},{1,5},{2,6},{3,7},{4,0},{5,1},{6,2},{7,3},{8,12},{9,13},{10,... | collective-permute-start | bytes 442376 | tf_op jit(solution)/shard_map/ppermute | solution.py:383
  275.5 11.0 %collective-permute-start.36 = (bf16[64,1152]{1,0:T(8,128)(2,1)S(1)}, bf16[64,1152]{1,0:T(8,128)(2,1)S(1)}, u32[]{:S(2)}, u32[]{:S(2)}) collective-permute-start(bf16[64,1152]{1,0:T(8,128)(2,1)S(1)} %get-tuple-element.67), channel_id=1, source_target_pairs={{0,6},{1,7},{2,0},{3,1},{4,2},{5,3},{6,4},{7,5},{8,14},{9,15},{10,... | collective-permute-start | bytes 442376 | tf_op jit(solution)/shard_map/ppermute | solution.py:383
  286.6 6.2 %collective-permute-start.37 = (bf16[64,1152]{1,0:T(8,128)(2,1)S(1)}, bf16[64,1152]{1,0:T(8,128)(2,1)S(1)}, u32[]{:S(2)}, u32[]{:S(2)}) collective-permute-start(bf16[64,1152]{1,0:T(8,128)(2,1)S(1)} %add_convert_fusion.2), channel_id=1, source_target_pairs={{0,24},{1,25},{2,26},{3,27},{4,28},{5,29},{6,30},{7,31},{8,16},{9,... | collective-permute-start | bytes 442376 | tf_op jit(solution)/shard_map/ppermute | solution.py:383
  286.6 9.3 %collective-permute-start.38 = (bf16[64,1152]{1,0:T(8,128)(2,1)S(1)}, bf16[64,1152]{1,0:T(8,128)(2,1)S(1)}, u32[]{:S(2)}, u32[]{:S(2)}) collective-permute-start(bf16[64,1152]{1,0:T(8,128)(2,1)S(1)} %add_convert_fusion.2), channel_id=1, source_target_pairs={{0,16},{1,17},{2,18},{3,19},{4,20},{5,21},{6,22},{7,23},{8,24},{9,... | collective-permute-start | bytes 442376 | tf_op jit(solution)/shard_map/ppermute | solution.py:383
  288.1 7.8 %collective-permute-start.39 = (bf16[64,1152]{1,0:T(8,128)(2,1)S(1)}, bf16[64,1152]{1,0:T(8,128)(2,1)S(1)}, u32[]{:S(2)}, u32[]{:S(2)}) collective-permute-start(bf16[64,1152]{1,0:T(8,128)(2,1)S(1)} %add_convert_fusion.2), channel_id=1, source_target_pairs={{0,8},{1,9},{2,10},{3,11},{4,12},{5,13},{6,14},{7,15},{8,0},{9,1},... | collective-permute-start | bytes 442376 | tf_op jit(solution)/shard_map/ppermute | solution.py:383
  (10 other events, 49.0 us)

commit v2 on v1

v2 whole, which is shorter than its diff:
```python
import functools

import jax
import jax.numpy as jnp
from jax import lax
from jax.experimental import pallas as pl
from jax.experimental.pallas import tpu as pltpu
from jax.sharding import PartitionSpec as P

HEADS = 8
epsilon = 1e-05
masked = -1e30
F32 = jnp.float32
BF = jnp.bfloat16
MIB = 1 << 20


def dot(a, b):
    return jnp.dot(a, b, preferred_element_type=F32)


def dot_nt(a, b):
    return lax.dot_general(a, b, (((1,), (1,)), ((), ())), preferred_element_type=F32)


def dot_tn(a, b):
    return lax.dot_general(a, b, (((0,), (0,)), ((), ())), preferred_element_type=F32)


def normed(v):
    center = v - jnp.mean(v, axis=-1, keepdims=True)
    rstd = lax.rsqrt(jnp.mean(center * center, axis=-1, keepdims=True) + epsilon)
    return center * rstd, rstd


def norm_back(e, n, rstd):
    return rstd * (
        e - jnp.mean(e, axis=-1, keepdims=True) - n * jnp.mean(e * n, axis=-1, keepdims=True)
    )


def two_heads_lanes(t):
    half = t.shape[0] // 2
    zero = jnp.zeros((half, t.shape[1]), t.dtype)
    left = jnp.concatenate([t[:half], zero], axis=0)
    right = jnp.concatenate([zero, t[half:]], axis=0)
    return jnp.concatenate([left, right], axis=1)


def two_heads_rows(a):
    first = lax.broadcasted_iota(jnp.int32, a.shape, 1) < a.shape[1] // 2
    zero = jnp.zeros_like(a)
    return jnp.concatenate([jnp.where(first, a, zero), jnp.where(first, zero, a)], axis=0)


def diagonal(t):
    rows, cols = t.shape[0] // 2, t.shape[1] // 2
    return jnp.concatenate([t[:rows, :cols], t[rows:, cols:]], axis=0)


def span_bias(doc_from, pooled):
    span = doc_from.shape[1]
    key = lax.broadcasted_iota(jnp.int32, (span, span), 0)
    query = lax.broadcasted_iota(jnp.int32, (span, span), 1)
    direct = jnp.where((key >= doc_from) & (key <= query), 0.0, masked).astype(F32)
    both = jnp.concatenate([direct, pooled], axis=0)
    return jnp.concatenate([both, both], axis=1)


def arriving(meta, sizes, pieces, places, sems, act, kind):
    zs, xs = sizes
    z, x, core = meta[0], meta[1], meta[2]
    at = 0
    for which in range(2):
        half = core if which == 0 else 1 - core
        for kx in range(xs):
            for kz in range(zs):
                shard = lax.rem(z - kz + zs, zs) * xs + lax.rem(x - kx + xs, xs)
                for src, dst in places[kind](pieces, which, kx, kz, shard, half):
                    copy = pltpu.make_async_copy(src, dst, sems.at[kind, at])
                    copy.start() if act == "start" else copy.wait()
                    at += 1


def pool_kernel(rel_ref, x_ref, out_ref, *, seqs, span):
    n, _ = normed(x_ref[...].astype(F32))
    for i in range(seqs):
        first = rel_ref[pl.program_id(0) * seqs + i]
        row = lax.broadcasted_iota(jnp.int32, (span, n.shape[1]), 0)
        part = jnp.where(row >= first, n[i * span : (i + 1) * span], 0.0)
        count = jnp.full((1, 1), span - first, jnp.int32).astype(F32)
        out_ref[i] = jnp.sum(part, axis=0, keepdims=True) / count


def padded(a, rows, value):
    shape = a.shape[:-2] + (rows - a.shape[-2], a.shape[-1])
    return jnp.concatenate([a, jnp.full(shape, value, a.dtype)], axis=-2) if shape[-2] else a


def vector(vecs_ref, i):
    return vecs_ref[i : i + 1, :]


def attend_kernel(meta, *refs, sizes, seqs, span, rps, whole):
    x_ref, vecs_ref, pool_ref, from_ref, pbias_ref = refs[:5]
    width = x_ref.shape[1]
    first = pl.program_id(0) == 0
    if whole:
        w_ref, _, _, _, qkv_ref, o_ref, lse_ref = refs[5:]
    else:
        xs = sizes[1]
        pieces = refs[5 : 5 + 2 * xs]
        w_ref, qkv_ref, o_ref, lse_ref, sems = refs[5 + 2 * xs :]
        nh = w_ref.shape[1] // 2

        def place(pieces, which, kx, kz, shard, half):
            yield (
                pieces[which * xs + kx].at[pl.ds(kz * rps, rps), :],
                w_ref.at[
                    pl.ds(pl.multiple_of(shard * rps, rps), rps),
                    pl.ds(pl.multiple_of(half * nh, 128), nh),
                ],
            )

        @pl.when(first)
        def _():
            arriving(meta, sizes, pieces, [place], sems, "start", 0)

    gain, shift = vector(vecs_ref, 1), vector(vecs_ref, 2)
    n, _ = normed(x_ref[...].astype(F32))
    h = (n * gain + shift).astype(BF)
    cp = -(-pool_ref.shape[1] // 16) * 16
    pooled_h = padded(pool_ref[...], cp, 0.0).reshape(seqs * cp, width) * gain + shift
    if not whole:

        @pl.when(first)
        def _():
            arriving(meta, sizes, pieces, [place], sems, "wait", 0)

    qkv = dot(h, w_ref[...]).astype(BF)
    q = qkv[:, :width] * jnp.asarray((width // HEADS) ** -0.5, BF)
    qkv_ref[:, :width] = q
    qkv_ref[:, width:] = qkv[:, width:]
    kvb = dot(pooled_h.astype(BF), w_ref[:, width:]).astype(BF)
    pairs = range(HEADS // 2)
    col = lambda part, p: slice(part * width + p * 128, part * width + (p + 1) * 128)
    for s in range(seqs):
        rows = slice(s * span, (s + 1) * span)
        prow = slice(s * cp, (s + 1) * cp)
        bias = span_bias(from_ref[s], padded(pbias_ref[s], cp, masked))
        both = lambda part, p: jnp.concatenate(
            [qkv[rows, col(part, p)], kvb[prow, col(part - 1, p)]], axis=0
        )
        query = [two_heads_lanes(q[rows, col(0, p)].T) for p in pairs]
        scores = [dot(both(1, p), query[p]) + bias for p in pairs]
        top = [jnp.max(scores[p], axis=0, keepdims=True) for p in pairs]
        e = [jnp.exp(scores[p] - top[p]) for p in pairs]
        total = [jnp.sum(e[p], axis=0, keepdims=True) for p in pairs]
        prob = [(e[p] * (1.0 / total[p])).astype(BF) for p in pairs]
        out = [diagonal(dot_tn(both(2, p), prob[p])).astype(BF) for p in pairs]
        for p in pairs:
            lse_ref[s, p : p + 1, :] = top[p] + jnp.log(total[p])
            o_ref[rows, col(0, p)] = out[p].T


def ffn_kernel(meta, *refs, sizes, rps):
    o_ref, x_ref, y_ref, vecs_ref = refs[:4]
    pieces = refs[4:8]
    (
        dr_ref,
        a_ref,
        keep_ref,
        send_ref,
        wp_ref,
        w2_ref,
        vec_ref,
        w1_ref,
        acc1_ref,
        acc2_ref,
        accp_ref,
        sems,
    ) = refs[8:]
    width, hidden = w1_ref.shape
    zs = sizes[0]
    per = hidden // width
    ph, wh = width // 2, hidden // 2
    step = pl.program_id(0)

    def source(ref, kx, kz):
        return ref, pl.ds((kx * zs + kz) * rps, rps)

    def place_p(pieces, which, kx, kz, shard, half):
        ref, src = source(pieces[which], kx, kz)
        yield (
            ref.at[src, pl.ds(0, ph)],
            wp_ref.at[
                pl.ds(pl.multiple_of(shard * rps, rps), rps),
                pl.ds(pl.multiple_of(half * ph, 128), ph),
            ],
        )

    def place_1(pieces, which, kx, kz, shard, half):
        ref, src = source(pieces[which], kx, kz)
        yield (
            ref.at[src, pl.ds(ph, wh)],
            w1_ref.at[
                pl.ds(pl.multiple_of(shard * rps, rps), rps),
                pl.ds(pl.multiple_of(half * wh, 128), wh),
            ],
        )

    def place_2(pieces, which, kx, kz, shard, half):
        ref, src = source(pieces[2 + which], kx, kz)
        for j in range(per // 2):
            at = (shard * per + half * (per // 2) + j) * rps
            yield (
                ref.at[src, pl.ds(j * width, width)],
                w2_ref.at[pl.ds(pl.multiple_of(at, rps), rps), :],
            )

    def weights(act, kind):
        @pl.when(step == 0)
        def _():
            arriving(meta, sizes, pieces, [place_p, place_1, place_2], sems, act, kind)

    for kind in range(3):
        weights("start", kind)

    @pl.when(step == 0)
    def _():
        acc1_ref[...] = jnp.zeros_like(acc1_ref)
        acc2_ref[...] = jnp.zeros_like(acc2_ref)
        accp_ref[...] = jnp.zeros_like(accp_ref)
        vec_ref[...] = jnp.zeros_like(vec_ref)

    weights("wait", 0)
    o, y = o_ref[...], y_ref[...]
    r1 = x_ref[...].astype(F32) + dot(o, wp_ref[...])
    n, rstd = normed(r1)
    gain = vector(vecs_ref, 3)
    h = (n * gain + vector(vecs_ref, 4)).astype(BF)
    ht = h.T
    dh = jnp.zeros_like(r1)
    weights("wait", 1)
    weights("wait", 2)
    for j in range(per):
        at = slice(j * width, (j + 1) * width)
        u = dot(h, w1_ref[:, at]) + vecs_ref[5 + j : 6 + j, :]
        da = dot_nt(y, w2_ref[at, :])
        cdf = 0.5 + 0.5 * lax.erf(u * 0.7071067811865476)
        pdf = jnp.exp(u * u * -0.5) * 0.3989422804014327
        a = (u * cdf).astype(BF)
        du = (da * (cdf + u * pdf)).astype(BF)
        a_ref[:, at] = a
        dh += dot_nt(du, w1_ref[:, at])
        acc1_ref[:, at] += dot(ht, du)
        acc2_ref[at, :] += dot_tn(a, y)
        vec_ref[0:1, at] += jnp.sum(du.astype(F32), axis=0, keepdims=True)
    yf = y.astype(F32)
    dr = yf + norm_back(dh * gain, n, rstd)
    dr_ref[...] = dr
    accp_ref[...] += dot_tn(o, dr.astype(BF))
    vec_ref[1:2, :width] += jnp.sum(yf, axis=0, keepdims=True)
    vec_ref[2:3, :width] += jnp.sum(dh * n, axis=0, keepdims=True)
    vec_ref[3:4, :width] += jnp.sum(dh, axis=0, keepdims=True)

    @pl.when(step == pl.num_programs(0) - 1)
    def _():
        for which, ref in ((0, keep_ref), (1, send_ref)):
            half = meta[2] if which == 0 else 1 - meta[2]
            pcol = pl.ds(pl.multiple_of(half * ph, 128), ph)
            ref[:, :ph] = accp_ref[:, pcol].astype(BF)
            ref[:, ph : ph + wh] = acc1_ref[:, pl.ds(pl.multiple_of(half * wh, 128), wh)].astype(BF)
            for shard in range(width // rps):
                for j in range(per):
                    at = (shard * per + j) * rps
                    ref[shard * rps : (shard + 1) * rps, ph + wh + j * ph : ph + wh + (j + 1) * ph] = (
                        acc2_ref[at : at + rps, pcol].astype(BF)
                    )


def out_kernel(o_ref, x_ref, a_ref, vecs_ref, wp_ref, w2_ref, out_ref):
    r1 = x_ref[...].astype(F32) + dot(o_ref[...], wp_ref[...])
    out_ref[...] = r1 + dot(a_ref[...], w2_ref[...]) + vector(vecs_ref, 0)


def back_kernel(meta, *refs, seqs, span, begin):
    (
        dr_ref,
        x_ref,
        qkv_ref,
        lse_ref,
        w_ref,
        wp_ref,
        vecs_ref,
        pool_ref,
        from_ref,
        pbias_ref,
    ) = refs[:10]
    if begin:
        dqkv_ref, dpool_ref, acc_ref, dkvb_ref = refs[10:]
    else:
        sum_ref, _, _, dqkv_ref, dpool_ref, keep_ref, send_ref, vec_ref, acc_ref, dkvb_ref = refs[10:]
    width = x_ref.shape[1]
    scale = (width // HEADS) ** -0.5
    step = pl.program_id(0)

    @pl.when(step == 0)
    def _():
        acc_ref[...] = jnp.zeros_like(acc_ref) if begin else sum_ref[...]

    gain, shift = vector(vecs_ref, 1), vector(vecs_ref, 2)
    cp = -(-pool_ref.shape[1] // 16) * 16
    pool = padded(pool_ref[...], cp, 0.0).reshape(seqs * cp, width)
    pooled_h = (pool * gain + shift).astype(BF)
    kvb = dot(pooled_h, w_ref[:, width:]).astype(BF)
    dr = dr_ref[...]
    do = dot_nt(dr.astype(BF), wp_ref[...]).astype(BF)
    pairs = range(HEADS // 2)
    col = lambda part, p: slice(part * width + p * 128, part * width + (p + 1) * 128)
    for s in range(seqs):
        rows = slice(s * span, (s + 1) * span)
        prow = slice(s * cp, (s + 1) * cp)
        bias = span_bias(from_ref[s], padded(pbias_ref[s], cp, masked))
        both = lambda part, p: jnp.concatenate(
            [qkv_ref[rows, col(part, p)], kvb[prow, col(part - 1, p)]], axis=0
        )
        q = [qkv_ref[rows, col(0, p)] for p in pairs]
        g = [do[rows, col(0, p)] for p in pairs]
        keys = [both(1, p) for p in pairs]
        scores = [dot(keys[p], two_heads_lanes(q[p].T)) + bias for p in pairs]
        dprob = [dot(both(2, p), two_heads_lanes(g[p].T)) for p in pairs]
        prob = [jnp.exp(scores[p] - lse_ref[s, p : p + 1, :]) for p in pairs]
        weighted = [prob[p] * dprob[p] for p in pairs]
        ds = [
            (weighted[p] - prob[p] * jnp.sum(weighted[p], axis=0, keepdims=True)).astype(BF)
            for p in pairs
        ]
        dv = [dot(prob[p].astype(BF), two_heads_rows(g[p])).astype(BF) for p in pairs]
        dq = [(diagonal(dot_tn(keys[p], ds[p])) * scale).astype(BF) for p in pairs]
        dk = [dot(ds[p], two_heads_rows(q[p])).astype(BF) for p in pairs]
        for p in pairs:
            dqkv_ref[rows, col(0, p)] = dq[p].T
            dqkv_ref[rows, col(1, p)] = dk[p][:span]
            dqkv_ref[rows, col(2, p)] = dv[p][:span]
            dkvb_ref[prow, col(0, p)] = dk[p][span:]
            dkvb_ref[prow, col(1, p)] = dv[p][span:]
    n, _ = normed(x_ref[...].astype(F32))
    h = (n * gain + shift).astype(BF)
    dqkv, dkvb = dqkv_ref[...], dkvb_ref[...]
    acc_ref[:width] += dot_tn(h, dqkv)
    acc_ref[:width, width:] += dot_tn(pooled_h, dkvb)
    acc_ref[width : width + 1] += jnp.sum(dqkv.astype(F32), axis=0, keepdims=True)
    acc_ref[width : width + 1, width:] += jnp.sum(dkvb.astype(F32), axis=0, keepdims=True)
    dpool_ref[...] = dot_nt(dkvb, w_ref[:, width:]).astype(BF).reshape(seqs, cp, width)
    if begin:
        return

    @pl.when(step == pl.num_programs(0) - 1)
    def _():
        nh = acc_ref.shape[1] // 2
        for which, ref in ((0, keep_ref), (1, send_ref)):
            half = meta[2] if which == 0 else 1 - meta[2]
            ref[...] = acc_ref[:width, pl.ds(pl.multiple_of(half * nh, 128), nh)].astype(BF)
        w = w_ref[...].astype(F32)

        def row(m):
            total = jnp.sum(m, axis=1, keepdims=True)
            return jnp.broadcast_to(total, (width, 128)).T[:1]

        dshift = row(w * acc_ref[width : width + 1])
        dgain = (row(w * acc_ref[:width]) - shift * dshift) / gain
        vec_ref[0:1] = dgain
        vec_ref[1:2] = dshift


def last_kernel(rel_ref, dr_ref, x_ref, dqkv_ref, w_ref, dpool_ref, vecs_ref, out_ref, *, seqs, span):
    n, rstd = normed(x_ref[...].astype(F32))
    dh = dot_nt(dqkv_ref[...], w_ref[...])
    for i in range(seqs):
        first = rel_ref[pl.program_id(0) * seqs + i]
        rows = slice(i * span, (i + 1) * span)
        count = jnp.full((1, 1), span - first, jnp.int32).astype(F32)
        share = dpool_ref[i] / count
        row = lax.broadcasted_iota(jnp.int32, (span, n.shape[1]), 0)
        e = (dh[rows] + jnp.where(row >= first, share, 0.0)) * vector(vecs_ref, 1)
        out_ref[rows, :] = dr_ref[rows, :] + norm_back(e, n[rows], rstd[rows])


def after(a, *first):
    return lax.optimization_barrier((a, *first))[0]


def params(mib):
    return pltpu.CompilerParams(dimension_semantics=("arbitrary",), vmem_limit_bytes=mib * MIB)


LITTLE = pl.CostEstimate(flops=1, bytes_accessed=1, transcendentals=0)


def local(
    tokens,
    cotangent,
    doc_lengths,
    attend,
    project,
    widen,
    narrow,
    hidden_bias,
    final_bias,
    gain_first,
    shift_first,
    gain_second,
    shift_second,
    *,
    sizes,
):
    zs, xs, ys, cs = sizes
    nshard = zs * xs
    seq_count, span, width = tokens.shape
    rows = seq_count * span
    hidden = widen.shape[1]
    rps = attend.shape[0]
    rep, shard = lax.axis_index("rep"), lax.axis_index("shard")
    z, x, y, core = shard // xs, shard % xs, rep // cs, rep % cs
    meta = jnp.stack([z, x, core]).astype(jnp.int32)

    def send(a, dz=0, dx=0, dy=0, dc=0):
        perm = []
        for r in range(ys * cs):
            for s in range(nshard):
                r2 = (r // cs + dy) % ys * cs + (r % cs + dc) % cs
                s2 = (s // xs + dz) % zs * xs + (s % xs + dx) % xs
                perm.append((r * nshard + s, r2 * nshard + s2))
        return lax.ppermute(a, ("rep", "shard"), perm)

    def levels(a):
        return jnp.concatenate([a] + [send(a, dz=k) for k in range(1, zs)], axis=0)

    def sides(a):
        return [a] + [send(a, dx=k) for k in range(1, xs)]

    ndoc = doc_lengths.shape[1]
    upto = jnp.arange(ndoc)[:, None] <= jnp.arange(ndoc)[None, :]
    ends = jnp.sum(jnp.where(upto[None], doc_lengths[:, :, None], 0), axis=1, dtype=jnp.int32)
    starts = ends - doc_lengths
    base = shard * span
    positions = base + jnp.arange(span, dtype=jnp.int32)
    segment = jnp.sum(
        (positions[None, :, None] >= ends[:, None, :]).astype(jnp.int32), axis=-1, dtype=jnp.int32
    )

    def start_at(at):
        before = starts[:, None, :] <= at[..., None]
        return jnp.max(jnp.where(before, starts[:, None, :], 0), axis=-1)

    doc_from = (start_at(positions[None, :]) - base)[:, None, :]
    slot = jnp.arange(nshard, dtype=jnp.int32)
    slot_span = (z - slot % zs + zs) % zs * xs + (x - slot // zs + xs) % xs
    slot_last = slot_span * span + span - 1
    last_doc = jnp.sum(
        (slot_last[None, :, None] >= ends[:, None, :]).astype(jnp.int32), axis=-1, dtype=jnp.int32
    )
    counts = jnp.minimum(span, slot_last[None, :] + 1 - start_at(slot_last[None, :]))
    seen = (slot_span[None, :, None] < shard) & (last_doc[:, :, None] == segment[:, None, :])
    pbias = jnp.where(seen, jnp.log(counts.astype(F32))[:, :, None], masked)
    cp = max(16, -(-nshard // 16) * 16)
    rel = span - counts[:, 0]

    x2 = tokens.reshape(rows, width)
    y2 = cotangent.reshape(rows, width)
    smem = pl.BlockSpec(memory_space=pltpu.SMEM)
    hbm = pl.BlockSpec(memory_space=pl.ANY)
    nh = attend.shape[1] // 2
    attend_col = levels(lax.dynamic_slice_in_dim(attend, core * nh, nh, 1))
    pool_seqs = 4
    pool = pl.pallas_call(
        functools.partial(pool_kernel, seqs=pool_seqs, span=span),
        grid=(seq_count // pool_seqs,),
        in_specs=[smem, pl.BlockSpec((pool_seqs * span, width), lambda i: (i, 0))],
        out_specs=pl.BlockSpec((pool_seqs, 1, width), lambda i: (i, 0, 0)),
        out_shape=jax.ShapeDtypeStruct((seq_count, 1, width), F32),
        compiler_params=params(16),
        cost_estimate=LITTLE,
        name="pool",
    )(rel, after(x2, attend_col))
    per = hidden // width
    hs = hidden_bias.shape[0]

    def own_lanes(v):
        n = v.shape[1]
        at = jnp.arange(nshard * n, dtype=jnp.int32) // n
        return jnp.where(at == shard, jnp.tile(v.astype(F32), (1, nshard)), 0.0)

    small = jnp.stack([final_bias, gain_first, shift_first, gain_second, shift_second])
    packed = jnp.concatenate(
        [
            pool.reshape(seq_count, width),
            own_lanes(small),
            own_lanes(hidden_bias[None]).reshape(per, width),
        ],
        axis=0,
    )
    small_col = levels(packed)

    ph, wh = width // 2, hidden // 2
    half_p = jnp.concatenate(
        [
            lax.dynamic_slice_in_dim(project, core * ph, ph, 1),
            lax.dynamic_slice_in_dim(widen, core * wh, wh, 1),
        ],
        axis=1,
    )
    nhalf = lax.dynamic_slice_in_dim(narrow, core * (narrow.shape[0] // 2), narrow.shape[0] // 2, 0)
    half_n = jnp.concatenate([nhalf[j * rps : (j + 1) * rps] for j in range(per // 2)], axis=1)
    attend_cols = sides(attend_col)
    attend_parts = attend_cols + [send(m, dc=1) for m in attend_cols]
    widen_col = levels(after(half_p, attend_col, pool))
    small_cols = sides(small_col)
    narrow_col = levels(after(half_n, widen_col))
    widen_sides = sides(after(widen_col, *attend_parts, *small_cols))

    slots = jnp.concatenate(small_cols, axis=0).reshape(nshard, -1, width)
    pool_all = jnp.transpose(slots[:, :seq_count], (1, 0, 2))
    vectors = jnp.sum(slots[:, seq_count:], axis=0)
    nvectors = vectors.shape[0]

    seqs = 4
    calls = 2
    steps = seq_count // seqs // calls
    all_spec = lambda a, b: pl.BlockSpec((a, b), lambda i, m: (0, 0))
    row_spec = lambda n, w, c=0: pl.BlockSpec((n, w), lambda i, m: (i + c * steps, 0))
    seq_spec = lambda n, a, b, c=0: pl.BlockSpec((n, a, b), lambda i, m: (i + c * steps, 0, 0))
    act_specs = lambda c: [
        row_spec(seqs * span, 3 * width, c),
        row_spec(seqs * span, width, c),
        seq_spec(seqs, HEADS // 2, 2 * span, c),
    ]
    act_shapes = [
        jax.ShapeDtypeStruct((rows, 3 * width), BF),
        jax.ShapeDtypeStruct((rows, width), BF),
        jax.ShapeDtypeStruct((seq_count, HEADS // 2, 2 * span), F32),
    ]

    def attention(c, x2, weights, before):
        body = functools.partial(
            attend_kernel, sizes=(zs, xs), seqs=seqs, span=span, rps=rps, whole=c > 0
        )
        return pl.pallas_call(
            body,
            grid_spec=pltpu.PrefetchScalarGridSpec(
                num_scalar_prefetch=1,
                grid=(steps,),
                in_specs=[
                    row_spec(seqs * span, width, c),
                    all_spec(nvectors, width),
                    seq_spec(seqs, nshard, width, c),
                    seq_spec(seqs, 1, span, c),
                    seq_spec(seqs, nshard, span, c),
                ]
                + ([all_spec(width, 3 * width)] if c else [hbm] * len(weights))
                + [hbm] * len(before),
                out_specs=([] if c else [all_spec(width, 3 * width)]) + act_specs(c),
                scratch_shapes=[] if c else [pltpu.SemaphoreType.DMA((1, 2 * nshard))],
            ),
            out_shape=([] if c else [jax.ShapeDtypeStruct((width, 3 * width), BF)]) + act_shapes,
            input_output_aliases={7 + i: i for i in range(len(before))},
            compiler_params=params(58),
            cost_estimate=LITTLE,
            name="attention",
        )(meta, x2, vectors, pool_all, doc_from, pbias, *weights, *before)

    w_all, qkv, o, lse = attention(0, after(x2, widen_col), attend_parts, [])
    widen_mine = jnp.concatenate(after(widen_sides, lse), axis=0)
    narrow_sides = sides(after(narrow_col, lse))
    widen_other = send(widen_mine, dc=1)
    qkv, o, lse = attention(1, after(x2, narrow_col, widen_mine), [w_all], [qkv, o, lse])
    narrow_mine = jnp.concatenate(after(narrow_sides, lse), axis=0)
    ffn_parts = [widen_mine, widen_other, narrow_mine, send(narrow_mine, dc=1)]

    tile = 512
    packet = ph + wh + per * ph
    steps = 0
    dr, a, keep_f, send_f, wp_all, w2_all, vec_f = pl.pallas_call(
        functools.partial(ffn_kernel, sizes=(zs, xs), rps=rps),
        grid_spec=pltpu.PrefetchScalarGridSpec(
            num_scalar_prefetch=1,
            grid=(rows // tile,),
            in_specs=[
                row_spec(tile, width),
                row_spec(tile, width),
                row_spec(tile, width),
                all_spec(nvectors, width),
            ]
            + [hbm] * 4,
            out_specs=[
                row_spec(tile, width),
                row_spec(tile, hidden),
                all_spec(width, packet),
                all_spec(width, packet),
                all_spec(width, width),
                all_spec(hidden, width),
                all_spec(8, hidden),
            ],
            scratch_shapes=[
                pltpu.VMEM((width, hidden), BF),
                pltpu.VMEM((width, hidden), F32),
                pltpu.VMEM((hidden, width), F32),
                pltpu.VMEM((width, width), F32),
                pltpu.SemaphoreType.DMA((3, nshard * per)),
            ],
        ),
        out_shape=[
            jax.ShapeDtypeStruct((rows, width), F32),
            jax.ShapeDtypeStruct((rows, hidden), BF),
            jax.ShapeDtypeStruct((width, packet), BF),
            jax.ShapeDtypeStruct((width, packet), BF),
            jax.ShapeDtypeStruct((width, width), BF),
            jax.ShapeDtypeStruct((hidden, width), BF),
            jax.ShapeDtypeStruct((8, hidden), F32),
        ],
        compiler_params=params(58),
        cost_estimate=LITTLE,
        name="ffn",
    )(meta, o, x2, y2, vectors, *ffn_parts)

    def add(parts, kind):
        total = parts[0].astype(F32)
        for p in parts[1:]:
            total = total + p.astype(F32)
        return total.astype(kind)

    def over_x(a):
        piece = lambda dx: lax.dynamic_slice_in_dim(a, (x + dx) % xs, 1, 1)
        return add([send(piece(dx), dx=dx) if dx else piece(0) for dx in range(xs)], BF)

    def over_y(a):
        n = a.shape[-1] // ys
        piece = lambda dy: lax.dynamic_slice_in_dim(a, (y + dy) % ys * n, n, a.ndim - 1)
        return add([send(piece(dy), dy=dy) if dy else piece(0) for dy in range(ys)], BF)

    def over_z(a, cover):
        k = a.shape[0] // zs
        piece = lambda dz: lax.dynamic_slice_in_dim(a, (z + dz) % zs * k, k, 0)
        parts = [send(piece(dz), dz=dz) if dz else piece(0) for dz in range(zs)]
        return add(after(parts, cover), BF)

    def over_xy(part, cover):
        n = part.shape[1] // ys
        k = part.shape[0] // nshard
        view = part.reshape(zs, xs, k, ys * n)

        def corner(dx, dy):
            at = (0, (x + dx) % xs, 0, (y + dy) % ys * n)
            return lax.dynamic_slice(view, at, (zs, 1, k, n)).reshape(zs * k, n)

        parts = [
            send(corner(dx, dy), dx=dx, dy=dy) if dx or dy else corner(0, 0)
            for dx in range(xs)
            for dy in range(ys)
        ]
        return add(after(parts, cover), BF)

    def replicas(part):
        found = {
            (dy, dc): send(part, dy=dy, dc=dc) if dy or dc else part
            for dy in range(ys)
            for dc in range(cs)
        }
        total = []
        for at in range(ys * cs):
            picked = jnp.zeros(part.shape, F32)
            for (dy, dc), piece in found.items():
                mine = ((y - dy + ys) % ys == at % ys) & ((core - dc + cs) % cs == at // ys)
                picked = jnp.where(mine, piece.astype(F32), picked)
            total.append(picked)
        return total

    steps = seq_count // seqs // calls

    def back(c, dr, before):
        nacc = width + 8
        sums = [all_spec(nacc, 3 * width)]
        halves = [all_spec(width, 3 * width // 2)] * 2 + [all_spec(8, width)]
        half_shapes = [
            jax.ShapeDtypeStruct((width, 3 * width // 2), BF),
            jax.ShapeDtypeStruct((width, 3 * width // 2), BF),
            jax.ShapeDtypeStruct((8, width), F32),
        ]
        return pl.pallas_call(
            functools.partial(back_kernel, seqs=seqs, span=span, begin=c == 0),
            grid_spec=pltpu.PrefetchScalarGridSpec(
                num_scalar_prefetch=1,
                grid=(steps,),
                in_specs=[
                    row_spec(seqs * span, width, c),
                    row_spec(seqs * span, width, c),
                    row_spec(seqs * span, 3 * width, c),
                    seq_spec(seqs, HEADS // 2, 2 * span, c),
                    all_spec(width, 3 * width),
                    all_spec(width, width),
                    all_spec(nvectors, width),
                    seq_spec(seqs, nshard, width, c),
                    seq_spec(seqs, 1, span, c),
                    seq_spec(seqs, nshard, span, c),
                ]
                + ((sums + [hbm, hbm]) if c else []),
                out_specs=[row_spec(seqs * span, 3 * width, c), seq_spec(seqs, cp, width, c)]
                + (halves if c else sums),
                scratch_shapes=([pltpu.VMEM((nacc, 3 * width), F32)] if c else [])
                + [pltpu.VMEM((seqs * cp, 2 * width), BF)],
            ),
            out_shape=[
                jax.ShapeDtypeStruct((rows, 3 * width), BF),
                jax.ShapeDtypeStruct((seq_count, cp, width), BF),
            ]
            + (half_shapes if c else [jax.ShapeDtypeStruct((nacc, 3 * width), F32)]),
            input_output_aliases={12: 0, 13: 1} if c else {},
            compiler_params=params(58),
            cost_estimate=LITTLE,
            name="back",
        )(meta, dr, x2, qkv, lse, w_all, wp_all, vectors, pool_all, doc_from, pbias, *before)

    dqkv, dpool, sums = back(0, dr, [])
    part_f = add([keep_f, after(send(send_f, dc=1), sums)], BF)
    dqkv, dpool, keep_a, send_a, vec_a = back(1, after(dr, part_f), [sums, dqkv, dpool])
    kf = part_f.shape[0] // nshard
    view = part_f.reshape(zs, xs, kf, packet)
    first_f = over_x(view[:, :, : kf // 2])
    second_f = over_y(view[:, :, kf // 2 :])

    dpool, keep_a = after((dpool, keep_a), first_f, second_f)
    part_a = add([keep_a, send(send_a, dc=1)], BF)
    part_f = jnp.concatenate([over_y(first_f), over_x(second_f)], axis=2)
    part_f = part_f.reshape(zs * kf, packet // ys)
    out_tile = 256
    block_out = pl.pallas_call(
        out_kernel,
        grid=(rows // out_tile,),
        in_specs=[
            pl.BlockSpec((out_tile, width), lambda i: (i, 0)),
            pl.BlockSpec((out_tile, width), lambda i: (i, 0)),
            pl.BlockSpec((out_tile, hidden), lambda i: (i, 0)),
            pl.BlockSpec((nvectors, width), lambda i: (0, 0)),
            pl.BlockSpec((width, width), lambda i: (0, 0)),
            pl.BlockSpec((hidden, width), lambda i: (0, 0)),
        ],
        out_specs=pl.BlockSpec((out_tile, width), lambda i: (i, 0)),
        out_shape=jax.ShapeDtypeStruct((rows, width), F32),
        compiler_params=params(58),
        cost_estimate=LITTLE,
        name="out",
    )(after(o, part_a, part_f), x2, a, vectors, wp_all, w2_all)
    share_a = over_xy(part_a, block_out)
    share_f = over_z(part_f, block_out)
    later_a = share_a
    grad_f = jnp.concatenate(replicas(share_f), axis=1)
    halves = [grad_f[:, i * packet : (i + 1) * packet] for i in range(2)]
    grad_project = jnp.concatenate([h[:, :ph] for h in halves], axis=1)
    grad_widen = jnp.concatenate([h[:, ph : ph + wh] for h in halves], axis=1)
    grad_narrow = jnp.concatenate(
        [
            jnp.concatenate(
                [h[:, ph + wh + j * ph : ph + wh + (j + 1) * ph] for h in halves], axis=1
            )
            for j in range(per)
        ],
        axis=0,
    )

    vec = jnp.concatenate(
        [vec_f[0].reshape(per, width), vec_f[1:2, :width], vec_a[:2], vec_f[2:4, :width]], axis=0
    ).astype(BF)
    nvec = vec.shape[0]
    dp = jnp.transpose(dpool[:, :nshard], (1, 0, 2)).reshape(xs, zs, seq_count, width)
    dp = jnp.concatenate([dp, jnp.broadcast_to(vec, (xs, zs, nvec, width))], axis=2)
    level = [send(dp[:, k], dz=-k) if k else dp[:, 0] for k in range(zs)]
    level = add(after(level, block_out), BF)
    own = add([send(level[k], dx=-k) if k else level[0] for k in range(xs)], F32)
    own_vec = jnp.concatenate(
        [lax.dynamic_slice(own[seq_count:].reshape(nvec * width), (shard * hs,), (hs,))]
        + [
            lax.dynamic_slice(own[seq_count + per + i], (shard * rps,), (rps,))
            for i in range(5)
        ]
    ).astype(BF)
    seqs = 2
    tokens_grad = pl.pallas_call(
        functools.partial(last_kernel, seqs=seqs, span=span),
        grid=(seq_count // seqs,),
        in_specs=[
            smem,
            pl.BlockSpec((seqs * span, width), lambda i: (i, 0)),
            pl.BlockSpec((seqs * span, width), lambda i: (i, 0)),
            pl.BlockSpec((seqs * span, 3 * width), lambda i: (i, 0)),
            pl.BlockSpec((width, 3 * width), lambda i: (0, 0)),
            pl.BlockSpec((seqs, 1, width), lambda i: (i, 0, 0)),
            pl.BlockSpec((nvectors, width), lambda i: (0, 0)),
        ],
        out_specs=pl.BlockSpec((seqs * span, width), lambda i: (i, 0)),
        out_shape=jax.ShapeDtypeStruct((rows, width), F32),
        compiler_params=params(58),
        cost_estimate=LITTLE,
        name="last",
    )(rel, after(dr, later_a), x2, dqkv, w_all, own[:seq_count].reshape(seq_count, 1, width), vectors)

    share_a = over_z(share_a, tokens_grad)
    ncol = share_a.shape[1]
    vrows = -(-own_vec.shape[0] // ncol)
    own_vec = jnp.pad(own_vec, (0, vrows * ncol - own_vec.shape[0])).reshape(vrows, ncol)
    found = replicas(jnp.concatenate([share_a, own_vec], axis=0))
    grad_attend = jnp.concatenate([f[:rps] for f in found], axis=1)
    vec = sum(f[rps:] for f in found).reshape(vrows * ncol)
    vecs = [vec[:hs]] + [vec[hs + i * rps : hs + (i + 1) * rps] for i in range(5)]
    return (
        block_out.reshape(tokens.shape),
        tokens_grad.reshape(tokens.shape),
        grad_attend,
        grad_project,
        grad_widen,
        grad_narrow,
        *vecs,
    )


def solution(mesh):
    first = mesh.devices[0]
    xs = len({d.coords[0] for d in first})
    cs = len({d.core_on_chip for d in mesh.devices[:, 0]})
    sizes = (mesh.shape["shard"] // xs, xs, mesh.shape["rep"] // cs, cs)
    row = P("shard", None)
    vec = P("shard")
    act = P("rep", "shard", None)
    return jax.shard_map(
        functools.partial(local, sizes=sizes),
        mesh=mesh,
        in_specs=(act, act, P("rep", None), row, row, row, row) + (vec,) * 6,
        out_specs=(act, act, row, row, row, row) + (vec,) * 6,
        check_vma=False,
    )
```

time: 300 us -> 230 us (0.77)
  waiting for transfers between devices: 88.1 us -> 27 us
  starting transfers between devices: 64.1 us -> 55.5 us
    ppermute x50 -> x45, waiting for transfers between devices: 88.1 us -> 27 us  [send(): return lax.ppermute(a, ('rep', 'shard'), perm)]
    ppermute x50 -> x45, starting transfers between devices: 64.1 us -> 55.5 us  [send(): return lax.ppermute(a, ('rep', 'shard'), perm)]
    pallas_call x1, Pallas kernels: 4.65 us -> 11.6 us  [local(): pl.pallas_call(functools.partial(last_kernel, seqs=seqs, span=span), grid...]
    pallas_call x3 -> x6, Pallas kernels: 109 us -> 104 us  [the longest x1 42.4 us: local(): pl.pallas_call(functools.partial(ffn_kernel, sizes=(zs, xs), rps=rps), gr...]
    unnamed x56 -> x42, local copies, waits for them, and re-layouts: 6.61 us -> 4.29 us
  transfers between devices with their start and end apart: 50 -> 45, of which waited for: 24 -> 13; matrix products, arithmetic and copies ran while one was open for 5% -> 9% of each run, Pallas kernels for 11% -> 32%
where the time goes in v2:
time: 230 us; the launch traced here: 229 us
  Pallas kernels  118 us (51%)
  starting transfers between devices  55.5 us (24%)
  waiting for transfers between devices  27 us (12%)
  local copies, waits for them, and re-layouts  14.9 us (6%)
  other arithmetic  11.7 us (5%)
    ppermute x45, starting transfers between devices, send(): return lax.ppermute(a, ('rep', 'shard'), perm)  55.5 us
    pallas_call x1, Pallas kernels, local(): pl.pallas_call(functools.partial(ffn_kernel, sizes=(zs, xs), rps=rps), gr...  42.4 us
    pallas_call x2, Pallas kernels, back(): pl.pallas_call(functools.partial(back_kernel, seqs=seqs, span=span, begin...  29.7 us
    ppermute x45, waiting for transfers between devices, send(): return lax.ppermute(a, ('rep', 'shard'), perm)  27 us
    pallas_call x2, Pallas kernels, attention(): pl.pallas_call(body, grid_spec=pltpu.PrefetchScalarGridSpec(num_scalar_pr...  19.3 us
    pallas_call x1, Pallas kernels, local(): pl.pallas_call(out_kernel, grid=(rows // out_tile,), in_specs=[pl.BlockSp...  12.8 us
    pallas_call x1, Pallas kernels, local(): pl.pallas_call(functools.partial(last_kernel, seqs=seqs, span=span), grid...  11.6 us
  transfers between devices with their start and end apart: 45, of which 13 were waited for; matrix products, arithmetic and copies ran while one was open for 9% of the time, Pallas kernels for 32%

profile of v2, /device:TPU:0, one launch (start us, length us, event | category | flops | bytes accessed | tf_op | source)
XLA Modules:
  0.0 228.7 jit_solution(16086776559755242540)
XLA Ops:
  0.7 1.1 constant_dynamic-slice_fusion.22
  1.7 3.0 %collective-permute-start = (bf16[64,768]{1,0:T(8,128)(2,1)S(1)}, bf16[64,768]{1,0:T(8,128)(2,1)S(1)}, u32[]{:S(2)}, u32[]{:S(2)}) collective-permute-start(bf16[64,768]{1,0:T(8,128)(2,1)S(1)} %constant_dynamic-slice_fusion.22), channel_id=1, source_target_pairs={{0,2},{1,3},{2,4},{3,5},{4,6},{5,7},{6,0},{7,1},{8,10},{9,11},{10,... | collective-permute-start | bytes 294920 | tf_op jit(solution)/shard_map/ppermute | solution.py:435
  4.8 2.6 %collective-permute-start.1 = (bf16[64,768]{1,0:T(8,128)(2,1)S(1)}, bf16[64,768]{1,0:T(8,128)(2,1)S(1)}, u32[]{:S(2)}, u32[]{:S(2)}) collective-permute-start(bf16[64,768]{1,0:T(8,128)(2,1)S(1)} %constant_dynamic-slice_fusion.22), channel_id=1, source_target_pairs={{0,4},{1,5},{2,6},{3,7},{4,0},{5,1},{6,2},{7,3},{8,12},{9,13},{10,... | collective-permute-start | bytes 294920 | tf_op jit(solution)/shard_map/ppermute | solution.py:435
  7.4 1.3 collective-permute-start.2
  8.8 0.8 select_reduce_fusion.1
  10.3 0.7 stack.39
  13.4 0.8 constant_dynamic-slice_fusion.24
  14.2 0.9 constant_dynamic-slice_fusion.21
  15.1 0.7 and_select_fusion.refs_4_.refs_9_
  16.0 2.2 pool.1
  18.3 0.7 collective-permute-start.12
  19.0 1.5 collective-permute-start.13
  20.5 1.7 collective-permute-start.14
  22.2 1.5 collective-permute-start.9
  24.7 1.0 collective-permute-start.4
  26.3 2.4 %collective-permute-start.5 = (bf16[64,1280]{1,0:T(8,128)(2,1)S(1)}, bf16[64,1280]{1,0:T(8,128)(2,1)S(1)}, u32[]{:S(2)}, u32[]{:S(2)}) collective-permute-start(bf16[64,1280]{1,0:T(8,128)(2,1)S(1)} %pad_maximum_fusion.4), channel_id=1, source_target_pairs={{0,6},{1,7},{2,0},{3,1},{4,2},{5,3},{6,4},{7,5},{8,14},{9,15},{10,... | collective-permute-start | bytes 491528 | tf_op jit(solution)/shard_map/ppermute | solution.py:435
  29.3 3.3 %collective-permute-done.3 = bf16[64,1280]{1,0:T(8,128)(2,1)S(1)} collective-permute-done((bf16[64,1280]{1,0:T(8,128)(2,1)S(1)}, bf16[64,1280]{1,0:T(8,128)(2,1)S(1)}, u32[]{:S(2)}, u32[]{:S(2)}) %collective-permute-start.3) | collective-permute-done | bytes 163872 | tf_op jit(solution)/shard_map/ppermute | solution.py:435
  32.6 1.1 collective-permute-start.15
  34.0 4.3 %collective-permute-done.4 = bf16[64,1280]{1,0:T(8,128)(2,1)S(1)} collective-permute-done((bf16[64,1280]{1,0:T(8,128)(2,1)S(1)}, bf16[64,1280]{1,0:T(8,128)(2,1)S(1)}, u32[]{:S(2)}, u32[]{:S(2)}) %collective-permute-start.4) | collective-permute-done | bytes 163872 | tf_op jit(solution)/shard_map/ppermute | solution.py:435
  38.3 1.4 collective-permute-done.15
  39.7 1.8 collective-permute-start.16
  42.1 3.4 %collective-permute-start.6 = (bf16[64,1024]{1,0:T(8,128)(2,1)S(1)}, bf16[64,1024]{1,0:T(8,128)(2,1)}, u32[]{:S(2)}, u32[]{:S(2)}) collective-permute-start(bf16[64,1024]{1,0:T(8,128)(2,1)S(1)} %pad_maximum_fusion.5), channel_id=1, source_target_pairs={{0,2},{1,3},{2,4},{3,5},{4,6},{5,7},{6,0},{7,1},{8,10},{9,11},{10,... | collective-permute-start | bytes 393224 | tf_op jit(solution)/shard_map/ppermute | solution.py:435
  45.5 1.9 collective-permute-start.7
  47.4 2.9 %collective-permute-start.8 = (bf16[64,1024]{1,0:T(8,128)(2,1)S(1)}, bf16[64,1024]{1,0:T(8,128)(2,1)}, u32[]{:S(2)}, u32[]{:S(2)}) collective-permute-start(bf16[64,1024]{1,0:T(8,128)(2,1)S(1)} %pad_maximum_fusion.5), channel_id=1, source_target_pairs={{0,6},{1,7},{2,0},{3,1},{4,2},{5,3},{6,4},{7,5},{8,14},{9,15},{10,... | collective-permute-start | bytes 393224 | tf_op jit(solution)/shard_map/ppermute | solution.py:435
  50.3 1.6 concatenate.91
  52.6 0.9 copy.48
  53.5 0.9 constant_dynamic-update-slice_fusion.6
  54.5 0.9 constant_dynamic-update-slice_fusion.5
  55.5 0.9 constant_dynamic-update-slice_fusion.4
  56.4 10.1 %attention.2 = (bf16[512,1536]{1,0:T(8,128)(2,1)}, bf16[2048,1536]{1,0:T(8,128)(2,1)}, bf16[2048,512]{1,0:T(8,128)(2,1)}, f32[16,4,256]{2,1,0:T(4,128)}) custom-call(s32[3]{0:T(128)} %pad_add_fusion.meta, bf16[2048,512]{1,0:T(8,128)(2,1)} %bitcast.57, f32[9,512]{1,0:T(8,128)} %slice_reduce_fusion.refs_1_.refs_3_.refs_6_.vecs_ref, f32[16,8,512]{2,1,0:T(8,128)} %bitcast.66, ...), custom_call_target="tpu_custom_call" | custom-call | flops 1 | bytes 1 | tf_op jit(solution)/shard_map/attention/pallas_call | solution.py:549
  67.3 9.2 %attention.3 = (bf16[2048,1536]{1,0:T(8,128)(2,1)}, bf16[2048,512]{1,0:T(8,128)(2,1)}, f32[16,4,256]{2,1,0:T(4,128)}) custom-call(s32[3]{0:T(128)} %pad_add_fusion.meta, bf16[2048,512]{1,0:T(8,128)(2,1)} %bitcast.58, f32[9,512]{1,0:T(8,128)} %slice_reduce_fusion.refs_1_.refs_3_.refs_6_.vecs_ref, ...), custom_call_target="tpu_custom_call", output_to_operand_aliasing={{0}: (7, {}), {1}: (8, {}), {2}: (9, {})} | custom-call | flops 1 | bytes 1 | tf_op jit(solution)/shard_map/attention/pallas_call | solution.py:549
  76.5 3.8 %collective-permute-done.18 = bf16[256,1024]{1,0:T(8,128)(2,1)S(1)} collective-permute-done((bf16[256,1024]{1,0:T(8,128)(2,1)S(1)}, bf16[256,1024]{1,0:T(8,128)(2,1)S(1)}, u32[]{:S(2)}, u32[]{:S(2)}) %collective-permute-start.18) | collective-permute-done | bytes 524320 | tf_op jit(solution)/shard_map/ppermute | solution.py:435
  80.5 2.6 %collective-permute-done.19.refs_7_ = bf16[512,1024]{1,0:T(8,128)(2,1)S(1)} collective-permute-done((bf16[512,1024]{1,0:T(8,128)(2,1)S(1)}, bf16[512,1024]{1,0:T(8,128)(2,1)S(1)}, u32[]{:S(2)}, u32[]{:S(2)}) %collective-permute-start.19) | collective-permute-done | bytes 1048608 | tf_op jit(solution)/shard_map/ppermute | solution.py:435
  83.1 1.0 copy-done.9
  84.5 42.4 %ffn.1 = (f32[2048,512]{1,0:T(8,128)}, bf16[2048,2048]{1,0:T(8,128)(2,1)}, bf16[512,2304]{1,0:T(8,128)(2,1)}, bf16[512,2304]{1,0:T(8,128)(2,1)}, bf16[512,512]{1...) custom-call(s32[3]{0:T(128)} %pad_add_fusion.meta, bf16[2048,512]{1,0:T(8,128)(2,1)} %get-tuple-element.98.refs_0_.o_ref, ...), custom_call_target="tpu_custom_call" | custom-call | flops 1 | bytes 1 | tf_op jit(solution)/shard_map/ffn/pallas_call | solution.py:584
  127.1 14.0 %back.2 = (bf16[2048,1536]{1,0:T(8,128)(2,1)}, bf16[16,16,512]{2,1,0:T(8,128)(2,1)}, f32[520,1536]{1,0:T(8,128)}) custom-call(s32[3]{0:T(128)} %pad_add_fusion.meta, f32[2048,512]{1,0:T(8,128)} %get-tuple-element.105.refs_0_.dr_ref, bf16[2048,512]{1,0:T(8,128)(2,1)} %bitcast.60, bf16[2048,1536]{1,0:T(8,128)(2,1)} %get-tuple-element.87.refs_2_, ...), custom_call_target="tpu_custom_call" | custom-call | flops 1 | bytes 1 | tf_op jit(solution)/shard_map/back/pallas_call | solution.py:690
  141.9 1.6 collective-permute-start.22
  143.5 0.8 convert.37
  145.0 15.7 %back.3 = (bf16[2048,1536]{1,0:T(8,128)(2,1)}, bf16[16,16,512]{2,1,0:T(8,128)(2,1)}, bf16[512,768]{1,0:T(8,128)(2,1)}, bf16[512,768]{1,0:T(8,128)(2,1)}, f32[8,512]{1,0:T(8,128)}) custom-call(s32[3]{0:T(128)} %pad_add_fusion.meta, f32[2048,512]{1,0:T(8,128)} %get-tuple-element.105.refs_0_.dr_ref, ...), custom_call_target="tpu_custom_call", output_to_operand_aliasing={{0}: (12, {}), {1}: (13, {})} | custom-call | flops 1 | bytes 1 | tf_op jit(solution)/shard_map/back/pallas_call | solution.py:690
  160.8 0.7 slice.309
  162.5 1.7 collective-permute-start.25
  164.3 1.1 collective-permute-start.29
  165.4 2.9 %collective-permute-start.30 = (bf16[2,25,512]{2,1,0:T(8,128)(2,1)S(1)}, bf16[2,25,512]{2,1,0:T(8,128)(2,1)S(1)}, u32[]{:S(2)}, u32[]{:S(2)}) collective-permute-start(bf16[2,25,512]{2,1,0:T(8,128)(2,1)S(1)} %get-tuple-element.152), channel_id=1, source_target_pairs={{0,4},{1,5},{2,6},{3,7},{4,0},{5,1},{6,2},{7,3},{8,12},{9,13},{10,... | collective-permute-start | bytes 153608 | tf_op jit(solution)/shard_map/ppermute | solution.py:435
  168.6 2.8 %collective-permute-done.24 = bf16[4,1,32,1152]{3,2,1,0:T(8,128)(2,1)S(1)} collective-permute-done((bf16[4,1,32,1152]{3,2,1,0:T(8,128)(2,1)S(1)}, bf16[4,1,32,1152]{3,2,1,0:T(8,128)(2,1)S(1)}, u32[]{:S(2)}, u32[]{:S(2)}) %collective-permute-start.24) | collective-permute-done | bytes 294944 | tf_op jit(solution)/shard_map/ppermute | solution.py:435
  172.0 1.7 collective-permute-start.27
  173.8 12.8 %out.1 = f32[2048,512]{1,0:T(8,128)} custom-call(bf16[2048,512]{1,0:T(8,128)(2,1)} %get-tuple-element.98.refs_0_.o_ref, bf16[2048,512]{1,0:T(8,128)(2,1)} %bitcast.62, bf16[2048,2048]{1,0:T(8,128)(2,1)} %get-tuple-element.99.a_ref, f32[9,512]{1,0:T(8,128)} %slice_reduce_fusion.refs_1_.refs_3_.refs_6_.vecs_ref, ...), custom_call_target="tpu_custom_call" | custom-call | flops 1 | bytes 1 | tf_op jit(solution)/shard_map/out/pallas_call | solution.py:737
  186.6 1.4 collective-permute-start.28
  188.0 1.7 collective-permute-start.32
  189.8 2.5 %collective-permute-start.39 = (bf16[64,1152]{1,0:T(8,128)(2,1)S(1)}, bf16[64,1152]{1,0:T(8,128)(2,1)S(1)}, u32[]{:S(2)}, u32[]{:S(2)}) collective-permute-start(bf16[64,1152]{1,0:T(8,128)(2,1)S(1)} %get-tuple-element.139), channel_id=1, source_target_pairs={{0,2},{1,3},{2,4},{3,5},{4,6},{5,7},{6,0},{7,1},{8,10},{9,11},{10,... | collective-permute-start | bytes 442376 | tf_op jit(solution)/shard_map/ppermute | solution.py:435
  192.2 2.0 collective-permute-done.32
  194.2 1.3 collective-permute-start.40
  196.0 1.2 collective-permute-start.33
  197.2 2.9 %collective-permute-start.34 = (bf16[64,384]{1,0:T(8,128)(2,1)S(1)}, bf16[64,384]{1,0:T(8,128)(2,1)S(1)}, u32[]{:S(2)}, u32[]{:S(2)}) collective-permute-start(bf16[64,384]{1,0:T(8,128)(2,1)S(1)} %get-tuple-element.160), channel_id=1, source_target_pairs={{0,4},{1,5},{2,6},{3,7},{4,0},{5,1},{6,2},{7,3},{8,12},{9,13},{10,... | collective-permute-start | bytes 147464 | tf_op jit(solution)/shard_map/ppermute | solution.py:435
  201.6 11.6 %last.1 = f32[2048,512]{1,0:T(8,128)} custom-call(s32[16]{0:T(128)} %copy-done.3, f32[2048,512]{1,0:T(8,128)} %get-tuple-element.105.refs_0_.dr_ref, bf16[2048,512]{1,0:T(8,128)(2,1)} %bitcast.63, bf16[2048,1536]{1,0:T(8,128)(2,1)} %get-tuple-element.106.dqkv_ref, bf16[512,1536]{1,0:T(8,128)(2,1)} %get-tuple-element.76.refs_5_.refs_4_.w_ref, ...), custom_call_target="tpu_custom_call" | custom-call | flops 1 | bytes 1 | tf_op jit(solution)/shard_map/last/pallas_call | solution.py:788
  213.2 1.0 collective-permute-start.41
  214.4 0.8 collective-permute-start.37
  215.2 1.0 collective-permute-start.38
  216.2 2.2 collective-permute-done.41
  219.2 1.3 collective-permute-start.44
  221.2 0.8 pad_maximum_fusion.3
  222.6 2.1 collective-permute-done.42
  224.7 1.3 collective-permute-done.43
  226.3 0.8 fusion
  227.8 0.9 maximum_maximum_fusion
  (180 shorter events, 17.4 us)
Async XLA Ops:
  0.6 12.7 %copy-start = (bf16[64,2048]{1,0:T(8,128)(2,1)S(1)}, bf16[64,2048]{1,0:T(8,128)(2,1)}, u32[]{:S(2)}) copy-start(bf16[64,2048]{1,0:T(8,128)(2,1)} %param.18) | copy-start | bytes 786436
  0.7 15.4 %copy-start.2 = (bf16[16,128,512]{2,1,0:T(8,128)(2,1)S(1)}, bf16[16,128,512]{2,1,0:T(8,128)(2,1)}, u32[]{:S(2)}) copy-start(bf16[16,128,512]{2,1,0:T(8,128)(2,1)} %param.13) | copy-start | bytes 6291460
  1.7 14.2 %collective-permute-start = (bf16[64,768]{1,0:T(8,128)(2,1)S(1)}, bf16[64,768]{1,0:T(8,128)(2,1)S(1)}, u32[]{:S(2)}, u32[]{:S(2)}) collective-permute-start(bf16[64,768]{1,0:T(8,128)(2,1)S(1)} %constant_dynamic-slice_fusion.22), channel_id=1, source_target_pairs={{0,2},{1,3},{2,4},{3,5},{4,6},{5,7},{6,0},{7,1},{8,10},{9,11},{10,... | collective-permute-start | bytes 294920 | tf_op jit(solution)/shard_map/ppermute | solution.py:435
  4.8 11.2 %collective-permute-start.1 = (bf16[64,768]{1,0:T(8,128)(2,1)S(1)}, bf16[64,768]{1,0:T(8,128)(2,1)S(1)}, u32[]{:S(2)}, u32[]{:S(2)}) collective-permute-start(bf16[64,768]{1,0:T(8,128)(2,1)S(1)} %constant_dynamic-slice_fusion.22), channel_id=1, source_target_pairs={{0,4},{1,5},{2,6},{3,7},{4,0},{5,1},{6,2},{7,3},{8,12},{9,13},{10,... | collective-permute-start | bytes 294920 | tf_op jit(solution)/shard_map/ppermute | solution.py:435
  7.4 8.6 %collective-permute-start.2 = (bf16[64,768]{1,0:T(8,128)(2,1)S(1)}, bf16[64,768]{1,0:T(8,128)(2,1)S(1)}, u32[]{:S(2)}, u32[]{:S(2)}) collective-permute-start(bf16[64,768]{1,0:T(8,128)(2,1)S(1)} %constant_dynamic-slice_fusion.22), channel_id=1, source_target_pairs={{0,6},{1,7},{2,0},{3,1},{4,2},{5,3},{6,4},{7,5},{8,14},{9,15},{10,... | collective-permute-start | bytes 294920 | tf_op jit(solution)/shard_map/ppermute | solution.py:435
  15.9 8.3 %copy-start.3 = (s32[16]{0:T(128)}, s32[16]{0:T(128)S(1)}, u32[]{:S(2)}) copy-start(s32[16]{0:T(128)S(1)} %fusion.10.rel_ref) | copy-start | bytes 196
  16.0 17.7 %copy-start.7 = (bf16[256,768]{1,0:T(8,128)(2,1)}, bf16[256,768]{1,0:T(8,128)(2,1)S(1)}, u32[]{:S(2)}) copy-start(bf16[256,768]{1,0:T(8,128)(2,1)S(1)} %pad_maximum_fusion.2.refs_5_) | copy-start | bytes 1179652
  18.3 6.5 %collective-permute-start.12 = (f32[25,512]{1,0:T(8,128)S(1)}, f32[25,512]{1,0:T(8,128)S(1)}, u32[]{:S(2)}, u32[]{:S(2)}) collective-permute-start(f32[25,512]{1,0:T(8,128)S(1)} %pad_maximum_fusion.8), channel_id=1, source_target_pairs={{0,2},{1,3},{2,4},{3,5},{4,6},{5,7},{6,0},{7,1},{8,10},{9,11},{10,... | collective-permute-start | bytes 153608 | tf_op jit(solution)/shard_map/ppermute | solution.py:435
  19.0 7.3 %collective-permute-start.13 = (f32[25,512]{1,0:T(8,128)S(1)}, f32[25,512]{1,0:T(8,128)S(1)}, u32[]{:S(2)}, u32[]{:S(2)}) collective-permute-start(f32[25,512]{1,0:T(8,128)S(1)} %pad_maximum_fusion.8), channel_id=1, source_target_pairs={{0,4},{1,5},{2,6},{3,7},{4,0},{5,1},{6,2},{7,3},{8,12},{9,13},{10,... | collective-permute-start | bytes 153608 | tf_op jit(solution)/shard_map/ppermute | solution.py:435
  20.5 8.2 %collective-permute-start.14 = (f32[25,512]{1,0:T(8,128)S(1)}, f32[25,512]{1,0:T(8,128)S(1)}, u32[]{:S(2)}, u32[]{:S(2)}) collective-permute-start(f32[25,512]{1,0:T(8,128)S(1)} %pad_maximum_fusion.8), channel_id=1, source_target_pairs={{0,6},{1,7},{2,0},{3,1},{4,2},{5,3},{6,4},{7,5},{8,14},{9,15},{10,... | collective-permute-start | bytes 153608 | tf_op jit(solution)/shard_map/ppermute | solution.py:435
  22.2 11.6 %collective-permute-start.9 = (bf16[256,768]{1,0:T(8,128)(2,1)S(1)}, bf16[256,768]{1,0:T(8,128)(2,1)S(1)}, u32[]{:S(2)}, u32[]{:S(2)}) collective-permute-start(bf16[256,768]{1,0:T(8,128)(2,1)S(1)} %pad_maximum_fusion.2.refs_5_), channel_id=1, source_target_pairs={{0,1},{1,0},{2,3},{3,2},{4,5},{5,4},{6,7},{7,6},{8,9},{9,8},{10,11... | collective-permute-start | bytes 1179656 | tf_op jit(solution)/shard_map/ppermute | solution.py:435
  23.6 8.9 %collective-permute-start.3 = (bf16[64,1280]{1,0:T(8,128)(2,1)S(1)}, bf16[64,1280]{1,0:T(8,128)(2,1)S(1)}, u32[]{:S(2)}, u32[]{:S(2)}) collective-permute-start(bf16[64,1280]{1,0:T(8,128)(2,1)S(1)} %pad_maximum_fusion.4), channel_id=1, source_target_pairs={{0,2},{1,3},{2,4},{3,5},{4,6},{5,7},{6,0},{7,1},{8,10},{9,11},{10,... | collective-permute-start | bytes 491528 | tf_op jit(solution)/shard_map/ppermute | solution.py:435
  24.7 13.5 %collective-permute-start.4 = (bf16[64,1280]{1,0:T(8,128)(2,1)S(1)}, bf16[64,1280]{1,0:T(8,128)(2,1)S(1)}, u32[]{:S(2)}, u32[]{:S(2)}) collective-permute-start(bf16[64,1280]{1,0:T(8,128)(2,1)S(1)} %pad_maximum_fusion.4), channel_id=1, source_target_pairs={{0,4},{1,5},{2,6},{3,7},{4,0},{5,1},{6,2},{7,3},{8,12},{9,13},{10,... | collective-permute-start | bytes 491528 | tf_op jit(solution)/shard_map/ppermute | solution.py:435
  26.3 12.0 %collective-permute-start.5 = (bf16[64,1280]{1,0:T(8,128)(2,1)S(1)}, bf16[64,1280]{1,0:T(8,128)(2,1)S(1)}, u32[]{:S(2)}, u32[]{:S(2)}) collective-permute-start(bf16[64,1280]{1,0:T(8,128)(2,1)S(1)} %pad_maximum_fusion.4), channel_id=1, source_target_pairs={{0,6},{1,7},{2,0},{3,1},{4,2},{5,3},{6,4},{7,5},{8,14},{9,15},{10,... | collective-permute-start | bytes 491528 | tf_op jit(solution)/shard_map/ppermute | solution.py:435
  28.7 11.0 %collective-permute-start.10 = (bf16[256,768]{1,0:T(8,128)(2,1)S(1)}, bf16[256,768]{1,0:T(8,128)(2,1)S(1)}, u32[]{:S(2)}, u32[]{:S(2)}) collective-permute-start(bf16[256,768]{1,0:T(8,128)(2,1)S(1)} %pad_maximum_fusion.2.refs_5_), channel_id=1, source_target_pairs={{0,8},{1,9},{2,10},{3,11},{4,12},{5,13},{6,14},{7,15},{8,0},{9,1},... | collective-permute-start | bytes 1179656 | tf_op jit(solution)/shard_map/ppermute | solution.py:435
  32.6 7.1 %collective-permute-start.15 = (f32[100,512]{1,0:T(8,128)S(1)}, f32[100,512]{1,0:T(8,128)}, u32[]{:S(2)}, u32[]{:S(2)}) collective-permute-start(f32[100,512]{1,0:T(8,128)S(1)} %concatenate.90), channel_id=1, source_target_pairs={{0,1},{1,0},{2,3},{3,2},{4,5},{5,4},{6,7},{7,6},{8,9},{9,8},{10,11... | collective-permute-start | bytes 614408 | tf_op jit(solution)/shard_map/ppermute | solution.py:435
  33.7 18.9 %copy-start.12 = (bf16[256,768]{1,0:T(8,128)(2,1)}, bf16[256,768]{1,0:T(8,128)(2,1)S(1)}, u32[]{:S(2)}) copy-start(bf16[256,768]{1,0:T(8,128)(2,1)S(1)} %collective-permute-done.9.refs_6_) | copy-start | bytes 1179652
  33.7 6.0 %collective-permute-start.11 = (bf16[256,768]{1,0:T(8,128)(2,1)S(1)}, bf16[256,768]{1,0:T(8,128)(2,1)S(1)}, u32[]{:S(2)}, u32[]{:S(2)}) collective-permute-start(bf16[256,768]{1,0:T(8,128)(2,1)S(1)} %collective-permute-done.9.refs_6_), channel_id=1, source_target_pairs={{0,8},{1,9},{2,10},{3,11},{4,12},{5,13},{6,14},{7,15},{8,0},{9,1},... | collective-permute-start | bytes 1179656 | tf_op jit(solution)/shard_map/ppermute | solution.py:435
  39.7 7.7 %copy-start.13 = (bf16[256,768]{1,0:T(8,128)(2,1)}, bf16[256,768]{1,0:T(8,128)(2,1)S(1)}, u32[]{:S(2)}) copy-start(bf16[256,768]{1,0:T(8,128)(2,1)S(1)} %collective-permute-done.10.refs_7_) | copy-start | bytes 1179652
  39.7 2.4 %copy-start.14 = (bf16[256,768]{1,0:T(8,128)(2,1)}, bf16[256,768]{1,0:T(8,128)(2,1)S(1)}, u32[]{:S(2)}) copy-start(bf16[256,768]{1,0:T(8,128)(2,1)S(1)} %collective-permute-done.11.refs_8_) | copy-start | bytes 1179652
  39.7 27.4 %collective-permute-start.16 = (bf16[256,1280]{1,0:T(8,128)(2,1)S(1)}, bf16[256,1280]{1,0:T(8,128)(2,1)S(1)}, u32[]{:S(2)}, u32[]{:S(2)}) collective-permute-start(bf16[256,1280]{1,0:T(8,128)(2,1)S(1)} %constant_dynamic-update-slice_fusion), channel_id=1, source_target_pairs={{0,1},{1,0},{2,3},{3,2},{4,5},{5,4},{6,7},{7,6},{8,9},{9,8},{10,11... | collective-permute-start | bytes 1966088 | tf_op jit(solution)/shard_map/ppermute | solution.py:435
  42.1 11.4 %collective-permute-start.6 = (bf16[64,1024]{1,0:T(8,128)(2,1)S(1)}, bf16[64,1024]{1,0:T(8,128)(2,1)}, u32[]{:S(2)}, u32[]{:S(2)}) collective-permute-start(bf16[64,1024]{1,0:T(8,128)(2,1)S(1)} %pad_maximum_fusion.5), channel_id=1, source_target_pairs={{0,2},{1,3},{2,4},{3,5},{4,6},{5,7},{6,0},{7,1},{8,10},{9,11},{10,... | collective-permute-start | bytes 393224 | tf_op jit(solution)/shard_map/ppermute | solution.py:435
  45.5 9.1 %collective-permute-start.7 = (bf16[64,1024]{1,0:T(8,128)(2,1)S(1)}, bf16[64,1024]{1,0:T(8,128)(2,1)}, u32[]{:S(2)}, u32[]{:S(2)}) collective-permute-start(bf16[64,1024]{1,0:T(8,128)(2,1)S(1)} %pad_maximum_fusion.5), channel_id=1, source_target_pairs={{0,4},{1,5},{2,6},{3,7},{4,0},{5,1},{6,2},{7,3},{8,12},{9,13},{10,... | collective-permute-start | bytes 393224 | tf_op jit(solution)/shard_map/ppermute | solution.py:435
  47.4 8.1 %collective-permute-start.8 = (bf16[64,1024]{1,0:T(8,128)(2,1)S(1)}, bf16[64,1024]{1,0:T(8,128)(2,1)}, u32[]{:S(2)}, u32[]{:S(2)}) collective-permute-start(bf16[64,1024]{1,0:T(8,128)(2,1)S(1)} %pad_maximum_fusion.5), channel_id=1, source_target_pairs={{0,6},{1,7},{2,0},{3,1},{4,2},{5,3},{6,4},{7,5},{8,14},{9,15},{10,... | collective-permute-start | bytes 393224 | tf_op jit(solution)/shard_map/ppermute | solution.py:435
  66.5 13.8 %collective-permute-start.18 = (bf16[256,1024]{1,0:T(8,128)(2,1)S(1)}, bf16[256,1024]{1,0:T(8,128)(2,1)S(1)}, u32[]{:S(2)}, u32[]{:S(2)}) collective-permute-start(bf16[256,1024]{1,0:T(8,128)(2,1)S(1)} %constant_dynamic-update-slice_fusion.4), channel_id=1, source_target_pairs={{0,1},{1,0},{2,3},{3,2},{4,5},{5,4},{6,7},{7,6},{8,9},{9,8},{10,11... | collective-permute-start | bytes 1572872 | tf_op jit(solution)/shard_map/ppermute | solution.py:435
  67.2 9.3 %copy-start.4 = (bf16[512,1280]{1,0:T(8,128)(2,1)}, bf16[512,1280]{1,0:T(8,128)(2,1)S(1)}, u32[]{:S(2)}) copy-start(bf16[512,1280]{1,0:T(8,128)(2,1)S(1)} %constant_dynamic-update-slice_fusion.8.refs_4_) | copy-start | bytes 3932164
  67.2 15.9 %collective-permute-start.17 = (bf16[512,1280]{1,0:T(8,128)(2,1)S(1)}, bf16[512,1280]{1,0:T(8,128)(2,1)S(1)}, u32[]{:S(2)}, u32[]{:S(2)}) collective-permute-start(bf16[512,1280]{1,0:T(8,128)(2,1)S(1)} %constant_dynamic-update-slice_fusion.8.refs_4_), channel_id=1, source_target_pairs={{0,8},{1,9},{2,10},{3,11},{4,12},{5,13},{6,14},{7,15},{8,0},{9,1},... | collective-permute-start | bytes 3932168 | tf_op jit(solution)/shard_map/ppermute | solution.py:435
  80.4 2.7 %copy-start.6 = (bf16[512,1024]{1,0:T(8,128)(2,1)}, bf16[512,1024]{1,0:T(8,128)(2,1)S(1)}, u32[]{:S(2)}) copy-start(bf16[512,1024]{1,0:T(8,128)(2,1)S(1)} %constant_dynamic-update-slice_fusion.10.refs_6_) | copy-start | bytes 3145732
  80.4 2.7 %collective-permute-start.19 = (bf16[512,1024]{1,0:T(8,128)(2,1)S(1)}, bf16[512,1024]{1,0:T(8,128)(2,1)S(1)}, u32[]{:S(2)}, u32[]{:S(2)}) collective-permute-start(bf16[512,1024]{1,0:T(8,128)(2,1)S(1)} %constant_dynamic-update-slice_fusion.10.refs_6_), channel_id=1, source_target_pairs={{0,8},{1,9},{2,10},{3,11},{4,12},{5,13},{6,14},{7,15},{8,0},{9,1},... | collective-permute-start | bytes 3145736 | tf_op jit(solution)/shard_map/ppermute | solution.py:435
  83.1 1.0 copy-start.9
  83.1 1.4 copy-start.8
  126.9 14.2 %collective-permute-start.20 = (bf16[512,2304]{1,0:T(8,128)(2,1)}, bf16[512,2304]{1,0:T(8,128)(2,1)S(1)}, u32[]{:S(2)}, u32[]{:S(2)}) collective-permute-start(bf16[512,2304]{1,0:T(8,128)(2,1)} %get-tuple-element.86), channel_id=1, source_target_pairs={{0,8},{1,9},{2,10},{3,11},{4,12},{5,13},{6,14},{7,15},{8,0},{9,1},... | collective-permute-start | bytes 7077896 | tf_op jit(solution)/shard_map/ppermute | solution.py:435
  127.1 14.0 %copy-start.5 = (bf16[512,2304]{1,0:T(8,128)(2,1)S(1)}, bf16[512,2304]{1,0:T(8,128)(2,1)}, u32[]{:S(2)}) copy-start(bf16[512,2304]{1,0:T(8,128)(2,1)} %get-tuple-element.85) | copy-start | bytes 7077892
  141.9 19.6 %collective-permute-start.22 = (bf16[4,2,32,1152]{3,2,1,0:T(8,128)(2,1)S(1)}, bf16[4,2,32,1152]{3,2,1,0:T(8,128)(2,1)S(1)}, u32[]{:S(2)}, u32[]{:S(2)}) collective-permute-start(bf16[4,2,32,1152]{3,2,1,0:T(8,128)(2,1)S(1)} %constant_dynamic-slice_fusion.19), channel_id=1, source_target_pairs={{0,16},{1,17},{2,18},{3,19},{4,20},{5,21},{6,22},{7,23},{8,24},{9,... | collective-permute-start | bytes 1769480 | tf_op jit(solution)/shard_map/ppermute | solution.py:435
  144.5 17.2 %collective-permute-start.21 = (bf16[4,1,32,2304]{3,2,1,0:T(8,128)(2,1)S(1)}, bf16[4,1,32,2304]{3,2,1,0:T(8,128)(2,1)S(1)}, u32[]{:S(2)}, u32[]{:S(2)}) collective-permute-start(bf16[4,1,32,2304]{3,2,1,0:T(8,128)(2,1)S(1)} %constant_dynamic-slice_fusion.20), channel_id=1, source_target_pairs={{0,1},{1,0},{2,3},{3,2},{4,5},{5,4},{6,7},{7,6},{8,9},{9,8},{10,11... | collective-permute-start | bytes 1769480 | tf_op jit(solution)/shard_map/ppermute | solution.py:435
  160.7 7.6 %collective-permute-start.23 = (bf16[512,768]{1,0:T(8,128)(2,1)}, bf16[512,768]{1,0:T(8,128)(2,1)S(1)}, u32[]{:S(2)}, u32[]{:S(2)}) collective-permute-start(bf16[512,768]{1,0:T(8,128)(2,1)} %get-tuple-element.97), channel_id=1, source_target_pairs={{0,8},{1,9},{2,10},{3,11},{4,12},{5,13},{6,14},{7,15},{8,0},{9,1},... | collective-permute-start | bytes 2359304 | tf_op jit(solution)/shard_map/ppermute | solution.py:435
  161.7 2.5 %copy-start.11 = (bf16[16,16,512]{2,1,0:T(8,128)(2,1)S(1)}, bf16[16,16,512]{2,1,0:T(8,128)(2,1)}, u32[]{:S(2)}) copy-start(bf16[16,16,512]{2,1,0:T(8,128)(2,1)} %get-tuple-element.107) | copy-start | bytes 786436
  161.9 6.4 %copy-start.10 = (bf16[512,768]{1,0:T(8,128)(2,1)S(1)}, bf16[512,768]{1,0:T(8,128)(2,1)}, u32[]{:S(2)}) copy-start(bf16[512,768]{1,0:T(8,128)(2,1)} %get-tuple-element.96) | copy-start | bytes 2359300
  161.9 9.5 %collective-permute-start.24 = (bf16[4,1,32,1152]{3,2,1,0:T(8,128)(2,1)S(1)}, bf16[4,1,32,1152]{3,2,1,0:T(8,128)(2,1)S(1)}, u32[]{:S(2)}, u32[]{:S(2)}) collective-permute-start(bf16[4,1,32,1152]{3,2,1,0:T(8,128)(2,1)S(1)} %constant_dynamic-slice_fusion.18), channel_id=1, source_target_pairs={{0,16},{1,17},{2,18},{3,19},{4,20},{5,21},{6,22},{7,23},{8,24},{9,... | collective-permute-start | bytes 884744 | tf_op jit(solution)/shard_map/ppermute | solution.py:435
  162.5 9.5 %collective-permute-start.25 = (bf16[4,1,32,1152]{3,2,1,0:T(8,128)(2,1)S(1)}, bf16[4,1,32,1152]{3,2,1,0:T(8,128)(2,1)S(1)}, u32[]{:S(2)}, u32[]{:S(2)}) collective-permute-start(bf16[4,1,32,1152]{3,2,1,0:T(8,128)(2,1)S(1)} %constant_dynamic-slice_fusion.17), channel_id=1, source_target_pairs={{0,1},{1,0},{2,3},{3,2},{4,5},{5,4},{6,7},{7,6},{8,9},{9,8},{10,11... | collective-permute-start | bytes 884744 | tf_op jit(solution)/shard_map/ppermute | solution.py:435
  164.3 22.3 %collective-permute-start.29 = (bf16[2,25,512]{2,1,0:T(8,128)(2,1)S(1)}, bf16[2,25,512]{2,1,0:T(8,128)(2,1)S(1)}, u32[]{:S(2)}, u32[]{:S(2)}) collective-permute-start(bf16[2,25,512]{2,1,0:T(8,128)(2,1)S(1)} %get-tuple-element.151), channel_id=1, source_target_pairs={{0,6},{1,7},{2,0},{3,1},{4,2},{5,3},{6,4},{7,5},{8,14},{9,15},{10,... | collective-permute-start | bytes 153608 | tf_op jit(solution)/shard_map/ppermute | solution.py:435
  165.4 22.6 %collective-permute-start.30 = (bf16[2,25,512]{2,1,0:T(8,128)(2,1)S(1)}, bf16[2,25,512]{2,1,0:T(8,128)(2,1)S(1)}, u32[]{:S(2)}, u32[]{:S(2)}) collective-permute-start(bf16[2,25,512]{2,1,0:T(8,128)(2,1)S(1)} %get-tuple-element.152), channel_id=1, source_target_pairs={{0,4},{1,5},{2,6},{3,7},{4,0},{5,1},{6,2},{7,3},{8,12},{9,13},{10,... | collective-permute-start | bytes 153608 | tf_op jit(solution)/shard_map/ppermute | solution.py:435
  168.3 19.7 %collective-permute-start.31 = (bf16[2,25,512]{2,1,0:T(8,128)(2,1)S(1)}, bf16[2,25,512]{2,1,0:T(8,128)(2,1)S(1)}, u32[]{:S(2)}, u32[]{:S(2)}) collective-permute-start(bf16[2,25,512]{2,1,0:T(8,128)(2,1)S(1)} %get-tuple-element.149), channel_id=1, source_target_pairs={{0,2},{1,3},{2,4},{3,5},{4,6},{5,7},{6,0},{7,1},{8,10},{9,11},{10,... | collective-permute-start | bytes 153608 | tf_op jit(solution)/shard_map/ppermute | solution.py:435
  171.4 24.5 %collective-permute-start.26 = (bf16[256,384]{1,0:T(8,128)(2,1)S(1)}, bf16[256,384]{1,0:T(8,128)(2,1)S(1)}, u32[]{:S(2)}, u32[]{:S(2)}) collective-permute-start(bf16[256,384]{1,0:T(8,128)(2,1)S(1)} %bitcast.86), channel_id=1, source_target_pairs={{0,16},{1,17},{2,18},{3,19},{4,20},{5,21},{6,22},{7,23},{8,24},{9,... | collective-permute-start | bytes 589832 | tf_op jit(solution)/shard_map/ppermute | solution.py:435
  172.0 23.9 %collective-permute-start.27 = (bf16[256,384]{1,0:T(8,128)(2,1)S(1)}, bf16[256,384]{1,0:T(8,128)(2,1)S(1)}, u32[]{:S(2)}, u32[]{:S(2)}) collective-permute-start(bf16[256,384]{1,0:T(8,128)(2,1)S(1)} %bitcast.85), channel_id=1, source_target_pairs={{0,1},{1,0},{2,3},{3,2},{4,5},{5,4},{6,7},{7,6},{8,9},{9,8},{10,11... | collective-permute-start | bytes 589832 | tf_op jit(solution)/shard_map/ppermute | solution.py:435
  186.6 9.3 %collective-permute-start.28 = (bf16[256,384]{1,0:T(8,128)(2,1)S(1)}, bf16[256,384]{1,0:T(8,128)(2,1)S(1)}, u32[]{:S(2)}, u32[]{:S(2)}) collective-permute-start(bf16[256,384]{1,0:T(8,128)(2,1)S(1)} %bitcast.84), channel_id=1, source_target_pairs={{0,17},{1,16},{2,19},{3,18},{4,21},{5,20},{6,23},{7,22},{8,25},{9,... | collective-permute-start | bytes 589832 | tf_op jit(solution)/shard_map/ppermute | solution.py:435
  188.0 6.2 %collective-permute-start.32 = (bf16[25,512]{1,0:T(8,128)(2,1)S(1)}, bf16[25,512]{1,0:T(8,128)(2,1)S(1)}, u32[]{:S(2)}, u32[]{:S(2)}) collective-permute-start(bf16[25,512]{1,0:T(8,128)(2,1)S(1)} %slice_bitcast_fusion.1), channel_id=1, source_target_pairs={{0,1},{1,0},{2,3},{3,2},{4,5},{5,4},{6,7},{7,6},{8,9},{9,8},{10,11... | collective-permute-start | bytes 76808 | tf_op jit(solution)/shard_map/ppermute | solution.py:435
  189.8 25.4 %collective-permute-start.39 = (bf16[64,1152]{1,0:T(8,128)(2,1)S(1)}, bf16[64,1152]{1,0:T(8,128)(2,1)S(1)}, u32[]{:S(2)}, u32[]{:S(2)}) collective-permute-start(bf16[64,1152]{1,0:T(8,128)(2,1)S(1)} %get-tuple-element.139), channel_id=1, source_target_pairs={{0,2},{1,3},{2,4},{3,5},{4,6},{5,7},{6,0},{7,1},{8,10},{9,11},{10,... | collective-permute-start | bytes 442376 | tf_op jit(solution)/shard_map/ppermute | solution.py:435
  194.2 22.0 %collective-permute-start.40 = (bf16[64,1152]{1,0:T(8,128)(2,1)S(1)}, bf16[64,1152]{1,0:T(8,128)(2,1)S(1)}, u32[]{:S(2)}, u32[]{:S(2)}) collective-permute-start(bf16[64,1152]{1,0:T(8,128)(2,1)S(1)} %get-tuple-element.138), channel_id=1, source_target_pairs={{0,4},{1,5},{2,6},{3,7},{4,0},{5,1},{6,2},{7,3},{8,12},{9,13},{10,... | collective-permute-start | bytes 442376 | tf_op jit(solution)/shard_map/ppermute | solution.py:435
  196.0 17.2 %collective-permute-start.33 = (bf16[64,384]{1,0:T(8,128)(2,1)S(1)}, bf16[64,384]{1,0:T(8,128)(2,1)S(1)}, u32[]{:S(2)}, u32[]{:S(2)}) collective-permute-start(bf16[64,384]{1,0:T(8,128)(2,1)S(1)} %get-tuple-element.161), channel_id=1, source_target_pairs={{0,2},{1,3},{2,4},{3,5},{4,6},{5,7},{6,0},{7,1},{8,10},{9,11},{10,... | collective-permute-start | bytes 147464 | tf_op jit(solution)/shard_map/ppermute | solution.py:435
  197.2 17.0 %collective-permute-start.34 = (bf16[64,384]{1,0:T(8,128)(2,1)S(1)}, bf16[64,384]{1,0:T(8,128)(2,1)S(1)}, u32[]{:S(2)}, u32[]{:S(2)}) collective-permute-start(bf16[64,384]{1,0:T(8,128)(2,1)S(1)} %get-tuple-element.160), channel_id=1, source_target_pairs={{0,4},{1,5},{2,6},{3,7},{4,0},{5,1},{6,2},{7,3},{8,12},{9,13},{10,... | collective-permute-start | bytes 147464 | tf_op jit(solution)/shard_map/ppermute | solution.py:435
  200.1 14.1 %collective-permute-start.35 = (bf16[64,384]{1,0:T(8,128)(2,1)S(1)}, bf16[64,384]{1,0:T(8,128)(2,1)S(1)}, u32[]{:S(2)}, u32[]{:S(2)}) collective-permute-start(bf16[64,384]{1,0:T(8,128)(2,1)S(1)} %get-tuple-element.159), channel_id=1, source_target_pairs={{0,6},{1,7},{2,0},{3,1},{4,2},{5,3},{6,4},{7,5},{8,14},{9,15},{10,... | collective-permute-start | bytes 147464 | tf_op jit(solution)/shard_map/ppermute | solution.py:435
  213.2 5.2 %collective-permute-start.41 = (bf16[64,1152]{1,0:T(8,128)(2,1)S(1)}, bf16[64,1152]{1,0:T(8,128)(2,1)S(1)}, u32[]{:S(2)}, u32[]{:S(2)}) collective-permute-start(bf16[64,1152]{1,0:T(8,128)(2,1)S(1)} %get-tuple-element.137), channel_id=1, source_target_pairs={{0,6},{1,7},{2,0},{3,1},{4,2},{5,3},{6,4},{7,5},{8,14},{9,15},{10,... | collective-permute-start | bytes 442376 | tf_op jit(solution)/shard_map/ppermute | solution.py:435
  214.3 4.9 %collective-permute-start.36 = (bf16[66,384]{1,0:T(8,128)(2,1)S(1)}, bf16[66,384]{1,0:T(8,128)(2,1)S(1)}, u32[]{:S(2)}, u32[]{:S(2)}) collective-permute-start(bf16[66,384]{1,0:T(8,128)(2,1)S(1)} %pad_maximum_fusion.9), channel_id=1, source_target_pairs={{0,24},{1,25},{2,26},{3,27},{4,28},{5,29},{6,30},{7,31},{8,16},{9,... | collective-permute-start | bytes 152072 | tf_op jit(solution)/shard_map/ppermute | solution.py:435
  214.4 6.1 %collective-permute-start.37 = (bf16[66,384]{1,0:T(8,128)(2,1)S(1)}, bf16[66,384]{1,0:T(8,128)(2,1)S(1)}, u32[]{:S(2)}, u32[]{:S(2)}) collective-permute-start(bf16[66,384]{1,0:T(8,128)(2,1)S(1)} %pad_maximum_fusion.9), channel_id=1, source_target_pairs={{0,16},{1,17},{2,18},{3,19},{4,20},{5,21},{6,22},{7,23},{8,24},{9,... | collective-permute-start | bytes 152072 | tf_op jit(solution)/shard_map/ppermute | solution.py:435
  215.2 5.2 %collective-permute-start.38 = (bf16[66,384]{1,0:T(8,128)(2,1)S(1)}, bf16[66,384]{1,0:T(8,128)(2,1)S(1)}, u32[]{:S(2)}, u32[]{:S(2)}) collective-permute-start(bf16[66,384]{1,0:T(8,128)(2,1)S(1)} %pad_maximum_fusion.9), channel_id=1, source_target_pairs={{0,8},{1,9},{2,10},{3,11},{4,12},{5,13},{6,14},{7,15},{8,0},{9,1},... | collective-permute-start | bytes 152072 | tf_op jit(solution)/shard_map/ppermute | solution.py:435
  218.5 6.2 %collective-permute-start.42 = (bf16[64,1152]{1,0:T(8,128)(2,1)S(1)}, bf16[64,1152]{1,0:T(8,128)(2,1)S(1)}, u32[]{:S(2)}, u32[]{:S(2)}) collective-permute-start(bf16[64,1152]{1,0:T(8,128)(2,1)S(1)} %add_convert_fusion.7), channel_id=1, source_target_pairs={{0,24},{1,25},{2,26},{3,27},{4,28},{5,29},{6,30},{7,31},{8,16},{9,... | collective-permute-start | bytes 442376 | tf_op jit(solution)/shard_map/ppermute | solution.py:435
  218.6 7.4 %collective-permute-start.43 = (bf16[64,1152]{1,0:T(8,128)(2,1)S(1)}, bf16[64,1152]{1,0:T(8,128)(2,1)S(1)}, u32[]{:S(2)}, u32[]{:S(2)}) collective-permute-start(bf16[64,1152]{1,0:T(8,128)(2,1)S(1)} %add_convert_fusion.7), channel_id=1, source_target_pairs={{0,16},{1,17},{2,18},{3,19},{4,20},{5,21},{6,22},{7,23},{8,24},{9,... | collective-permute-start | bytes 442376 | tf_op jit(solution)/shard_map/ppermute | solution.py:435
  219.2 6.8 %collective-permute-start.44 = (bf16[64,1152]{1,0:T(8,128)(2,1)S(1)}, bf16[64,1152]{1,0:T(8,128)(2,1)S(1)}, u32[]{:S(2)}, u32[]{:S(2)}) collective-permute-start(bf16[64,1152]{1,0:T(8,128)(2,1)S(1)} %add_convert_fusion.7), channel_id=1, source_target_pairs={{0,8},{1,9},{2,10},{3,11},{4,12},{5,13},{6,14},{7,15},{8,0},{9,1},... | collective-permute-start | bytes 442376 | tf_op jit(solution)/shard_map/ppermute | solution.py:435
  226.3 2.4 %copy-start.1 = (bf16[64,2048]{1,0:T(8,128)(2,1)S(1)}, bf16[64,2048]{1,0:T(8,128)(2,1)}, u32[]{:S(2)}) copy-start(bf16[64,2048]{1,0:T(8,128)(2,1)} %param.18) | copy-start | bytes 786436
